TPU v7x, 256 devices: a whole 4x4x8 slice. The times are simulated.
256 devices in a mesh: rollout: 2 (over core), context: 32 (over z, x), head: 4 (over y).
Axes of the slice: x: 4, y: 4, z: 8, core: 2. Of those that a mesh axis runs over, the one named last changes fastest.
Arguments:
- inner_raw: bfloat16 [16384, 8192], P(('rollout', 'context', 'head')), parts along dimension 0, may hold values from -6 to 6
- pairs_raw: bfloat16 [16384, 8, 2, 128], P(('rollout', 'context', 'head')), parts along dimension 0, may hold values from -2.5 to 2.5
- gate_raw: bfloat16 [16384, 8192], P(('rollout', 'context'), 'head'), parts along dimension 0, may hold values from -6 to 6
- step_raw: bfloat16 [16384, 128], P(('rollout', 'context'), 'head'), parts along dimension 0, may hold values from -3 to 3
- step_bias: float32 [128], P('head'), may hold values from -0.5 to 0.5
- rate_log: float32 [128], P('head'), may hold values from -13.5 to -2.8, as said below
- skip_gain: float32 [128], P('head'), may hold values from 0.5 to 2
- conv_inner: float32 [5, 8192], replicated, may hold values from -2.5 to 2.5
- conv_pairs: float32 [5, 8, 2, 128], replicated, may hold values from -2.5 to 2.5
- norm_gain: float32 [8192], P('head'), may hold values from 0.5 to 1.5
Outputs:
- mixer_out: bfloat16 [16384, 8192], P(('rollout', 'context', 'head')), parts along dimension 0
There are 2 independent parts, one for each index of `rollout`. A program takes and returns all parts, laid end to end along the dimension named above; an argument that names none is the same for every part. Nothing has to cross between parts.
Inputs may be any that keep to these rules, and one draw needn't show every extreme that they name: `rate_log`: one value a head.
All inputs are finite; a program needn't handle non-finite values.
Results may differ from a plain program's by a relative error of at most 0.012.
The roundings to bfloat16 on the way count: a program that leaves them out, or rounds other values in their place, can miss the bound.
Values may be sent and summed in bfloat16 or wider, within the bound.
No kernel may reach another device: no remote copies, remote signals or barrier semaphores. Data moves between devices by JAX's collectives and lax.ppermute only.
A program may use at most 128 MiB of HBM per device.

v0:
```python
import jax
import jax.numpy as jnp
from jax import lax
from jax.sharding import PartitionSpec as P

BLOCK = 256


def from_behind(block, axis, distance):
    devices = range(lax.axis_size(axis))
    route = [(i - distance, i) for i in devices if i - distance in devices]
    return lax.ppermute(block, axis, route)


def prefix(part, axis, combine, identity):
    place = lax.axis_index(axis)
    gathered = jax.tree.map(lambda a: lax.all_gather(a, axis), part)
    state = jax.tree.map(lambda a, e: jnp.zeros_like(a) + jnp.asarray(e, a.dtype), part, identity)

    def one(lap, state):
        return combine(
            state, jax.tree.map(lambda a: lax.dynamic_index_in_dim(a, lap, 0, False), gathered)
        )

    return lax.fori_loop(0, place, one, state)


def convolve(raw_rows, before, weight):
    tap_count = weight.shape[0] - 1
    row_count = raw_rows.shape[0]
    extended = jnp.concatenate([before, raw_rows], axis=0).astype(jnp.float32)
    summed = weight[tap_count][None, :] + weight[0][None, :] * extended[0:row_count]
    for offset in range(1, tap_count):
        summed = summed + weight[offset][None, :] * extended[offset : offset + row_count]
    return jax.nn.silu(summed).astype(jnp.bfloat16)


def block_intra(inner_conv, pairs_conv, step_size, log_cum, groups):
    block_len, head_count = step_size.shape
    per_group = head_count // groups
    head_width = inner_conv.shape[1] // head_count
    pair_view = pairs_conv.reshape(block_len, groups, 2, -1)
    scores = jnp.einsum(
        "ign,jgn->gij", pair_view[:, :, 1], pair_view[:, :, 0], preferred_element_type=jnp.float32
    )
    lower_tri = lax.broadcasted_iota(jnp.int32, (block_len, block_len), 0) >= lax.broadcasted_iota(
        jnp.int32, (block_len, block_len), 1
    )
    cum_t = log_cum.T
    log_gap = jnp.minimum(cum_t[:, :, None] - cum_t[:, None, :], 0.0)
    decay_mat = jnp.where(lower_tri[None], jnp.exp(log_gap), 0.0) * step_size.T[:, None, :]
    weights = (scores[:, None] * decay_mat.reshape(groups, per_group, block_len, block_len)).astype(
        jnp.bfloat16
    )
    inner_view = inner_conv.reshape(block_len, groups, per_group, head_width)
    intra_out = jnp.einsum(
        "gkij,jgkp->igkp", weights, inner_view, preferred_element_type=jnp.float32
    )
    return intra_out.reshape(block_len, head_count * head_width)


def block_state(inner_conv, pairs_conv, step_size, log_cum, groups):
    block_len, head_count = step_size.shape
    per_group = head_count // groups
    head_width = inner_conv.shape[1] // head_count
    tail_w = jnp.exp(log_cum[-1][None, :] - log_cum) * step_size
    weighted = (
        inner_conv.reshape(block_len, head_count, head_width).astype(jnp.float32)
        * tail_w[:, :, None]
    ).astype(jnp.bfloat16)
    weighted = weighted.reshape(block_len, groups, per_group, head_width)
    bmat = pairs_conv.reshape(block_len, groups, 2, -1)[:, :, 0]
    local_state = jnp.einsum("jgn,jgkp->gknp", bmat, weighted, preferred_element_type=jnp.float32)
    return (local_state.reshape(head_count, -1, head_width), jnp.exp(log_cum[-1]))


def finish(
    inner_conv, pairs_conv, gate_rows, intra_out, carry_state, log_cum, skip_gain, norm_gain, groups
):
    block_len, head_count = log_cum.shape
    per_group = head_count // groups
    head_width = inner_conv.shape[1] // head_count
    cmat = pairs_conv.reshape(block_len, groups, 2, -1)[:, :, 1]
    held = carry_state.astype(jnp.bfloat16).reshape(groups, per_group, -1, head_width)
    carried = jnp.einsum("ign,gknp->igkp", cmat, held, preferred_element_type=jnp.float32)
    carried = carried.reshape(block_len, head_count, head_width) * jnp.exp(log_cum)[:, :, None]
    mixed = (
        intra_out
        + carried.reshape(block_len, -1)
        + jnp.repeat(skip_gain, head_width)[None, :] * inner_conv.astype(jnp.float32)
    )
    gated_out = mixed * jax.nn.silu(gate_rows.astype(jnp.float32))
    grouped = gated_out.reshape(block_len, groups, -1)
    inv_rms = lax.rsqrt(jnp.mean(grouped * grouped, axis=2, keepdims=True) + 1e-05)
    return ((grouped * inv_rms).reshape(block_len, -1) * norm_gain[None, :]).astype(jnp.bfloat16)


def chain_combine(earlier, later):
    return (earlier[0] * later[0], later[0][:, None, None] * earlier[1] + later[1])


def absorb(running, element):
    local_state, block_decay = element
    return (block_decay[:, None, None] * running + local_state, None)


def on_device(
    inner_raw,
    pairs_raw,
    gate_raw,
    step_raw,
    step_bias,
    rate_log,
    skip_gain,
    conv_inner,
    conv_pairs,
    norm_gain,
):
    shards = lax.axis_size("head")
    row_count = inner_raw.shape[0]
    tap_count = conv_inner.shape[0] - 1
    inner_full = inner_raw.shape[1]
    pairs_flat = pairs_raw.reshape(row_count, -1)
    conv_flat = conv_pairs.reshape(tap_count + 1, -1)
    width_local = gate_raw.shape[1]
    head_local = step_raw.shape[1]
    groups_local = pairs_raw.shape[1] // shards
    last_rows = jnp.concatenate(
        [inner_raw[row_count - tap_count :], pairs_flat[row_count - tap_count :]], axis=1
    )
    before = from_behind(last_rows, ("context", "head"), 1)
    outgoing_inner = convolve(inner_raw, before[:, :inner_full], conv_inner)
    outgoing_pairs = convolve(pairs_flat, before[:, inner_full:], conv_flat)
    got_inner, got_pairs = (
        lax.all_to_all(outgoing_inner, "head", split_axis=1, concat_axis=0, tiled=True),
        lax.all_to_all(outgoing_pairs, "head", split_axis=1, concat_axis=0, tiled=True),
    )
    length = got_inner.shape[0]
    block_count = length // BLOCK
    step_size = jax.nn.softplus(step_raw.astype(jnp.float32) + step_bias[None, :])
    log_steps = (-jnp.exp(rate_log)[None, :] * step_size).reshape(block_count, BLOCK, head_local)
    lower_tri = (
        lax.broadcasted_iota(jnp.int32, (BLOCK, BLOCK), 0)
        >= lax.broadcasted_iota(jnp.int32, (BLOCK, BLOCK), 1)
    ).astype(jnp.float32)
    log_cum = jnp.einsum("ij,cjh->cih", lower_tri, log_steps, precision=lax.Precision.HIGHEST)
    step_blocks = step_size.reshape(block_count, BLOCK, head_local)
    inner_blocks = got_inner.reshape(block_count, BLOCK, -1)
    pair_blocks = got_pairs.reshape(block_count, BLOCK, -1)
    gate_blocks = gate_raw.reshape(block_count, BLOCK, -1)
    inputs = (inner_blocks, pair_blocks, step_blocks, log_cum)

    def intra_part(element):
        return block_intra(element[0], element[1], element[2], element[3], groups_local)

    def state_part(element):
        return block_state(element[0], element[1], element[2], element[3], groups_local)

    def both_parts(element):
        local_state, block_decay = state_part(element)
        return (intra_part(element), local_state, block_decay)

    intra_all, states, decays = lax.map(both_parts, inputs)
    start_zero = jnp.zeros(states.shape[1:], jnp.float32)
    device_state, _ = lax.scan(absorb, start_zero, (states, decays))
    device_decay = jnp.prod(decays, axis=0)
    incoming = prefix(
        (device_decay, device_state),
        "context",
        chain_combine,
        (jnp.ones_like(device_decay), jnp.zeros_like(device_state)),
    )

    def emit(carry_state, element):
        inner_rows, pair_rows, gate_rows, intra_out, cum_rows, local_state, block_decay = element
        result = finish(
            inner_rows,
            pair_rows,
            gate_rows,
            intra_out,
            carry_state,
            cum_rows,
            skip_gain,
            norm_gain,
            groups_local,
        )
        return (block_decay[:, None, None] * carry_state + local_state, result)

    _, results = lax.scan(
        emit,
        incoming[1],
        (inner_blocks, pair_blocks, gate_blocks, intra_all, log_cum, states, decays),
    )
    head_rows = results.reshape(length, width_local)
    return lax.all_to_all(head_rows, "head", split_axis=0, concat_axis=1, tiled=True)


def solution(mesh):
    placed = (
        P(("rollout", "context", "head"), None),
        P(("rollout", "context", "head"), None, None, None),
        P(("rollout", "context"), "head"),
        P(("rollout", "context"), "head"),
        P("head"),
        P("head"),
        P("head"),
        P(),
        P(),
        P("head"),
    )
    return jax.shard_map(
        on_device,
        mesh=mesh,
        in_specs=placed,
        out_specs=P(("rollout", "context", "head"), None),
        check_vma=False,
    )
```

profile of v0, /device:TPU:230, one launch (start us, length us, event | category | flops | bytes accessed | tf_op | source)
XLA Modules:
  0.0 496.4 jit_solution(1473578907943598542)
XLA Ops:
  8.3 3.5 collective-permute-start
  13.3 1.7 fusion.49
  19.2 4.2 all-to-all-start.1
  23.7 1.3 multiply_convert_fusion.2
  26.1 4.0 all-to-all-done.1
  30.0 3.5 all-to-all-start
  36.2 11.0 %all-to-all-done = bf16[64,4,2048]{2,0,1:T(8,128)(2,1)S(1)} async-done(((bf16[64,4,2048]{2,0,1:T(8,128)(2,1)}), bf16[64,4,2048]{2,0,1:T(8,128)(2,1)S(1)}, u32[]{:S(2)}, u32[]{:S(2)}) %all-to-all-start) | async-done | bytes 1048608 | tf_op jit(solution)/shard_map/all_to_all | solution.py:135
  47.2 2.2 reshape.197
  49.4 2.5 copy.90
  51.9 1.7 fusion.23
  58.4 38.2 %all-gather = f32[32,1,32]{2,1,0:T(1,128)} all-gather(f32[1,1,32]{2,1,0:T(1,128)S(1)} %get-tuple-element.157), channel_id=2, replica_groups=mesh['rollout'=2,'context'=32,'head'=4] {'context'}, dimensions={0}, use_global_device_ids=true | all-gather | bytes 4224 | tf_op jit(solution)/shard_map/all_gather | solution.py:17
  98.6 1.8 copy.97
  100.4 5.3 %fusion = f32[2,16,64,256]{3,2,1,0:T(8,128)} fusion(bf16[256,2,16,64]{0,3,2,1:T(8,128)(2,1)S(1)} %copy-done.1, f32[2,16,256]{2,1,0:T(8,128)S(1)} %bitcast.138, f32[2,16,256]{2,1,0:T(8,128)S(1)} %bitcast.136, f32[2,256,256]{2,1,0:T(8,128)} %fusion.35, pred[256,256]{1,0:T(8,128)(4,1)S(1)} %copy-done.11), kind=kOutput, calls=%fused_computation.4 | convolution fusion | flops 281018368 | bytes 3801088 | tf_op jit(solution)/shard_map/while/body/eval_jaxpr/gkij,jgkp->igkp/dot_general | solution.py:56
  105.7 177.0 %all-gather.3.cloned.1.call-done = f32[32,32,128,64]{2,3,1,0:T(8,128)} async-done(((f32[1,32,128,64]{2,3,1,0:T(8,128)}), f32[32,32,128,64]{2,3,1,0:T(8,128)}) %all-gather.3.cloned.1.call-update) | async-done | bytes 33554448 | tf_op jit(solution)/shard_map/all_gather | solution.py:17
  282.7 1.5 broadcast.72
  284.2 178.0 %while.3 = (s32[]{:T(128)}, f32[32,128,64]{2,1,0:T(8,128)}, s32[]{:T(128)}, f32[32,32]{1,0:T(8,128)}, f32[32,32,128,64]{2,3,1,0:T(8,128)}, /*index=5*/s32[]{:T(128)}, s32[]{:T(128)}, s32[]{:T(128)}) while((s32[]{:T(128)}, f32[32,128,64]{2,1,0:T(8,128)}, s32[]{:T(128)}, f32[32,32]{1,0:T(8,128)}, f32[32,32,128,64]{2,3,1,0:T(8,128)}, ...), condition=%wide.region_1.2_spmd, body=%wide.region_0.1_spmd.sunk | while | flops 524293 | bytes 7340551 | solution.py:25
  284.9 1.3 constant_dynamic-slice_fusion.2
  286.8 3.2 bitcast_add_fusion.3
  292.6 3.2 bitcast_add_fusion.3
  298.3 3.2 bitcast_add_fusion.3
  302.2 1.3 constant_dynamic-slice_fusion.2
  304.1 3.2 bitcast_add_fusion.3
  307.9 1.3 constant_dynamic-slice_fusion.2
  309.8 3.2 bitcast_add_fusion.3
  315.6 3.2 bitcast_add_fusion.3
  321.3 3.2 bitcast_add_fusion.3
  325.2 1.3 constant_dynamic-slice_fusion.2
  327.1 3.2 bitcast_add_fusion.3
  330.9 1.3 constant_dynamic-slice_fusion.2
  332.8 3.2 bitcast_add_fusion.3
  336.6 1.3 constant_dynamic-slice_fusion.2
  338.5 3.2 bitcast_add_fusion.3
  342.4 1.3 constant_dynamic-slice_fusion.2
  344.3 3.2 bitcast_add_fusion.3
  348.1 1.3 constant_dynamic-slice_fusion.2
  350.0 3.2 bitcast_add_fusion.3
  353.9 1.3 constant_dynamic-slice_fusion.2
  355.8 3.2 bitcast_add_fusion.3
  359.6 1.3 constant_dynamic-slice_fusion.2
  361.5 3.2 bitcast_add_fusion.3
  365.3 1.3 constant_dynamic-slice_fusion.2
  367.2 3.2 bitcast_add_fusion.3
  371.1 1.3 constant_dynamic-slice_fusion.2
  373.0 3.2 bitcast_add_fusion.3
  376.8 1.3 constant_dynamic-slice_fusion.2
  378.7 3.2 bitcast_add_fusion.3
  384.5 3.2 bitcast_add_fusion.3
  390.2 3.2 bitcast_add_fusion.3
  396.0 3.2 bitcast_add_fusion.3
  401.7 3.2 bitcast_add_fusion.3
  407.5 3.2 bitcast_add_fusion.3
  413.2 3.2 bitcast_add_fusion.3
  418.9 3.2 bitcast_add_fusion.3
  424.7 3.2 bitcast_add_fusion.3
  430.4 3.2 bitcast_add_fusion.3
  436.2 3.2 bitcast_add_fusion.3
  441.9 3.2 bitcast_add_fusion.3
  447.6 3.2 bitcast_add_fusion.3
  453.4 3.2 bitcast_add_fusion.3
  459.1 3.2 bitcast_add_fusion.3
  462.3 1.9 convert_element_type.68
  464.5 3.1 fusion.11
  467.6 1.4 fusion.21
  469.7 18.8 %all_to_all.51 = bf16[4,64,2048]{2,1,0:T(8,128)(2,1)S(1)} all-to-all(bf16[4,64,2048]{2,1,0:T(8,128)(2,1)S(1)} %bitcast.118), channel_id=1, replica_groups=mesh['rollout'=2,'context'=32,'head'=4] {'head'}, dimensions={0} | all-to-all | bytes 2097152 | tf_op jit(solution)/shard_map/all_to_all | solution.py:195
  (159 shorter events, 83.1 us)
Async XLA Ops:
  8.3 9.7 %collective-permute-start = (bf16[4,10240]{1,0:T(4,128)(2,1)S(1)}, bf16[4,10240]{1,0:T(4,128)(2,1)S(1)}, u32[]{:S(2)}, u32[]{:S(2)}) collective-permute-start(bf16[4,10240]{1,0:T(4,128)(2,1)S(1)} %pad_maximum_fusion), channel_id=1, source_target_pairs={{0,1},{1,2},{2,3},{3,4},{4,5},{5,6},{6,7},{7,8},{8,9},{9,10},{10,1... | collective-permute-start | bytes 245768 | tf_op jit(solution)/shard_map/ppermute | solution.py:12
  16.0 2.0 copy-start.12
  18.0 5.4 %copy-start.5 = (bf16[64,8192]{1,0:T(8,128)(2,1)S(1)}, bf16[64,8192]{1,0:T(8,128)(2,1)}, u32[]{:S(2)}) copy-start(bf16[64,8192]{1,0:T(8,128)(2,1)} %param.12) | copy-start | bytes 3145732
  19.2 10.8 %all-to-all-start.1 = ((bf16[64,4,512]{2,0,1:T(8,128)(2,1)}), bf16[64,4,512]{2,0,1:T(8,128)(2,1)S(1)}, u32[]{:S(2)}, u32[]{:S(2)}) async-start(bf16[64,4,512]{2,0,1:T(8,128)(2,1)} %bitcast.111), calls=%async_computation.1 | async-start | bytes 524288 | tf_op jit(solution)/shard_map/all_to_all | solution.py:136
  25.0 8.6 %copy-start.17 = (f32[32]{0:T(128)S(1)}, f32[32]{0:T(128)}, u32[]{:S(2)}) copy-start(f32[32]{0:T(128)} %param.16) | copy-start | bytes 388
  30.0 17.2 %all-to-all-start = ((bf16[64,4,2048]{2,0,1:T(8,128)(2,1)}), bf16[64,4,2048]{2,0,1:T(8,128)(2,1)S(1)}, u32[]{:S(2)}, u32[]{:S(2)}) async-start(bf16[64,4,2048]{2,0,1:T(8,128)(2,1)} %bitcast.110), calls=%async_computation | async-start | bytes 2097152 | tf_op jit(solution)/shard_map/all_to_all | solution.py:135
  33.6 249.1 %all-gather.3.cloned.1.call-start = ((), (), s32[]{:S(2)}) async-start(), calls=%async_computation.3 | async-start | bytes 34603008 | tf_op jit(solution)/shard_map/all_gather | solution.py:17
  53.6 1.2 copy-start.18
  53.6 2.1 copy-start.9
  53.6 2.8 copy-start.8
  53.6 3.5 copy-start.6
  54.7 42.5 %copy-start.7 = (bf16[256,2,1,128]{3,2,1,0:T(2,128)(2,1)S(1)}, bf16[256,2,1,128]{3,2,1,0:T(2,128)(2,1)}, u32[]{:S(2)}) copy-start(bf16[256,2,1,128]{3,2,1,0:T(2,128)(2,1)} %get-tuple-element.147) | copy-start | bytes 393220
  98.5 1.9 copy-start.1
  98.5 1.8 copy-start.11
  98.5 1.8 copy-start.13
  98.6 1.8 copy-start.15
  462.3 1.9 copy-start.2
  462.3 2.2 copy-start.3
  462.3 2.2 copy-start.14
  464.4 3.2 copy-start
  464.4 3.2 copy-start.4
  464.4 3.2 copy-start.10
  464.4 3.2 copy-start.16
Sparse Core Ops, SparseCore 0:
  54.9 227.7 all-gather.2
where the time goes:
time: 500 us; the launch traced here: 496 us
  waiting for transfers between devices  192 us (38%)
  other arithmetic  107 us (21%)
  local copies, waits for them, and re-layouts  103 us (21%)
  blocking collectives  57 us (11%)
  between operations  13.8 us (3%)
  matrix products  12.1 us (2%)
  starting transfers between devices  11.2 us (2%)
    all_gather x1, waiting for transfers between devices, prefix(): gathered = jax.tree.map(lambda a: lax.all_gather(a, axis), part)  177 us
    add x31, other arithmetic, chain_combine(): later[0][:, None, None] * earlier[1] + later[1]  97.7 us
    dynamic_slice x62, local copies, waits for them, and re-layouts, one(): lax.dynamic_index_in_dim(a, lap, 0, False)  58.8 us
    all_gather x1, blocking collectives, prefix(): gathered = jax.tree.map(lambda a: lax.all_gather(a, axis), part)  38.2 us
    mul x31, local copies, waits for them, and re-layouts, chain_combine(): later[0][:, None, None] * earlier[1] + later[1]  21.1 us
    all_to_all x1, blocking collectives, on_device(): lax.all_to_all(head_rows, 'head', split_axis=0, concat_axis=1, tiled=True)  18.8 us
    all_to_all x1, waiting for transfers between devices, on_device(): lax.all_to_all(outgoing_inner, 'head', split_axis=1, concat_axis=0, tiled...  11 us
  transfers between devices with their start and end apart: 4, of which 3 were waited for; matrix products, arithmetic and copies ran while one was open for 5% of the time, Pallas kernels for 0%

commit v1 on v0

v1 whole, which is shorter than its diff:
```python
import functools

import jax
import jax.numpy as jnp
from jax import lax
from jax.experimental import pallas as pl
from jax.experimental.pallas import tpu as pltpu
from jax.sharding import PartitionSpec as P

BLOCK = 256
HIGH = lax.Precision.HIGHEST
F32 = jnp.float32
BF16 = jnp.bfloat16
LANES = 128
ANY = pl.BlockSpec(memory_space=pl.ANY)
VMEM = pl.BlockSpec(memory_space=pltpu.VMEM)
SMEM = pl.BlockSpec(memory_space=pltpu.SMEM)
PARAMS = pltpu.CompilerParams(vmem_limit_bytes=48 * 1024 * 1024)


def cost(flops, bytes_accessed, transcendentals=0):
    return pl.CostEstimate(
        flops=flops, bytes_accessed=bytes_accessed, transcendentals=transcendentals
    )


def group_of(member):
    return 2 * (member % 4) + member // 4


def iota(shape, dim):
    return lax.broadcasted_iota(jnp.int32, shape, dim)


def spread(rows, channels, head_width):
    return (iota((rows, channels), 1) // head_width == iota((rows, channels), 0)).astype(F32)


def silu(v):
    return v / (1.0 + jnp.exp(-v))


def pack_kernel(inner, pairs, out, sem):
    wide = inner.shape[1] // 8
    narrow = pairs.shape[1] // 8
    copies = []
    for member in range(8):
        group = group_of(member)
        copies.append(
            pltpu.make_async_copy(
                inner.at[:, pl.ds(group * wide, wide)],
                out.at[member, :, pl.ds(0, wide)],
                sem.at[2 * member],
            )
        )
        copies.append(
            pltpu.make_async_copy(
                pairs.at[:, pl.ds(group * narrow, narrow)],
                out.at[member, :, pl.ds(wide, narrow)],
                sem.at[2 * member + 1],
            )
        )
    for copy in copies:
        copy.start()
    for copy in copies:
        copy.wait()


def pack(inner, pairs):
    rows = inner.shape[0]
    width = (inner.shape[1] + pairs.shape[1]) // 8
    return pl.pallas_call(
        pack_kernel,
        out_shape=jax.ShapeDtypeStruct((8, rows, width), BF16),
        in_specs=[ANY, ANY],
        out_specs=ANY,
        scratch_shapes=[pltpu.SemaphoreType.DMA((16,))],
        compiler_params=PARAMS,
        cost_estimate=cost(0, 4 * 8 * rows * width),
        name="pack",
    )(inner, pairs)


def unpack_kernel(slabs, out, sem):
    wide = slabs.shape[2]
    copies = [
        pltpu.make_async_copy(
            slabs.at[member], out.at[:, pl.ds(group_of(member) * wide, wide)], sem.at[member]
        )
        for member in range(8)
    ]
    for copy in copies:
        copy.start()
    for copy in copies:
        copy.wait()


def unpack(slabs):
    _, rows, wide = slabs.shape
    return pl.pallas_call(
        unpack_kernel,
        out_shape=jax.ShapeDtypeStruct((rows, 8 * wide), BF16),
        in_specs=[ANY],
        out_specs=ANY,
        scratch_shapes=[pltpu.SemaphoreType.DMA((8,))],
        compiler_params=PARAMS,
        cost_estimate=cost(0, 4 * 8 * rows * wide),
        name="unpack",
    )(slabs)


def prep_kernel(side_ref, own, got, bias, rate, lc, dt, lc_t, dt_t):
    side = side_ref[0]
    own_heads = own.shape[1]
    heads = own_heads // 2
    mine = own[...].astype(F32)
    theirs = got[...].astype(F32)
    low = jnp.where(side == 0, mine, theirs)
    high = jnp.where(side == 0, theirs, mine)
    column = iota((own_heads, LANES), 1)
    pick = ((iota((own_heads, LANES), 0) == column + heads * side) & (column < heads)).astype(F32)
    tri = (iota((BLOCK, BLOCK), 0) >= iota((BLOCK, BLOCK), 1)).astype(F32)
    neg_rate = -jnp.exp(rate[...])
    for b, raw in enumerate((low, high)):
        v = raw + bias[...]
        step = jnp.maximum(v, 0.0) + jnp.log1p(jnp.exp(-jnp.abs(v)))
        picked = jnp.dot(step, pick, precision=HIGH, preferred_element_type=F32)
        logs = jnp.dot(step * neg_rate, pick, precision=HIGH, preferred_element_type=F32)
        cum = jnp.dot(tri, logs, precision=HIGH, preferred_element_type=F32)
        lc[b] = cum
        dt[b] = picked
        lc_t[b] = cum.T[:heads]
        dt_t[b] = picked.T[:heads]


def prep(side, own, got, bias, rate):
    heads = own.shape[1] // 2
    tall = jax.ShapeDtypeStruct((2, BLOCK, LANES), F32)
    flat = jax.ShapeDtypeStruct((2, heads, BLOCK), F32)
    return pl.pallas_call(
        prep_kernel,
        out_shape=(tall, tall, flat, flat),
        in_specs=[SMEM, VMEM, VMEM, VMEM, VMEM],
        out_specs=(VMEM,) * 4,
        compiler_params=PARAMS,
        cost_estimate=cost(2 * 10**8, 10**6, 10**5),
        name="prep",
    )(side, own, got, bias, rate)


def taps(ext, row, rows, cols, weight):
    window = ext[pl.ds(row, rows + 8), cols]
    total = weight[4:5] + weight[0:1] * window[4 : 4 + rows]
    for k in range(1, 4):
        total = total + weight[k : k + 1] * window[4 + k : 4 + k + rows]
    return silu(total).astype(BF16)


def conv_kernel(group, recv, w_inner, w_pairs, xc, bc, ext):
    members, rows, width = recv.shape
    wide = xc.shape[1]
    ext[0:8] = jnp.zeros((8, width), F32)
    for m in range(members):
        ext[8 + m * rows : 8 + (m + 1) * rows] = recv[m].astype(F32)

    def chunk(m, _):
        row = pl.multiple_of(m * rows, rows)
        for start in range(0, wide, 128):
            cols = slice(start, start + 128)
            xc[pl.ds(row, rows), cols] = taps(ext, row, rows, cols, w_inner[:, cols])
        for start in range(0, width - wide, 128):
            bc[pl.ds(row, rows), start : start + 128] = taps(
                ext,
                row,
                rows,
                slice(wide + start, wide + start + 128),
                w_pairs[:, start : start + 128],
            )
        return 0

    lax.fori_loop(0, members, chunk, 0)


def conv(group, recv, conv_inner, conv_pairs):
    members, rows, width = recv.shape
    wide = conv_inner.shape[1] // 8
    narrow = width - wide
    total = members * rows
    return pl.pallas_call(
        conv_kernel,
        out_shape=(
            jax.ShapeDtypeStruct((total, wide), BF16),
            jax.ShapeDtypeStruct((total, narrow), BF16),
        ),
        grid_spec=pltpu.PrefetchScalarGridSpec(
            num_scalar_prefetch=1,
            grid=(1,),
            in_specs=[
                pl.BlockSpec((members, rows, width), lambda i, g: (0, 0, 0)),
                pl.BlockSpec((5, wide), lambda i, g: (0, g[0])),
                pl.BlockSpec((5, narrow), lambda i, g: (0, g[0])),
            ],
            out_specs=(
                pl.BlockSpec((total, wide), lambda i, g: (0, 0)),
                pl.BlockSpec((total, narrow), lambda i, g: (0, 0)),
            ),
            scratch_shapes=[pltpu.VMEM((8 + total, width), F32)],
        ),
        compiler_params=PARAMS,
        cost_estimate=cost(20 * total * width, 4 * total * width, 2 * total * width),
        name="conv",
    )(group, recv, conv_inner, conv_pairs)


def state_kernel(
    group, first, halo, w_inner, w_pairs, xc0, bc0, lc, dt, xc, bc, first_state, payload, ext
):
    fix = first.shape[0]
    wide = xc.shape[1]
    narrow = bc.shape[1]
    ext[0:8] = halo[fix - 8 : fix].astype(F32)
    ext[8 : 8 + fix] = first[...].astype(F32)
    xc[...] = xc0[...]
    bc[...] = bc0[...]
    for start in range(0, wide, 128):
        cols = slice(start, start + 128)
        xc[0:fix, cols] = taps(ext, 0, fix, cols, w_inner[:, cols])
    for start in range(0, narrow, 128):
        bc[0:fix, start : start + 128] = taps(
            ext, 0, fix, slice(wide + start, wide + start + 128), w_pairs[:, start : start + 128]
        )
    heads = wide // 64
    one_hot = spread(LANES, wide, wide // heads)
    states = []
    for b in range(2):
        rows = slice(b * BLOCK, (b + 1) * BLOCK)
        cum = lc[b]
        tail = jnp.exp(cum[BLOCK - 1 : BLOCK] - cum) * dt[b]
        tail = jnp.dot(tail, one_hot, precision=HIGH, preferred_element_type=F32)
        weighted = (xc[rows].astype(F32) * tail).astype(BF16)
        states.append(
            lax.dot_general(
                bc[rows, 0:128],
                weighted,
                (((0,), (0,)), ((), ())),
                preferred_element_type=F32,
            )
        )
    last = [lc[b, BLOCK - 1 : BLOCK] for b in range(2)]
    decay = jnp.dot(
        jnp.broadcast_to(jnp.exp(last[1]), (8, LANES)),
        one_hot,
        precision=HIGH,
        preferred_element_type=F32,
    )
    first_state[...] = states[0]
    total = decay[0:1] * states[0] + states[1]
    parts = payload.shape[0]
    payload[:, :, 0:wide] = total.reshape(parts, -1, wide)
    depth = payload.shape[1]
    log_decay = jnp.broadcast_to(last[0] + last[1], (depth, LANES))
    for part in range(parts):
        payload[part, :, wide : wide + LANES] = log_decay


def state(group, first, halo, conv_inner, conv_pairs, xc0, bc0, lc, dt, parts):
    fix, width = first.shape
    total, wide = xc0.shape
    narrow = width - wide
    state_rows = narrow // 2

    def whole(shape):
        return pl.BlockSpec(shape, lambda i, g: (0,) * len(shape))

    payload_shape = (parts, state_rows // parts, wide + LANES)
    return pl.pallas_call(
        state_kernel,
        out_shape=(
            jax.ShapeDtypeStruct((total, wide), BF16),
            jax.ShapeDtypeStruct((total, narrow), BF16),
            jax.ShapeDtypeStruct((state_rows, wide), F32),
            jax.ShapeDtypeStruct(payload_shape, F32),
        ),
        grid_spec=pltpu.PrefetchScalarGridSpec(
            num_scalar_prefetch=1,
            grid=(1,),
            in_specs=[
                whole((fix, width)),
                whole((fix, width)),
                pl.BlockSpec((5, wide), lambda i, g: (0, g[0])),
                pl.BlockSpec((5, narrow), lambda i, g: (0, g[0])),
                whole((total, wide)),
                whole((total, narrow)),
                whole(lc.shape),
                whole(dt.shape),
            ],
            out_specs=(
                whole((total, wide)),
                whole((total, narrow)),
                whole((state_rows, wide)),
                whole(payload_shape),
            ),
            scratch_shapes=[pltpu.VMEM((8 + fix, width), F32)],
        ),
        compiler_params=PARAMS,
        cost_estimate=cost(4 * total * wide * 128, 8 * total * wide),
        name="state",
    )(group, first, halo, conv_inner, conv_pairs, xc0, bc0, lc, dt)


def intra_kernel(side_ref, xc, bc, lc, lc_t, dt_t, skip, out):
    side = side_ref[0]
    wide = xc.shape[1]
    heads = lc_t.shape[1]
    head_width = wide // heads
    state_rows = bc.shape[1] // 2
    scores = lax.dot_general(
        bc[:, state_rows:],
        bc[:, 0:state_rows],
        (((1,), (1,)), ((), ())),
        preferred_element_type=F32,
    )
    lower = iota((BLOCK, BLOCK), 0) >= iota((BLOCK, BLOCK), 1)
    own_heads = skip.shape[1]
    row = iota((own_heads, wide), 0)
    gain = jnp.dot(
        jnp.broadcast_to(skip[...], (8, own_heads)),
        (iota((own_heads, wide), 1) // head_width + heads * side == row).astype(F32),
        precision=HIGH,
        preferred_element_type=F32,
    )[0:1]
    cum = lc[0]
    for pair in range(heads // 2):
        outs = []
        for h in (2 * pair, 2 * pair + 1):
            gap = cum[:, h : h + 1] - lc_t[0, h : h + 1]
            decay = jnp.exp(jnp.where(lower, gap, -jnp.inf))
            weights = (scores * (decay * dt_t[0, h : h + 1])).astype(BF16)
            outs.append(
                jnp.dot(
                    weights,
                    xc[:, h * head_width : (h + 1) * head_width],
                    preferred_element_type=F32,
                )
            )
        cols = slice(2 * pair * head_width, 2 * (pair + 1) * head_width)
        out[:, cols] = jnp.concatenate(outs, axis=1) + gain[:, cols] * xc[:, cols].astype(F32)


def intra(side, xc, bc, lc, lc_t, dt_t, skip):
    total, wide = xc.shape
    narrow = bc.shape[1]
    heads = lc_t.shape[1]
    return pl.pallas_call(
        intra_kernel,
        out_shape=jax.ShapeDtypeStruct((total, wide), F32),
        grid_spec=pltpu.PrefetchScalarGridSpec(
            num_scalar_prefetch=1,
            grid=(total // BLOCK,),
            in_specs=[
                pl.BlockSpec((BLOCK, wide), lambda b, s: (b, 0)),
                pl.BlockSpec((BLOCK, narrow), lambda b, s: (b, 0)),
                pl.BlockSpec((1, BLOCK, LANES), lambda b, s: (b, 0, 0)),
                pl.BlockSpec((1, heads, BLOCK), lambda b, s: (b, 0, 0)),
                pl.BlockSpec((1, heads, BLOCK), lambda b, s: (b, 0, 0)),
                pl.BlockSpec(skip.shape, lambda b, s: (0, 0)),
            ],
            out_specs=pl.BlockSpec((BLOCK, wide), lambda b, s: (b, 0)),
        ),
        compiler_params=PARAMS,
        cost_estimate=cost(2 * total * BLOCK * wide * 4, 8 * total * wide, heads * total * BLOCK),
        name="intra",
    )(side, xc, bc, lc, lc_t, dt_t, skip)


def scan_kernel(recv, out):
    chunks, rows, width = recv.shape
    wide = out.shape[2]
    one_hot = spread(LANES, wide, 64)
    logs = jnp.concatenate([recv[k, 0:1, wide:width] for k in range(chunks)], axis=0)
    decay = jnp.dot(jnp.exp(logs), one_hot, precision=HIGH, preferred_element_type=F32)
    carry = jnp.zeros((rows, wide), F32)
    for k in range(chunks):
        out[k] = carry
        carry = decay[k : k + 1] * carry + recv[k, :, 0:wide]


def scan(recv):
    chunks, rows, width = recv.shape
    return pl.pallas_call(
        scan_kernel,
        out_shape=jax.ShapeDtypeStruct((chunks, rows, width - LANES), F32),
        in_specs=[VMEM],
        out_specs=VMEM,
        compiler_params=PARAMS,
        cost_estimate=cost(4 * chunks * rows * width, 4 * chunks * rows * width),
        name="scan",
    )(recv)


def finish_kernel(side_ref, carry, first_state, bc, lc, lc0, mixed, own, got, gain, out):
    side = side_ref[0]
    b = pl.program_id(0)
    wide = mixed.shape[1]
    state_rows = bc.shape[1] // 2
    one_hot = spread(LANES, wide, 64)
    start = carry[...].reshape(state_rows, wide)
    decay = jnp.dot(
        jnp.broadcast_to(jnp.exp(lc0[0, BLOCK - 1 : BLOCK]), (8, LANES)),
        one_hot,
        precision=HIGH,
        preferred_element_type=F32,
    )[0:1]
    start = jnp.where(b == 0, start, decay * start + first_state[...]).astype(BF16)
    carried = jnp.dot(bc[:, state_rows:], start, preferred_element_type=F32)
    scale = jnp.dot(jnp.exp(lc[0]), one_hot, precision=HIGH, preferred_element_type=F32)
    gate = jnp.where(b == side, own[...].astype(F32), got[...].astype(F32))
    gated = (mixed[...] + carried * scale) * silu(gate)
    inv = lax.rsqrt(jnp.mean(gated * gated, axis=1, keepdims=True) + 1e-5)
    result = (gated * inv * gain[...]).astype(BF16)
    out[...] = result.reshape(out.shape)


def finish(side, carry, first_state, bc, lc, mixed, gate, got, gain):
    total, wide = mixed.shape
    narrow = bc.shape[1]

    def whole(shape):
        return pl.BlockSpec(shape, lambda b, s: (0,) * len(shape))

    return pl.pallas_call(
        finish_kernel,
        out_shape=jax.ShapeDtypeStruct((8, total // 8, wide), BF16),
        grid_spec=pltpu.PrefetchScalarGridSpec(
            num_scalar_prefetch=1,
            grid=(total // BLOCK,),
            in_specs=[
                whole(carry.shape),
                whole(first_state.shape),
                pl.BlockSpec((BLOCK, narrow), lambda b, s: (b, 0)),
                pl.BlockSpec((1, BLOCK, LANES), lambda b, s: (b, 0, 0)),
                pl.BlockSpec((1, BLOCK, LANES), lambda b, s: (0, 0, 0)),
                pl.BlockSpec((BLOCK, wide), lambda b, s: (b, 0)),
                pl.BlockSpec((BLOCK, wide), lambda b, s: (0, s[0])),
                whole(got.shape),
                pl.BlockSpec((1, wide), lambda b, s: (0, s[0])),
            ],
            out_specs=pl.BlockSpec((4, total // 8, wide), lambda b, s: (b, 0, 0)),
        ),
        compiler_params=PARAMS,
        cost_estimate=cost(2 * total * wide * 200, 10 * total * wide, total * wide),
        name="finish",
    )(side, carry, first_state, bc, lc, lc, mixed, gate, got, gain)


def on_device(
    inner_raw,
    pairs_raw,
    gate_raw,
    step_raw,
    step_bias,
    rate_log,
    skip_gain,
    conv_inner,
    conv_pairs,
    norm_gain,
):
    places = lax.axis_size("context")
    shards = lax.axis_size("head")
    chunks = places // 2
    side = lax.axis_index("context") % 2
    group = (2 * lax.axis_index("head") + side).astype(jnp.int32).reshape(1)
    side = side.astype(jnp.int32)
    side_arr = side.reshape(1)
    rows = inner_raw.shape[0]
    partner = [(c, c ^ 1) for c in range(places)]
    after = [(c, c + 2) for c in range(places - 2)]
    teams = [list(range(8 * k, 8 * k + 8)) for k in range(places * shards // 8)]
    lines = [[2 * k + s for k in range(chunks)] for s in range(2)]

    packed = pack(inner_raw, pairs_raw.reshape(rows, -1))
    step_got = lax.ppermute(step_raw, "context", partner)
    recv = lax.all_to_all(
        packed, ("context", "head"), split_axis=0, concat_axis=0, axis_index_groups=teams
    )
    halo = lax.ppermute(recv[7, rows - 16 :], "context", after)
    half = gate_raw.shape[1] // 2
    gate_out = lax.dynamic_slice_in_dim(gate_raw, (1 - side) * half, half, 1)
    gate_out, recv = lax.optimization_barrier((gate_out, recv))
    gate_got = lax.ppermute(gate_out, "context", partner)

    lc, dt, lc_t, dt_t = prep(
        side_arr, step_raw, step_got, step_bias.reshape(1, -1), rate_log.reshape(1, -1)
    )
    pair_taps = conv_pairs.reshape(conv_pairs.shape[0], -1)
    xc0, bc0 = conv(group, recv, conv_inner, pair_taps)
    xc, bc, first_state, payload = state(
        group, recv[0, :16], halo, conv_inner, pair_taps, xc0, bc0, lc, dt, chunks
    )
    states = lax.all_to_all(
        payload, "context", split_axis=0, concat_axis=0, axis_index_groups=lines
    )
    mixed = intra(side_arr, xc, bc, lc, lc_t, dt_t, skip_gain.reshape(1, -1))
    carries = scan(states)
    carry = lax.all_to_all(
        carries, "context", split_axis=0, concat_axis=0, axis_index_groups=lines
    )
    slabs = finish(
        side_arr, carry, first_state, bc, lc, mixed, gate_raw, gate_got, norm_gain.reshape(1, -1)
    )
    slabs = lax.all_to_all(
        slabs, ("context", "head"), split_axis=0, concat_axis=0, axis_index_groups=teams
    )
    return unpack(slabs)


def solution(mesh):
    placed = (
        P(("rollout", "context", "head"), None),
        P(("rollout", "context", "head"), None, None, None),
        P(("rollout", "context"), "head"),
        P(("rollout", "context"), "head"),
        P("head"),
        P("head"),
        P("head"),
        P(),
        P(),
        P("head"),
    )
    return jax.shard_map(
        on_device,
        mesh=mesh,
        in_specs=placed,
        out_specs=P(("rollout", "context", "head"), None),
        check_vma=False,
    )
```

time: 500 us -> 112 us (0.22)
  the two profiles are of different devices: /device:TPU:230 before, /device:TPU:8 now
where the time goes in v1:
time: 112 us; the launch traced here: 109 us
  blocking collectives  44.5 us (40%)
  waiting for transfers between devices  23.2 us (21%)
  Pallas kernels  18.4 us (16%)
  starting transfers between devices  16.3 us (15%)
  local copies, waits for them, and re-layouts  6.9 us (6%)
    all_to_all x1, blocking collectives, on_device(): lax.all_to_all(payload, 'context', split_axis=0, concat_axis=0, axis_inde...  29.4 us
    all_to_all x1, blocking collectives, on_device(): lax.all_to_all(slabs, ('context', 'head'), split_axis=0, concat_axis=0, a...  15.1 us
    ppermute x1, waiting for transfers between devices, on_device(): step_got = lax.ppermute(step_raw, 'context', partner)  14.7 us
    ppermute x1, waiting for transfers between devices, on_device(): gate_got = lax.ppermute(gate_out, 'context', partner)  8.45 us
    all_to_all x1, starting transfers between devices, on_device(): lax.all_to_all(packed, ('context', 'head'), split_axis=0, concat_axis=0,...  5.99 us
    unnamed x25, local copies, waits for them, and re-layouts  4.89 us
    ppermute x1, starting transfers between devices, on_device(): halo = lax.ppermute(recv[7, rows - 16:], 'context', after)  4.64 us
    pallas_call x1, Pallas kernels, finish(): pl.pallas_call(finish_kernel, out_shape=jax.ShapeDtypeStruct((8, total //...  4.26 us
  transfers between devices with their start and end apart: 5, of which 2 were waited for; matrix products, arithmetic and copies ran while one was open for 1% of the time, Pallas kernels for 8%

profile of v1, /device:TPU:8, one launch (start us, length us, event | category | flops | bytes accessed | tf_op | source)
XLA Modules:
  0.0 109.5 jit_solution(11358530342272023866)
XLA Ops:
  0.0 1.1 %reshape.26.pairs = bf16[64,2048]{1,0:T(8,128)(2,1)S(1)} reshape(bf16[64,8,2,128]{3,2,1,0:T(2,128)(2,1)} %param.11) | data formatting | bytes 524288 | tf_op jit(solution)/shard_map/reshape | solution.py:481
  1.1 0.0 copy-start.2
  1.1 1.2 %copy-done.2 = bf16[64,8192]{1,0:T(8,128)(2,1)S(1)} copy-done((bf16[64,8192]{1,0:T(8,128)(2,1)S(1)}, bf16[64,8192]{1,0:T(8,128)(2,1)}, u32[]{:S(2)}) %copy-start.2) | copy-done | bytes 1048600
  2.4 1.2 %pack.1 = bf16[8,64,1280]{2,1,0:T(8,128)(2,1)} custom-call(bf16[64,8192]{1,0:T(8,128)(2,1)S(1)} %copy-done.2, bf16[64,2048]{1,0:T(8,128)(2,1)S(1)} %reshape.26.pairs), custom_call_target="tpu_custom_call" | custom-call | bytes 2621440 | tf_op jit(solution)/shard_map/pack/pallas_call | solution.py:72
  3.6 0.0 copy-start.11
  3.6 0.0 copy-start
  3.6 0.0 copy-start.10
  3.6 0.0 copy-start.7
  3.6 0.0 copy-start.8
  3.6 6.0 %all-to-all-start = ((bf16[8,64,1280]{2,1,0:T(8,128)(2,1)}), bf16[8,64,1280]{2,1,0:T(8,128)(2,1)S(1)}, u32[]{:S(2)}, u32[]{:S(2)}) async-start(bf16[8,64,1280]{2,1,0:T(8,128)(2,1)} %pack.1), calls=%async_computation | async-start | bytes 2621440 | tf_op jit(solution)/shard_map/all_to_all | solution.py:483
  9.6 0.0 copy-done.11
  9.6 0.0 copy-start.3
  9.6 0.1 copy.12.own
  9.8 1.6 %collective-permute-start.1 = (bf16[256,32]{1,0:T(8,128)(2,1)S(1)}, bf16[256,32]{1,0:T(8,128)(2,1)S(1)}, u32[]{:S(2)}, u32[]{:S(2)}) collective-permute-start(bf16[256,32]{1,0:T(8,128)(2,1)S(1)} %copy.12.own), channel_id=1, source_target_pairs={{0,4},{4,0},{8,12},{12,8},{16,20},{20,16},{24,28},{28,24},{32,36},... | collective-permute-start | bytes 49160 | tf_op jit(solution)/shard_map/ppermute | solution.py:482
  11.3 0.0 copy-done
  11.3 0.8 constant_dynamic-slice_fusion
  12.1 0.0 copy-done.10
  12.2 14.7 %collective-permute-done.1.got = bf16[256,32]{1,0:T(8,128)(2,1)S(1)} collective-permute-done((bf16[256,32]{1,0:T(8,128)(2,1)S(1)}, bf16[256,32]{1,0:T(8,128)(2,1)S(1)}, u32[]{:S(2)}, u32[]{:S(2)}) %collective-permute-start.1) | collective-permute-done | bytes 16416 | tf_op jit(solution)/shard_map/ppermute | solution.py:482
  26.9 0.0 copy-done.7
  26.9 0.0 copy-done.8
  26.9 1.7 %prep.1 = (f32[2,256,128]{2,1,0:T(8,128)S(1)}, f32[2,256,128]{2,1,0:T(8,128)S(1)}, f32[2,16,256]{2,1,0:T(8,128)S(1)}, f32[2,16,256]{2,1,0:T(8,128)S(1)}) custom-call(s32[1]{0:T(128)} %bitcast.side_ref, bf16[256,32]{1,0:T(8,128)(2,1)S(1)} %copy.12.own, bf16[256,32]{1,0:T(8,128)(2,1)S(1)} %collective-permute-done.1.got, f32[1,32]{1,0:T(1,128)S(1)} %bitcast.11, ...), custom_call_target="tpu_custom_call" | custom-call | flops 200000000 | bytes 1000000 | tf_op jit(solution)/shard_map/prep/pallas_call | solution.py:140
  28.7 0.0 all-to-all-done.recv
  28.7 4.6 %collective-permute-start = (bf16[16,1280]{1,0:T(8,128)(2,1)S(1)}, bf16[16,1280]{1,0:T(8,128)(2,1)S(1)}, u32[]{:S(2)}, u32[]{:S(2)}) collective-permute-start(bf16[16,1280]{1,0:T(8,128)(2,1)S(1)} %slice_bitcast_fusion), channel_id=1, source_target_pairs={{0,8},{4,12},{8,16},{12,20},{16,24},{20,28},{24,32},{28,36},{32,40... | collective-permute-start | bytes 122888 | tf_op jit(solution)/shard_map/ppermute | solution.py:486
  33.4 0.0 copy-done.3
  33.4 2.6 %conv.1 = (bf16[512,1024]{1,0:T(8,128)(2,1)S(1)}, bf16[512,256]{1,0:T(8,128)(2,1)S(1)}) custom-call(s32[1]{0:T(128)} %bitcast.1.group, bf16[8,64,1280]{2,1,0:T(8,128)(2,1)S(1)} %all-to-all-done.recv, f32[5,8192]{1,0:T(8,128)S(1)} %copy-done.3, f32[5,2048]{1,0:T(8,128)S(1)} %reshape.27.w_pairs), custom_call_target="tpu_custom_call" | custom-call | flops 13107200 | bytes 2621440 | tf_op jit(solution)/shard_map/conv/pallas_call | solution.py:189
  36.0 0.0 collective-permute-done.halo
  36.0 2.2 %state.1 = (bf16[512,1024]{1,0:T(8,128)(2,1)S(1)}, bf16[512,256]{1,0:T(8,128)(2,1)S(1)}, f32[128,1024]{1,0:T(8,128)S(1)}, f32[16,8,1152]{2,1,0:T(8,128)S(1)}) custom-call(s32[1]{0:T(128)} %bitcast.1.group, bf16[16,1280]{1,0:T(8,128)(2,1)S(1)} %slice_bitcast_fusion.1.first, bf16[16,1280]{1,0:T(8,128)(2,1)S(1)} %collective-permute-done.halo, ...), custom_call_target="tpu_custom_call" | custom-call | flops 268435456 | bytes 4194304 | tf_op jit(solution)/shard_map/state/pallas_call | solution.py:276
  38.3 0.0 copy-start.5
  38.3 1.0 copy-done.5
  39.2 29.4 %all_to_all.20.recv = f32[16,8,1152]{2,1,0:T(8,128)S(1)} all-to-all(f32[16,8,1152]{2,1,0:T(8,128)S(1)} %get-tuple-element.22), channel_id=1, replica_groups={{0,8,16,24,32,40,48,56,64,72,80,88,96,104,112,120},{4,12,20,28,36,44,52..., dimensions={0} | all-to-all | bytes 1179648 | tf_op jit(solution)/shard_map/all_to_all | solution.py:500
  68.6 0.0 copy-start.9
  68.6 1.1 scan.1
  69.7 3.6 %all-to-all-start.2 = ((f32[16,8,1024]{2,1,0:T(8,128)}), f32[16,8,1024]{2,1,0:T(8,128)S(1)}, u32[]{:S(2)}, u32[]{:S(2)}) async-start(f32[16,8,1024]{2,1,0:T(8,128)} %scan.1), calls=%async_computation.2 | async-start | bytes 1048576 | tf_op jit(solution)/shard_map/all_to_all | solution.py:505
  73.3 0.5 collective-permute-start.2
  73.8 0.0 copy-done.9
  73.8 0.0 copy-start.6
  73.8 1.2 %copy-done.6 = bf16[512,1024]{1,0:T(8,128)(2,1)S(1)} copy-done((bf16[512,1024]{1,0:T(8,128)(2,1)S(1)}, bf16[512,1024]{1,0:T(8,128)(2,1)}, u32[]{:S(2)}) %copy-start.6) | copy-done | bytes 1048600
  75.1 0.0 copy-start.4
  75.1 4.2 %intra.1.mixed = f32[512,1024]{1,0:T(8,128)S(1)} custom-call(s32[1]{0:T(128)} %bitcast.side_ref, bf16[512,1024]{1,0:T(8,128)(2,1)S(1)} %copy-done.6, bf16[512,256]{1,0:T(8,128)(2,1)S(1)} %get-tuple-element.24.bc, f32[2,256,128]{2,1,0:T(8,128)S(1)} %get-tuple-element.20.lc.lc0, f32[2,16,256]{2,1,0:T(8,128)S(1)} %get-tuple-element.26.lc_t, ...), custom_call_target="tpu_custom_call" | custom-call | flops 1073741824 | bytes 4194304 | tf_op jit(solution)/shard_map/intra/pallas_call | solution.py:354
  79.3 0.0 copy-start.1
  79.3 1.3 %copy-done.1 = f32[512,1024]{1,0:T(8,128)} copy-done((f32[512,1024]{1,0:T(8,128)}, f32[512,1024]{1,0:T(8,128)S(1)}, u32[]{:S(2)}) %copy-start.1) | copy-done | bytes 2097176
  80.6 8.4 %collective-permute-done.2.got = bf16[256,1024]{1,0:T(8,128)(2,1)S(1)} collective-permute-done((bf16[256,1024]{1,0:T(8,128)(2,1)}, bf16[256,1024]{1,0:T(8,128)(2,1)S(1)}, u32[]{:S(2)}, u32[]{:S(2)}) %collective-permute-start.2) | collective-permute-done | bytes 524320 | tf_op jit(solution)/shard_map/ppermute | solution.py:490
  89.1 0.0 all-to-all-done.2.carry
  89.1 0.0 copy-done.4
  89.1 4.3 %finish.1 = bf16[8,64,1024]{2,1,0:T(8,128)(2,1)S(1)} custom-call(s32[1]{0:T(128)} %bitcast.side_ref, f32[16,8,1024]{2,1,0:T(8,128)S(1)} %all-to-all-done.2.carry, f32[128,1024]{1,0:T(8,128)S(1)} %get-tuple-element.23.first_state, bf16[512,256]{1,0:T(8,128)(2,1)S(1)} %get-tuple-element.24.bc, f32[2,256,128]{2,1,0:T(8,128)S(1)} %get-tuple-element.20.lc.lc0, ...), custom_call_target="tpu_custom_call" | custom-call | flops 209715200 | bytes 5242880 | tf_op jit(solution)/shard_map/finish/pallas_call | solution.py:431
  93.3 15.1 %all_to_all.21.slabs = bf16[8,64,1024]{2,1,0:T(8,128)(2,1)S(1)} all-to-all(bf16[8,64,1024]{2,1,0:T(8,128)(2,1)S(1)} %finish.1), channel_id=1, replica_groups={{0,1,2,3,4,5,6,7},{8,9,10,11,12,13,14,15},{16,17,18,19,20,21,22,23},{24..., dimensions={0} | all-to-all | bytes 2097152 | tf_op jit(solution)/shard_map/all_to_all | solution.py:511
  108.4 1.0 unpack.1
  (3 shorter events, 0.0 us)
Async XLA Ops:
  1.1 1.2 %copy-start.2 = (bf16[64,8192]{1,0:T(8,128)(2,1)S(1)}, bf16[64,8192]{1,0:T(8,128)(2,1)}, u32[]{:S(2)}) copy-start(bf16[64,8192]{1,0:T(8,128)(2,1)} %inner.1) | copy-start | bytes 3145732
  3.6 6.0 %copy-start.11 = (bf16[256,32]{0,1:T(8,128)(2,1)S(1)}, bf16[256,32]{0,1:T(8,128)(2,1)}, u32[]{:S(2)}) copy-start(bf16[256,32]{0,1:T(8,128)(2,1)} %param.13) | copy-start | bytes 49156
  3.6 7.7 %copy-start = (bf16[256,2048]{1,0:T(8,128)(2,1)S(1)}, bf16[256,2048]{1,0:T(8,128)(2,1)}, u32[]{:S(2)}) copy-start(bf16[256,2048]{1,0:T(8,128)(2,1)} %own.2) | copy-start | bytes 3145732
  3.6 8.5 %copy-start.10 = (f32[5,8,2,128]{3,2,1,0:T(2,128)S(1)}, f32[5,8,2,128]{3,2,1,0:T(2,128)}, u32[]{:S(2)}) copy-start(f32[5,8,2,128]{3,2,1,0:T(2,128)} %param.18) | copy-start | bytes 122884
  3.6 23.3 %copy-start.7 = (f32[32]{0:T(128)S(1)}, f32[32]{0:T(128)}, u32[]{:S(2)}) copy-start(f32[32]{0:T(128)} %param.14) | copy-start | bytes 388
  3.6 23.3 %copy-start.8 = (f32[32]{0:T(128)S(1)}, f32[32]{0:T(128)}, u32[]{:S(2)}) copy-start(f32[32]{0:T(128)} %param.15) | copy-start | bytes 388
  3.6 25.0 %all-to-all-start = ((bf16[8,64,1280]{2,1,0:T(8,128)(2,1)}), bf16[8,64,1280]{2,1,0:T(8,128)(2,1)S(1)}, u32[]{:S(2)}, u32[]{:S(2)}) async-start(bf16[8,64,1280]{2,1,0:T(8,128)(2,1)} %pack.1), calls=%async_computation | async-start | bytes 2621440 | tf_op jit(solution)/shard_map/all_to_all | solution.py:483
  9.6 23.7 %copy-start.3 = (f32[5,8192]{1,0:T(8,128)S(1)}, f32[5,8192]{1,0:T(8,128)}, u32[]{:S(2)}) copy-start(f32[5,8192]{1,0:T(8,128)} %w_inner.3) | copy-start | bytes 491524
  9.8 17.2 %collective-permute-start.1 = (bf16[256,32]{1,0:T(8,128)(2,1)S(1)}, bf16[256,32]{1,0:T(8,128)(2,1)S(1)}, u32[]{:S(2)}, u32[]{:S(2)}) collective-permute-start(bf16[256,32]{1,0:T(8,128)(2,1)S(1)} %copy.12.own), channel_id=1, source_target_pairs={{0,4},{4,0},{8,12},{12,8},{16,20},{20,16},{24,28},{28,24},{32,36},... | collective-permute-start | bytes 49160 | tf_op jit(solution)/shard_map/ppermute | solution.py:482
  28.7 7.3 %collective-permute-start = (bf16[16,1280]{1,0:T(8,128)(2,1)S(1)}, bf16[16,1280]{1,0:T(8,128)(2,1)S(1)}, u32[]{:S(2)}, u32[]{:S(2)}) collective-permute-start(bf16[16,1280]{1,0:T(8,128)(2,1)S(1)} %slice_bitcast_fusion), channel_id=1, source_target_pairs={{0,8},{4,12},{8,16},{12,20},{16,24},{20,28},{24,32},{28,36},{32,40... | collective-permute-start | bytes 122888 | tf_op jit(solution)/shard_map/ppermute | solution.py:486
  38.3 1.0 copy-start.5
  68.6 5.2 %copy-start.9 = (f32[32]{0:T(128)S(1)}, f32[32]{0:T(128)}, u32[]{:S(2)}) copy-start(f32[32]{0:T(128)} %param.16) | copy-start | bytes 388
  69.7 19.3 %all-to-all-start.2 = ((f32[16,8,1024]{2,1,0:T(8,128)}), f32[16,8,1024]{2,1,0:T(8,128)S(1)}, u32[]{:S(2)}, u32[]{:S(2)}) async-start(f32[16,8,1024]{2,1,0:T(8,128)} %scan.1), calls=%async_computation.2 | async-start | bytes 1048576 | tf_op jit(solution)/shard_map/all_to_all | solution.py:505
  73.3 15.8 %collective-permute-start.2 = (bf16[256,1024]{1,0:T(8,128)(2,1)}, bf16[256,1024]{1,0:T(8,128)(2,1)S(1)}, u32[]{:S(2)}, u32[]{:S(2)}) collective-permute-start(bf16[256,1024]{1,0:T(8,128)(2,1)} %constant_dynamic-slice_fusion), channel_id=1, source_target_pairs={{0,4},{4,0},{8,12},{12,8},{16,20},{20,16},{24,28},{28,24},{32,36},... | collective-permute-start | bytes 1572872 | tf_op jit(solution)/shard_map/ppermute | solution.py:490
  73.8 1.2 %copy-start.6 = (bf16[512,1024]{1,0:T(8,128)(2,1)S(1)}, bf16[512,1024]{1,0:T(8,128)(2,1)}, u32[]{:S(2)}) copy-start(bf16[512,1024]{1,0:T(8,128)(2,1)} %copy-done.5) | copy-start | bytes 3145732
  75.1 14.0 %copy-start.4 = (f32[2048]{0:T(1024)S(1)}, f32[2048]{0:T(1024)}, u32[]{:S(2)}) copy-start(f32[2048]{0:T(1024)} %param.19) | copy-start | bytes 24580
  79.3 1.3 %copy-start.1 = (f32[512,1024]{1,0:T(8,128)}, f32[512,1024]{1,0:T(8,128)S(1)}, u32[]{:S(2)}) copy-start(f32[512,1024]{1,0:T(8,128)S(1)} %intra.1.mixed) | copy-start | bytes 6291460

commit v2 on v1

v2 whole, which is shorter than its diff:
```python
import functools

import jax
import jax.numpy as jnp
from jax import lax
from jax.experimental import pallas as pl
from jax.experimental.pallas import tpu as pltpu
from jax.sharding import PartitionSpec as P

BLOCK = 256
HIGH = lax.Precision.HIGHEST
F32 = jnp.float32
BF16 = jnp.bfloat16
LANES = 128
ANY = pl.BlockSpec(memory_space=pl.ANY)
VMEM = pl.BlockSpec(memory_space=pltpu.VMEM)
SMEM = pl.BlockSpec(memory_space=pltpu.SMEM)
PARAMS = pltpu.CompilerParams(vmem_limit_bytes=24 * 1024 * 1024)


def cost(flops, bytes_accessed, transcendentals=0):
    return pl.CostEstimate(
        flops=flops, bytes_accessed=bytes_accessed, transcendentals=transcendentals
    )


def group_of(member):
    return 2 * (member % 4) + member // 4


def iota(shape, dim):
    return lax.broadcasted_iota(jnp.int32, shape, dim)


def spread(rows, channels, head_width):
    return (iota((rows, channels), 1) // head_width == iota((rows, channels), 0)).astype(F32)


def silu(v):
    return v / (1.0 + jnp.exp(-v))


def taps(ext, rows, cols, weight):
    window = ext[0 : rows + 8, cols]
    total = weight[4:5] + weight[0:1] * window[4 : 4 + rows]
    for k in range(1, 4):
        total = total + weight[k : k + 1] * window[4 + k : 4 + k + rows]
    return silu(total).astype(BF16)


def conv_kernel(inner, pairs, w_inner, w_pairs, out, ext):
    rows, wide = inner.shape
    width = out.shape[2]
    ext[0:8] = jnp.zeros((8, width), F32)
    ext[8:, 0:wide] = inner[...].astype(F32)
    ext[8:, wide:width] = pairs[...].astype(F32)
    for start in range(0, width, LANES):
        cols = slice(start, start + LANES)
        weight = w_inner[:, cols] if start < wide else w_pairs[:, start - wide : start - wide + LANES]
        out[0, :, cols] = taps(ext, rows, cols, weight)


def conv(inner, pairs, w_inner, w_pairs):
    rows = inner.shape[0]
    wide, narrow = inner.shape[1] // 8, pairs.shape[1] // 8
    width = wide + narrow

    def column(member):
        return (0, 2 * lax.rem(member, 4) + lax.div(member, 4))

    return pl.pallas_call(
        conv_kernel,
        out_shape=jax.ShapeDtypeStruct((8, rows, width), BF16),
        grid=(8,),
        in_specs=[
            pl.BlockSpec((rows, wide), column),
            pl.BlockSpec((rows, narrow), column),
            pl.BlockSpec((5, wide), column),
            pl.BlockSpec((5, narrow), column),
        ],
        out_specs=pl.BlockSpec((1, rows, width), lambda m: (m, 0, 0)),
        scratch_shapes=[pltpu.VMEM((8 + rows, width), F32)],
        compiler_params=PARAMS,
        cost_estimate=cost(160 * rows * width, 32 * rows * width, 16 * rows * width),
        name="conv",
    )(inner, pairs, w_inner, w_pairs)


FIX = 16


def fix_kernel(inner, pairs, halo_inner, halo_pairs, w_inner, w_pairs, _, out, ext):
    full = inner.shape[1]
    wide, narrow = full // 8, pairs.shape[1] // 8
    ext[0:8, 0:full] = halo_inner[...].astype(F32)
    ext[8:, 0:full] = inner[...].astype(F32)
    ext[0:8, full:] = halo_pairs[...].astype(F32)
    ext[8:, full:] = pairs[...].astype(F32)
    for member in range(8):
        group = group_of(member)
        for start in range(0, wide, LANES):
            at = group * wide + start
            cols = slice(at, at + LANES)
            out[member, :, start : start + LANES] = taps(ext, FIX, cols, w_inner[:, cols])
        for start in range(0, narrow, LANES):
            at = group * narrow + start
            out[member, :, wide + start : wide + start + LANES] = taps(
                ext, FIX, slice(full + at, full + at + LANES), w_pairs[:, at : at + LANES]
            )


def fix(inner, pairs, halo_inner, halo_pairs, w_inner, w_pairs, packed):
    full, pairs_full = inner.shape[1], pairs.shape[1]

    def whole(shape):
        return pl.BlockSpec(shape, lambda i: (0,) * len(shape))

    return pl.pallas_call(
        fix_kernel,
        out_shape=jax.ShapeDtypeStruct(packed.shape, BF16),
        grid=(1,),
        in_specs=[
            whole((FIX, full)),
            whole((FIX, pairs_full)),
            whole(halo_inner.shape),
            whole(halo_pairs.shape),
            whole(w_inner.shape),
            whole(w_pairs.shape),
            ANY,
        ],
        out_specs=whole((8, FIX, packed.shape[2])),
        scratch_shapes=[pltpu.VMEM((8 + FIX, full + pairs_full), F32)],
        input_output_aliases={6: 0},
        compiler_params=PARAMS,
        cost_estimate=cost(20 * FIX * (full + pairs_full), 8 * FIX * (full + pairs_full)),
        name="fix",
    )(inner, pairs, halo_inner, halo_pairs, w_inner, w_pairs, packed)


def unpack_kernel(slabs, out, sem):
    wide = slabs.shape[2]
    copies = [
        pltpu.make_async_copy(
            slabs.at[member], out.at[:, pl.ds(group_of(member) * wide, wide)], sem.at[member]
        )
        for member in range(8)
    ]
    for copy in copies:
        copy.start()
    for copy in copies:
        copy.wait()


def unpack(slabs):
    _, rows, wide = slabs.shape
    return pl.pallas_call(
        unpack_kernel,
        out_shape=jax.ShapeDtypeStruct((rows, 8 * wide), BF16),
        in_specs=[ANY],
        out_specs=ANY,
        scratch_shapes=[pltpu.SemaphoreType.DMA((8,))],
        compiler_params=PARAMS,
        cost_estimate=cost(0, 4 * 8 * rows * wide),
        name="unpack",
    )(slabs)


def widen(value, one_hot):
    return jnp.dot(value, one_hot, precision=HIGH, preferred_element_type=F32)


def prep_kernel(side_ref, own, got, bias, rate, lc, lc_t, dt_t, tail, scale, last):
    side = side_ref[0]
    own_heads = own.shape[1]
    heads = own_heads // 2
    wide = tail.shape[2]
    mine = own[...].astype(F32)
    theirs = got[...].astype(F32)
    low = jnp.where(side == 0, mine, theirs)
    high = jnp.where(side == 0, theirs, mine)
    column = iota((own_heads, LANES), 1)
    pick = ((iota((own_heads, LANES), 0) == column + heads * side) & (column < heads)).astype(F32)
    tri = (iota((BLOCK, BLOCK), 0) >= iota((BLOCK, BLOCK), 1)).astype(F32)
    one_hot = spread(LANES, wide, wide // heads)
    neg_rate = -jnp.exp(rate[...])
    for b, raw in enumerate((low, high)):
        v = raw + bias[...]
        step = jnp.maximum(v, 0.0) + jnp.log1p(jnp.exp(-jnp.abs(v)))
        picked = widen(step, pick)
        cum = widen(tri, widen(step * neg_rate, pick))
        end = cum[BLOCK - 1 : BLOCK]
        lc[b] = cum
        lc_t[b] = cum.T[:heads]
        dt_t[b] = picked.T[:heads]
        tail[b] = widen(jnp.exp(end - cum) * picked, one_hot)
        scale[b] = widen(jnp.exp(cum), one_hot)
        last[b] = jnp.broadcast_to(end, (8, LANES))


def prep(side, own, got, bias, rate, wide):
    heads = own.shape[1] // 2
    tall = jax.ShapeDtypeStruct((2, BLOCK, LANES), F32)
    flat = jax.ShapeDtypeStruct((2, heads, BLOCK), F32)
    full = jax.ShapeDtypeStruct((2, BLOCK, wide), F32)
    last = jax.ShapeDtypeStruct((2, 8, LANES), F32)
    return pl.pallas_call(
        prep_kernel,
        out_shape=(tall, flat, flat, full, full, last),
        in_specs=[SMEM, VMEM, VMEM, VMEM, VMEM],
        out_specs=(VMEM,) * 6,
        compiler_params=PARAMS,
        cost_estimate=cost(2 * 10**9, 6 * 10**6, 10**5),
        name="prep",
    )(side, own, got, bias, rate)


def state_kernel(recv, tail, last, first_state, payload):
    members, rows, width = recv.shape
    wide = tail.shape[2]
    half = members // 2
    heads = wide // 64
    states = []
    for b in range(2):
        block = recv[b * half : (b + 1) * half].reshape(half * rows, width)
        weighted = (block[:, 0:wide].astype(F32) * tail[b]).astype(BF16)
        states.append(
            lax.dot_general(
                block[:, wide : wide + LANES],
                weighted,
                (((0,), (0,)), ((), ())),
                preferred_element_type=F32,
            )
        )
    decay = widen(jnp.exp(last[1]), spread(LANES, wide, wide // heads))
    first_state[...] = states[0]
    total = decay[0:1] * states[0] + states[1]
    parts, depth, _ = payload.shape
    payload[:, :, 0:wide] = total.reshape(parts, depth, wide)
    log_decay = jnp.broadcast_to(last[0, 0:1] + last[1, 0:1], (depth, LANES))
    for part in range(parts):
        payload[part, :, wide : wide + LANES] = log_decay


def state(recv, tail, last, parts):
    members, rows, width = recv.shape
    wide = tail.shape[2]
    state_rows = (width - wide) // 2
    return pl.pallas_call(
        state_kernel,
        out_shape=(
            jax.ShapeDtypeStruct((state_rows, wide), F32),
            jax.ShapeDtypeStruct((parts, state_rows // parts, wide + LANES), F32),
        ),
        in_specs=[VMEM, VMEM, VMEM],
        out_specs=(VMEM, VMEM),
        compiler_params=PARAMS,
        cost_estimate=cost(2 * members * rows * wide * 128, 8 * members * rows * wide),
        name="state",
    )(recv, tail, last)


def intra_kernel(side_ref, recv, lc, lc_t, dt_t, skip, scale, own, got, out, factor):
    side = side_ref[0]
    half, rows, width = recv.shape
    wide = out.shape[1]
    heads = lc_t.shape[1]
    head_width = wide // heads
    block = recv[...].reshape(half * rows, width)
    xc = block[:, 0:wide]
    scores = lax.dot_general(
        block[:, wide + LANES : wide + 2 * LANES],
        block[:, wide : wide + LANES],
        (((1,), (1,)), ((), ())),
        preferred_element_type=F32,
    )
    lower = iota((BLOCK, BLOCK), 0) >= iota((BLOCK, BLOCK), 1)
    own_heads = skip.shape[1]
    row = iota((own_heads, wide), 0)
    gain = widen(
        jnp.broadcast_to(skip[...], (8, own_heads)),
        (iota((own_heads, wide), 1) // head_width + heads * side == row).astype(F32),
    )[0:1]
    gate = jnp.where(pl.program_id(0) == side, own[...].astype(F32), got[...].astype(F32))
    gate = silu(gate)
    factor[...] = gate * scale[0]
    cum = lc[0]
    for pair in range(heads // 2):
        outs = []
        for h in (2 * pair, 2 * pair + 1):
            gap = cum[:, h : h + 1] - lc_t[0, h : h + 1]
            decay = jnp.exp(jnp.where(lower, gap, -jnp.inf))
            weights = (scores * (decay * dt_t[0, h : h + 1])).astype(BF16)
            outs.append(
                jnp.dot(
                    weights,
                    xc[:, h * head_width : (h + 1) * head_width],
                    preferred_element_type=F32,
                )
            )
        cols = slice(2 * pair * head_width, 2 * (pair + 1) * head_width)
        mixed = jnp.concatenate(outs, axis=1) + gain[:, cols] * xc[:, cols].astype(F32)
        out[:, cols] = mixed * gate[:, cols]


def intra(side, recv, lc, lc_t, dt_t, skip, scale, gate, got):
    members, rows, width = recv.shape
    wide = scale.shape[2]
    total = members * rows
    heads = lc_t.shape[1]
    half = members // 2
    return pl.pallas_call(
        intra_kernel,
        out_shape=(jax.ShapeDtypeStruct((total, wide), F32),) * 2,
        grid_spec=pltpu.PrefetchScalarGridSpec(
            num_scalar_prefetch=1,
            grid=(2,),
            in_specs=[
                pl.BlockSpec((half, rows, width), lambda b, s: (b, 0, 0)),
                pl.BlockSpec((1, BLOCK, LANES), lambda b, s: (b, 0, 0)),
                pl.BlockSpec((1, heads, BLOCK), lambda b, s: (b, 0, 0)),
                pl.BlockSpec((1, heads, BLOCK), lambda b, s: (b, 0, 0)),
                pl.BlockSpec(skip.shape, lambda b, s: (0, 0)),
                pl.BlockSpec((1, BLOCK, wide), lambda b, s: (b, 0, 0)),
                pl.BlockSpec((BLOCK, wide), lambda b, s: (0, s[0])),
                pl.BlockSpec(got.shape, lambda b, s: (0, 0)),
            ],
            out_specs=(pl.BlockSpec((BLOCK, wide), lambda b, s: (b, 0)),) * 2,
        ),
        compiler_params=PARAMS,
        cost_estimate=cost(2 * total * BLOCK * wide * 4, 12 * total * wide, heads * total * BLOCK),
        name="intra",
    )(side, recv, lc, lc_t, dt_t, skip, scale, gate, got)


def scan_kernel(recv, out):
    chunks, rows, width = recv.shape
    wide = out.shape[2]
    one_hot = spread(LANES, wide, 64)
    logs = jnp.concatenate([recv[k, 0:1, wide:width] for k in range(chunks)], axis=0)
    decay = jnp.dot(jnp.exp(logs), one_hot, precision=HIGH, preferred_element_type=F32)
    carry = jnp.zeros((rows, wide), F32)
    for k in range(chunks):
        out[k] = carry
        carry = decay[k : k + 1] * carry + recv[k, :, 0:wide]


def scan(recv):
    chunks, rows, width = recv.shape
    return pl.pallas_call(
        scan_kernel,
        out_shape=jax.ShapeDtypeStruct((chunks, rows, width - LANES), F32),
        in_specs=[VMEM],
        out_specs=VMEM,
        compiler_params=PARAMS,
        cost_estimate=cost(4 * chunks * rows * width, 4 * chunks * rows * width),
        name="scan",
    )(recv)


def finish_kernel(side_ref, carry, first_state, recv, last, mixed, factor, gain, out):
    b = pl.program_id(0)
    half, rows, width = recv.shape
    wide = mixed.shape[1]
    state_rows = first_state.shape[0]
    start = carry[...].reshape(state_rows, wide)
    decay = widen(jnp.exp(last[0]), spread(LANES, wide, 64))[0:1]
    start = jnp.where(b == 0, start, decay * start + first_state[...]).astype(BF16)
    read = recv[:, :, wide + LANES : wide + 2 * LANES].reshape(half * rows, LANES)
    carried = jnp.dot(read, start, preferred_element_type=F32)
    gated = mixed[...] + carried * factor[...]
    inv = lax.rsqrt(jnp.mean(gated * gated, axis=1, keepdims=True) + 1e-5)
    out[...] = (gated * inv * gain[...]).astype(BF16).reshape(out.shape)


def finish(side, carry, first_state, recv, last, mixed, factor, gain):
    total, wide = mixed.shape
    members, rows, width = recv.shape
    half = members // 2

    def whole(shape):
        return pl.BlockSpec(shape, lambda b, s: (0,) * len(shape))

    return pl.pallas_call(
        finish_kernel,
        out_shape=jax.ShapeDtypeStruct((members, rows, wide), BF16),
        grid_spec=pltpu.PrefetchScalarGridSpec(
            num_scalar_prefetch=1,
            grid=(2,),
            in_specs=[
                whole(carry.shape),
                whole(first_state.shape),
                pl.BlockSpec((half, rows, width), lambda b, s: (b, 0, 0)),
                whole(last.shape),
                pl.BlockSpec((BLOCK, wide), lambda b, s: (b, 0)),
                pl.BlockSpec((BLOCK, wide), lambda b, s: (b, 0)),
                pl.BlockSpec((1, wide), lambda b, s: (0, s[0])),
            ],
            out_specs=pl.BlockSpec((half, rows, wide), lambda b, s: (b, 0, 0)),
        ),
        compiler_params=PARAMS,
        cost_estimate=cost(2 * total * wide * 200, 10 * total * wide),
        name="finish",
    )(side, carry, first_state, recv, last, mixed, factor, gain)


def on_device(
    inner_raw,
    pairs_raw,
    gate_raw,
    step_raw,
    step_bias,
    rate_log,
    skip_gain,
    conv_inner,
    conv_pairs,
    norm_gain,
):
    places = lax.axis_size("context")
    shards = lax.axis_size("head")
    chunks = places // 2
    side = (lax.axis_index("context") % 2).astype(jnp.int32)
    side_arr = side.reshape(1)
    rows = inner_raw.shape[0]
    partner = [(c, c ^ 1) for c in range(places)]
    after = [(d, d + 1) for d in range(places * shards - 1)]
    teams = [list(range(8 * k, 8 * k + 8)) for k in range(places * shards // 8)]
    lines = [[2 * k + s for k in range(chunks)] for s in range(2)]

    halo_inner = lax.ppermute(inner_raw[rows - 8 :], ("context", "head"), after)
    pairs = pairs_raw.reshape(rows, -1)
    halo_pairs = lax.ppermute(pairs[rows - 8 :], ("context", "head"), after)
    step_got = lax.ppermute(step_raw, "context", partner)
    pair_taps = conv_pairs.reshape(conv_pairs.shape[0], -1)
    packed = conv(inner_raw, pairs, conv_inner, pair_taps)
    packed = fix(inner_raw, pairs, halo_inner, halo_pairs, conv_inner, pair_taps, packed)
    packed, step_got = lax.optimization_barrier((packed, step_got))
    recv = lax.all_to_all(
        packed, ("context", "head"), split_axis=0, concat_axis=0, axis_index_groups=teams
    )
    half = gate_raw.shape[1] // 2
    gate_out = lax.dynamic_slice_in_dim(gate_raw, (1 - side) * half, half, 1)
    gate_out, recv = lax.optimization_barrier((gate_out, recv))
    gate_got = lax.ppermute(gate_out, "context", partner)

    lc, lc_t, dt_t, tail, scale, last = prep(
        side_arr, step_raw, step_got, step_bias.reshape(1, -1), rate_log.reshape(1, -1), half
    )
    first_state, payload = state(recv, tail, last, chunks)
    states = lax.all_to_all(
        payload, "context", split_axis=0, concat_axis=0, axis_index_groups=lines
    )
    states, gate_got = lax.optimization_barrier((states, gate_got))
    carries = scan(states)
    carry = lax.all_to_all(
        carries, "context", split_axis=0, concat_axis=0, axis_index_groups=lines
    )
    mixed, factor = intra(
        side_arr, recv, lc, lc_t, dt_t, skip_gain.reshape(1, -1), scale, gate_raw, gate_got
    )
    slabs = finish(
        side_arr, carry, first_state, recv, last, mixed, factor, norm_gain.reshape(1, -1)
    )
    slabs = lax.all_to_all(
        slabs, ("context", "head"), split_axis=0, concat_axis=0, axis_index_groups=teams
    )
    return unpack(slabs)


def solution(mesh):
    placed = (
        P(("rollout", "context", "head"), None),
        P(("rollout", "context", "head"), None, None, None),
        P(("rollout", "context"), "head"),
        P(("rollout", "context"), "head"),
        P("head"),
        P("head"),
        P("head"),
        P(),
        P(),
        P("head"),
    )
    return jax.shard_map(
        on_device,
        mesh=mesh,
        in_specs=placed,
        out_specs=P(("rollout", "context", "head"), None),
        check_vma=False,
    )
```

time: 112 us -> 128 us (1.14)
  blocking collectives: 44.5 us -> 15.6 us
  starting transfers between devices: 16.3 us -> 34.7 us
  local copies, waits for them, and re-layouts: 6.9 us -> 22.7 us
  waiting for transfers between devices: 23.2 us -> 32.9 us
  Pallas kernels: 18.4 us -> 20.6 us
    all_to_all x1 -> x0, blocking collectives: 29.4 us -> none  [on_device(): lax.all_to_all(payload, 'context', split_axis=0, concat_axis=0, axis_inde...]
    ppermute x1, waiting for transfers between devices: 14.7 us -> 0.01 us  [on_device(): step_got = lax.ppermute(step_raw, 'context', partner)]
    unnamed x25 -> x39, local copies, waits for them, and re-layouts: 4.89 us -> 18.2 us
    all_to_all x0 -> x1, starting transfers between devices: none -> 10.8 us  [on_device(): lax.all_to_all(payload, 'context', split_axis=0, concat_axis=0, axis_inde...]
    ppermute x1, waiting for transfers between devices: 8.45 us -> 18.2 us  [on_device(): gate_got = lax.ppermute(gate_out, 'context', partner)]
    all_to_all x1, waiting for transfers between devices: 0.01 us -> 8.49 us  [on_device(): lax.all_to_all(carries, 'context', split_axis=0, concat_axis=0, axis_inde...]
    all_to_all x1, starting transfers between devices: 3.57 us -> 9.87 us  [on_device(): lax.all_to_all(carries, 'context', split_axis=0, concat_axis=0, axis_inde...]
    all_to_all x1, waiting for transfers between devices: 0.01 us -> 6.08 us  [on_device(): lax.all_to_all(packed, ('context', 'head'), split_axis=0, concat_axis=0,...]
  transfers between devices with their start and end apart: 5 -> 7, of which waited for: 2 -> 4; matrix products, arithmetic and copies ran while one was open for 1% -> 4% of each run, Pallas kernels for 8% -> 12%
where the time goes in v2:
time: 128 us; the launch traced here: 127 us
  starting transfers between devices  34.7 us (27%)
  waiting for transfers between devices  32.9 us (26%)
  local copies, waits for them, and re-layouts  22.7 us (18%)
  Pallas kernels  20.6 us (16%)
  blocking collectives  15.6 us (12%)
    unnamed x39, local copies, waits for them, and re-layouts  18.2 us
    ppermute x1, waiting for transfers between devices, on_device(): gate_got = lax.ppermute(gate_out, 'context', partner)  18.2 us
    all_to_all x1, blocking collectives, on_device(): lax.all_to_all(slabs, ('context', 'head'), split_axis=0, concat_axis=0, a...  15.6 us
    all_to_all x1, starting transfers between devices, on_device(): lax.all_to_all(payload, 'context', split_axis=0, concat_axis=0, axis_inde...  10.8 us
    all_to_all x1, starting transfers between devices, on_device(): lax.all_to_all(carries, 'context', split_axis=0, concat_axis=0, axis_inde...  9.87 us
    all_to_all x1, waiting for transfers between devices, on_device(): lax.all_to_all(carries, 'context', split_axis=0, concat_axis=0, axis_inde...  8.49 us
    all_to_all x1, waiting for transfers between devices, on_device(): lax.all_to_all(packed, ('context', 'head'), split_axis=0, concat_axis=0,...  6.08 us
    pallas_call x1, Pallas kernels, prep(): pl.pallas_call(prep_kernel, out_shape=(tall, flat, flat, full, full, last...  5.29 us
  transfers between devices with their start and end apart: 7, of which 4 were waited for; matrix products, arithmetic and copies ran while one was open for 4% of the time, Pallas kernels for 12%

profile of v2, /device:TPU:8, one launch (start us, length us, event | category | flops | bytes accessed | tf_op | source)
XLA Modules:
  0.0 126.6 jit_solution(9584761419142808383)
XLA Ops:
  0.0 0.9 slice.9
  0.9 3.5 %collective-permute-start = (bf16[8,8192]{1,0:T(8,128)(2,1)S(1)}, bf16[8,8192]{1,0:T(8,128)(2,1)S(1)}, u32[]{:S(2)}, u32[]{:S(2)}) collective-permute-start(bf16[8,8192]{1,0:T(8,128)(2,1)S(1)} %slice.9), channel_id=1, source_target_pairs={{0,1},{1,2},{2,3},{3,4},{4,5},{5,6},{6,7},{7,8},{8,9},{9,10},{10,1... | collective-permute-start | bytes 393224 | tf_op jit(solution)/shard_map/ppermute | solution.py:429
  4.4 0.8 slice.10
  5.2 3.2 %collective-permute-start.1 = (bf16[8,2048]{1,0:T(8,128)(2,1)S(1)}, bf16[8,2048]{1,0:T(8,128)(2,1)S(1)}, u32[]{:S(2)}, u32[]{:S(2)}) collective-permute-start(bf16[8,2048]{1,0:T(8,128)(2,1)S(1)} %slice.11), channel_id=1, source_target_pairs={{0,1},{1,2},{2,3},{3,4},{4,5},{5,6},{6,7},{7,8},{8,9},{9,10},{10,1... | collective-permute-start | bytes 98312 | tf_op jit(solution)/shard_map/ppermute | solution.py:431
  8.4 0.8 copy.12.own
  9.3 1.6 %collective-permute-start.2 = (bf16[256,32]{1,0:T(8,128)(2,1)S(1)}, bf16[256,32]{1,0:T(8,128)(2,1)S(1)}, u32[]{:S(2)}, u32[]{:S(2)}) collective-permute-start(bf16[256,32]{1,0:T(8,128)(2,1)S(1)} %copy.12.own), channel_id=1, source_target_pairs={{0,4},{4,0},{8,12},{12,8},{16,20},{20,16},{24,28},{28,24},{32,36},... | collective-permute-start | bytes 49160 | tf_op jit(solution)/shard_map/ppermute | solution.py:432
  10.8 1.1 reshape.23.pairs
  12.0 0.8 reshape.24.w_pairs
  12.8 0.0 copy-start
  12.8 1.2 copy-done
  14.0 0.0 copy-start.10
  14.0 0.9 copy-done.10
  15.0 4.4 %conv.1._ = bf16[8,64,1280]{2,1,0:T(8,128)(2,1)} custom-call(bf16[64,8192]{1,0:T(8,128)(2,1)S(1)} %copy-done, bf16[64,2048]{1,0:T(8,128)(2,1)S(1)} %reshape.23.pairs, f32[5,8192]{1,0:T(8,128)S(1)} %copy-done.10, f32[5,2048]{1,0:T(8,128)S(1)} %reshape.24.w_pairs), custom_call_target="tpu_custom_call" | custom-call | flops 13107200 | bytes 2621440 | tf_op jit(solution)/shard_map/conv/pallas_call | solution.py:71
  19.4 0.0 collective-permute-done.1.halo_pairs
  19.4 0.0 collective-permute-done.halo_inner
  19.4 1.5 %fix.1 = bf16[8,64,1280]{2,1,0:T(8,128)(2,1)} custom-call(bf16[64,8192]{1,0:T(8,128)(2,1)S(1)} %copy-done, bf16[64,2048]{1,0:T(8,128)(2,1)S(1)} %reshape.23.pairs, bf16[8,8192]{1,0:T(8,128)(2,1)S(1)} %collective-permute-done.halo_inner, bf16[8,2048]{1,0:T(8,128)(2,1)S(1)} %collective-permute-done.1.halo_pairs, ...), custom_call_target="tpu_custom_call", output_to_operand_aliasing={{}: (6, {})} | custom-call | flops 3276800 | bytes 1310720 | tf_op jit(solution)/shard_map/fix/pallas_call | solution.py:118
  20.9 0.0 copy-start.1
  20.9 0.0 copy-start.17
  20.9 0.0 copy-start.18
  20.9 0.0 collective-permute-done.2.got
  20.9 4.7 %all-to-all-start = ((bf16[8,64,1280]{2,1,0:T(8,128)(2,1)}), bf16[8,64,1280]{2,1,0:T(8,128)(2,1)S(1)}, u32[]{:S(2)}, u32[]{:S(2)}) async-start(bf16[8,64,1280]{2,1,0:T(8,128)(2,1)} %fix.1), calls=%async_computation | async-start | bytes 2621440 | tf_op jit(solution)/shard_map/all_to_all | solution.py:437
  25.7 0.0 copy-done.1
  25.7 0.9 constant_dynamic-slice_fusion
  26.5 0.0 copy-done.17
  26.5 0.0 copy-done.18
  26.5 5.3 %prep.1 = (f32[2,256,128]{2,1,0:T(8,128)S(1)}, f32[2,16,256]{2,1,0:T(8,128)S(1)}, f32[2,16,256]{2,1,0:T(8,128)S(1)}, f32[2,256,1024]{2,1,0:T(8,128)S(1)}, f32[2,...) custom-call(s32[1]{0:T(128)} %bitcast.side_ref, bf16[256,32]{1,0:T(8,128)(2,1)S(1)} %copy.12.own, ...), custom_call_target="tpu_custom_call" | custom-call | flops 2000000000 | bytes 6000000 | tf_op jit(solution)/shard_map/prep/pallas_call | solution.py:206
  31.8 0.0 copy-start.2
  31.8 1.3 %copy-done.2 = f32[2,256,1024]{2,1,0:T(8,128)} copy-done((f32[2,256,1024]{2,1,0:T(8,128)}, f32[2,256,1024]{2,1,0:T(8,128)S(1)}, u32[]{:S(2)}) %copy-start.2) | copy-done | bytes 2097176
  33.2 0.0 copy-start.4
  33.2 1.3 %copy-done.4 = f32[2,256,1024]{2,1,0:T(8,128)} copy-done((f32[2,256,1024]{2,1,0:T(8,128)}, f32[2,256,1024]{2,1,0:T(8,128)S(1)}, u32[]{:S(2)}) %copy-start.4) | copy-done | bytes 2097176
  34.5 0.0 copy-start.13
  34.5 0.7 copy-done.13
  35.2 6.1 %all-to-all-done.recv = bf16[8,64,1280]{2,1,0:T(8,128)(2,1)S(1)} async-done(((bf16[8,64,1280]{2,1,0:T(8,128)(2,1)}), bf16[8,64,1280]{2,1,0:T(8,128)(2,1)S(1)}, u32[]{:S(2)}, u32[]{:S(2)}) %all-to-all-start) | async-done | bytes 1310752 | tf_op jit(solution)/shard_map/all_to_all | solution.py:437
  41.3 0.0 copy-start.5
  41.3 1.6 %copy-done.5 = f32[2,256,1024]{2,1,0:T(8,128)S(1)} copy-done((f32[2,256,1024]{2,1,0:T(8,128)S(1)}, f32[2,256,1024]{2,1,0:T(8,128)}, u32[]{:S(2)}) %copy-start.5) | copy-done | bytes 2097176
  42.9 1.3 %state.1 = (f32[128,1024]{1,0:T(8,128)S(1)}, f32[16,8,1152]{2,1,0:T(8,128)}) custom-call(bf16[8,64,1280]{2,1,0:T(8,128)(2,1)S(1)} %all-to-all-done.recv, f32[2,256,1024]{2,1,0:T(8,128)S(1)} %copy-done.5, f32[2,8,128]{2,1,0:T(8,128)S(1)} %get-tuple-element.25.last), custom_call_target="tpu_custom_call" | custom-call | flops 134217728 | bytes 4194304 | tf_op jit(solution)/shard_map/state/pallas_call | solution.py:248
  44.1 0.0 copy-start.11
  44.1 0.8 copy-done.11
  45.0 0.0 copy-start.16
  45.0 10.8 %all-to-all-start.1 = ((f32[16,8,1152]{2,1,0:T(8,128)}), f32[16,8,1152]{2,1,0:T(8,128)S(1)}, u32[]{:S(2)}, u32[]{:S(2)}) async-start(f32[16,8,1152]{2,1,0:T(8,128)} %get-tuple-element.26), calls=%async_computation.1 | async-start | bytes 1179648 | tf_op jit(solution)/shard_map/all_to_all | solution.py:449
  55.8 0.9 collective-permute-start.3
  56.8 18.2 %collective-permute-done.3.got = bf16[256,1024]{1,0:T(8,128)(2,1)S(1)} collective-permute-done((bf16[256,1024]{1,0:T(8,128)(2,1)}, bf16[256,1024]{1,0:T(8,128)(2,1)S(1)}, u32[]{:S(2)}, u32[]{:S(2)}) %collective-permute-start.3) | collective-permute-done | bytes 524320 | tf_op jit(solution)/shard_map/ppermute | solution.py:443
  74.9 0.1 all-to-all-done.1.recv
  75.1 1.1 scan.1
  76.2 9.9 %all-to-all-start.2 = ((f32[16,8,1024]{2,1,0:T(8,128)}), f32[16,8,1024]{2,1,0:T(8,128)S(1)}, u32[]{:S(2)}, u32[]{:S(2)}) async-start(f32[16,8,1024]{2,1,0:T(8,128)} %scan.1), calls=%async_computation.2 | async-start | bytes 1048576 | tf_op jit(solution)/shard_map/all_to_all | solution.py:454
  86.1 0.0 copy-done.16
  86.1 0.0 copy-start.3
  86.1 1.6 %copy-done.3 = f32[2,256,1024]{2,1,0:T(8,128)S(1)} copy-done((f32[2,256,1024]{2,1,0:T(8,128)S(1)}, f32[2,256,1024]{2,1,0:T(8,128)}, u32[]{:S(2)}) %copy-start.3) | copy-done | bytes 2097176
  87.7 0.0 copy-start.14
  87.7 0.9 copy-done.14
  88.6 0.0 copy-start.15
  88.6 4.4 %intra.1 = (f32[512,1024]{1,0:T(8,128)S(1)}, f32[512,1024]{1,0:T(8,128)S(1)}) custom-call(s32[1]{0:T(128)} %bitcast.side_ref, bf16[8,64,1280]{2,1,0:T(8,128)(2,1)S(1)} %all-to-all-done.recv, f32[2,256,128]{2,1,0:T(8,128)S(1)} %copy-done.14, f32[2,16,256]{2,1,0:T(8,128)S(1)} %get-tuple-element.31.lc_t, f32[2,16,256]{2,1,0:T(8,128)S(1)} %get-tuple-element.32.dt_t, ...), custom_call_target="tpu_custom_call" | custom-call | flops 1073741824 | bytes 6291456 | tf_op jit(solution)/shard_map/intra/pallas_call | solution.py:311
  93.1 0.0 copy-start.6
  93.1 1.3 %copy-done.6 = f32[512,1024]{1,0:T(8,128)} copy-done((f32[512,1024]{1,0:T(8,128)}, f32[512,1024]{1,0:T(8,128)S(1)}, u32[]{:S(2)}) %copy-start.6) | copy-done | bytes 2097176
  94.4 0.0 copy-start.8
  94.4 1.3 %copy-done.8 = f32[512,1024]{1,0:T(8,128)} copy-done((f32[512,1024]{1,0:T(8,128)}, f32[512,1024]{1,0:T(8,128)S(1)}, u32[]{:S(2)}) %copy-start.8) | copy-done | bytes 2097176
  95.7 8.5 %all-to-all-done.2.carry = f32[16,8,1024]{2,1,0:T(8,128)S(1)} async-done(((f32[16,8,1024]{2,1,0:T(8,128)}), f32[16,8,1024]{2,1,0:T(8,128)S(1)}, u32[]{:S(2)}, u32[]{:S(2)}) %all-to-all-start.2) | async-done | bytes 524320 | tf_op jit(solution)/shard_map/all_to_all | solution.py:454
  104.2 0.0 copy-done.15
  104.2 1.6 %copy-done.7 = f32[512,1024]{1,0:T(8,128)S(1)} copy-done((f32[512,1024]{1,0:T(8,128)S(1)}, f32[512,1024]{1,0:T(8,128)}, u32[]{:S(2)}) %copy-start.7) | copy-done | bytes 2097176
  105.8 1.6 %copy-done.9 = f32[512,1024]{1,0:T(8,128)S(1)} copy-done((f32[512,1024]{1,0:T(8,128)S(1)}, f32[512,1024]{1,0:T(8,128)}, u32[]{:S(2)}) %copy-start.9) | copy-done | bytes 2097176
  107.4 1.0 copy-done.12
  108.5 1.5 %finish.1 = bf16[8,64,1024]{2,1,0:T(8,128)(2,1)S(1)} custom-call(s32[1]{0:T(128)} %bitcast.side_ref, f32[16,8,1024]{2,1,0:T(8,128)S(1)} %all-to-all-done.2.carry, f32[128,1024]{1,0:T(8,128)S(1)} %copy-done.12, bf16[8,64,1280]{2,1,0:T(8,128)(2,1)S(1)} %all-to-all-done.recv, f32[2,8,128]{2,1,0:T(8,128)S(1)} %get-tuple-element.25.last, ...), custom_call_target="tpu_custom_call" | custom-call | flops 209715200 | bytes 5242880 | tf_op jit(solution)/shard_map/finish/pallas_call | solution.py:383
  110.0 15.6 %all_to_all.20.slabs = bf16[8,64,1024]{2,1,0:T(8,128)(2,1)S(1)} all-to-all(bf16[8,64,1024]{2,1,0:T(8,128)(2,1)S(1)} %finish.1), channel_id=1, replica_groups={{0,1,2,3,4,5,6,7},{8,9,10,11,12,13,14,15},{16,17,18,19,20,21,22,23},{24..., dimensions={0} | all-to-all | bytes 2097152 | tf_op jit(solution)/shard_map/all_to_all | solution.py:463
  125.6 1.0 unpack.1
  (4 shorter events, 0.0 us)
Async XLA Ops:
  0.9 18.5 %collective-permute-start = (bf16[8,8192]{1,0:T(8,128)(2,1)S(1)}, bf16[8,8192]{1,0:T(8,128)(2,1)S(1)}, u32[]{:S(2)}, u32[]{:S(2)}) collective-permute-start(bf16[8,8192]{1,0:T(8,128)(2,1)S(1)} %slice.9), channel_id=1, source_target_pairs={{0,1},{1,2},{2,3},{3,4},{4,5},{5,6},{6,7},{7,8},{8,9},{9,10},{10,1... | collective-permute-start | bytes 393224 | tf_op jit(solution)/shard_map/ppermute | solution.py:429
  5.2 14.1 %collective-permute-start.1 = (bf16[8,2048]{1,0:T(8,128)(2,1)S(1)}, bf16[8,2048]{1,0:T(8,128)(2,1)S(1)}, u32[]{:S(2)}, u32[]{:S(2)}) collective-permute-start(bf16[8,2048]{1,0:T(8,128)(2,1)S(1)} %slice.11), channel_id=1, source_target_pairs={{0,1},{1,2},{2,3},{3,4},{4,5},{5,6},{6,7},{7,8},{8,9},{9,10},{10,1... | collective-permute-start | bytes 98312 | tf_op jit(solution)/shard_map/ppermute | solution.py:431
  9.3 11.6 %collective-permute-start.2 = (bf16[256,32]{1,0:T(8,128)(2,1)S(1)}, bf16[256,32]{1,0:T(8,128)(2,1)S(1)}, u32[]{:S(2)}, u32[]{:S(2)}) collective-permute-start(bf16[256,32]{1,0:T(8,128)(2,1)S(1)} %copy.12.own), channel_id=1, source_target_pairs={{0,4},{4,0},{8,12},{12,8},{16,20},{20,16},{24,28},{28,24},{32,36},... | collective-permute-start | bytes 49160 | tf_op jit(solution)/shard_map/ppermute | solution.py:432
  12.8 1.2 copy-start
  14.0 0.9 copy-start.10
  20.9 4.8 %copy-start.1 = (bf16[256,2048]{1,0:T(8,128)(2,1)S(1)}, bf16[256,2048]{1,0:T(8,128)(2,1)}, u32[]{:S(2)}) copy-start(bf16[256,2048]{1,0:T(8,128)(2,1)} %own.2) | copy-start | bytes 3145732
  20.9 5.6 %copy-start.17 = (f32[32]{0:T(128)S(1)}, f32[32]{0:T(128)}, u32[]{:S(2)}) copy-start(f32[32]{0:T(128)} %param.14) | copy-start | bytes 388
  20.9 5.6 %copy-start.18 = (f32[32]{0:T(128)S(1)}, f32[32]{0:T(128)}, u32[]{:S(2)}) copy-start(f32[32]{0:T(128)} %param.15) | copy-start | bytes 388
  20.9 20.3 %all-to-all-start = ((bf16[8,64,1280]{2,1,0:T(8,128)(2,1)}), bf16[8,64,1280]{2,1,0:T(8,128)(2,1)S(1)}, u32[]{:S(2)}, u32[]{:S(2)}) async-start(bf16[8,64,1280]{2,1,0:T(8,128)(2,1)} %fix.1), calls=%async_computation | async-start | bytes 2621440 | tf_op jit(solution)/shard_map/all_to_all | solution.py:437
  31.8 1.3 %copy-start.2 = (f32[2,256,1024]{2,1,0:T(8,128)}, f32[2,256,1024]{2,1,0:T(8,128)S(1)}, u32[]{:S(2)}) copy-start(f32[2,256,1024]{2,1,0:T(8,128)S(1)} %get-tuple-element.33.scale) | copy-start | bytes 6291460
  33.2 1.3 %copy-start.4 = (f32[2,256,1024]{2,1,0:T(8,128)}, f32[2,256,1024]{2,1,0:T(8,128)S(1)}, u32[]{:S(2)}) copy-start(f32[2,256,1024]{2,1,0:T(8,128)S(1)} %get-tuple-element.24.tail) | copy-start | bytes 6291460
  34.5 0.7 copy-start.13
  41.3 1.6 %copy-start.5 = (f32[2,256,1024]{2,1,0:T(8,128)S(1)}, f32[2,256,1024]{2,1,0:T(8,128)}, u32[]{:S(2)}) copy-start(f32[2,256,1024]{2,1,0:T(8,128)} %copy-done.4) | copy-start | bytes 6291460
  44.1 0.8 copy-start.11
  45.0 41.1 %copy-start.16 = (f32[32]{0:T(128)S(1)}, f32[32]{0:T(128)}, u32[]{:S(2)}) copy-start(f32[32]{0:T(128)} %param.16) | copy-start | bytes 388
  45.0 30.1 %all-to-all-start.1 = ((f32[16,8,1152]{2,1,0:T(8,128)}), f32[16,8,1152]{2,1,0:T(8,128)S(1)}, u32[]{:S(2)}, u32[]{:S(2)}) async-start(f32[16,8,1152]{2,1,0:T(8,128)} %get-tuple-element.26), calls=%async_computation.1 | async-start | bytes 1179648 | tf_op jit(solution)/shard_map/all_to_all | solution.py:449
  55.8 19.1 %collective-permute-start.3 = (bf16[256,1024]{1,0:T(8,128)(2,1)}, bf16[256,1024]{1,0:T(8,128)(2,1)S(1)}, u32[]{:S(2)}, u32[]{:S(2)}) collective-permute-start(bf16[256,1024]{1,0:T(8,128)(2,1)} %constant_dynamic-slice_fusion), channel_id=1, source_target_pairs={{0,4},{4,0},{8,12},{12,8},{16,20},{20,16},{24,28},{28,24},{32,36},... | collective-permute-start | bytes 1572872 | tf_op jit(solution)/shard_map/ppermute | solution.py:443
  76.2 28.0 %all-to-all-start.2 = ((f32[16,8,1024]{2,1,0:T(8,128)}), f32[16,8,1024]{2,1,0:T(8,128)S(1)}, u32[]{:S(2)}, u32[]{:S(2)}) async-start(f32[16,8,1024]{2,1,0:T(8,128)} %scan.1), calls=%async_computation.2 | async-start | bytes 1048576 | tf_op jit(solution)/shard_map/all_to_all | solution.py:454
  86.1 1.6 %copy-start.3 = (f32[2,256,1024]{2,1,0:T(8,128)S(1)}, f32[2,256,1024]{2,1,0:T(8,128)}, u32[]{:S(2)}) copy-start(f32[2,256,1024]{2,1,0:T(8,128)} %copy-done.2) | copy-start | bytes 6291460
  87.7 0.9 copy-start.14
  88.6 15.6 %copy-start.15 = (f32[2048]{0:T(1024)S(1)}, f32[2048]{0:T(1024)}, u32[]{:S(2)}) copy-start(f32[2048]{0:T(1024)} %param.19) | copy-start | bytes 24580
  93.1 1.3 %copy-start.6 = (f32[512,1024]{1,0:T(8,128)}, f32[512,1024]{1,0:T(8,128)S(1)}, u32[]{:S(2)}) copy-start(f32[512,1024]{1,0:T(8,128)S(1)} %get-tuple-element.35.mixed) | copy-start | bytes 6291460
  94.4 1.3 %copy-start.8 = (f32[512,1024]{1,0:T(8,128)}, f32[512,1024]{1,0:T(8,128)S(1)}, u32[]{:S(2)}) copy-start(f32[512,1024]{1,0:T(8,128)S(1)} %get-tuple-element.36.factor) | copy-start | bytes 6291460
  104.2 1.6 %copy-start.7 = (f32[512,1024]{1,0:T(8,128)S(1)}, f32[512,1024]{1,0:T(8,128)}, u32[]{:S(2)}) copy-start(f32[512,1024]{1,0:T(8,128)} %copy-done.6) | copy-start | bytes 6291460
  105.8 1.6 %copy-start.9 = (f32[512,1024]{1,0:T(8,128)S(1)}, f32[512,1024]{1,0:T(8,128)}, u32[]{:S(2)}) copy-start(f32[512,1024]{1,0:T(8,128)} %copy-done.8) | copy-start | bytes 6291460
  107.4 1.0 copy-start.12

commit v3 on v0

v3 whole, which is shorter than its diff:
```python
import functools

import jax
import jax.numpy as jnp
from jax import lax
from jax.experimental import pallas as pl
from jax.experimental.pallas import tpu as pltpu
from jax.sharding import PartitionSpec as P

BLOCK = 256
HIGH = lax.Precision.HIGHEST
F32 = jnp.float32
BF16 = jnp.bfloat16
LANES = 128
ANY = pl.BlockSpec(memory_space=pl.ANY)
VMEM = pl.BlockSpec(memory_space=pltpu.VMEM)
SMEM = pl.BlockSpec(memory_space=pltpu.SMEM)
HBM = pl.BlockSpec(memory_space=pltpu.HBM)
PARAMS = pltpu.CompilerParams(vmem_limit_bytes=24 * 1024 * 1024)
LARGE = pltpu.CompilerParams(vmem_limit_bytes=56 * 1024 * 1024)
TEAM = 16
EXTRA = 8


def cost(flops, bytes_accessed, transcendentals=0):
    return pl.CostEstimate(
        flops=flops, bytes_accessed=bytes_accessed, transcendentals=transcendentals
    )


def iota(shape, dim):
    return lax.broadcasted_iota(jnp.int32, shape, dim)


def spread(rows, channels):
    return (iota((rows, channels), 1) // 64 == iota((rows, channels), 0)).astype(F32)


def widen(value, one_hot):
    return jnp.dot(value, one_hot, precision=HIGH, preferred_element_type=F32)


def columns(value):
    padding = jnp.zeros((LANES - value.shape[0], value.shape[1]), F32)
    return jnp.concatenate([value, padding], axis=0).T


def silu(v):
    return v / (1.0 + jnp.exp(-v))


def pack_kernel(place, inner, pairs, steps, gain, out, extra, sem, pairs_sem, extra_sem):
    x = place[0]
    rows, full = inner.shape
    wide, narrow = full // TEAM, pairs.shape[1] // 8
    copies = []
    for member in range(TEAM):
        px, py = member // 4, member % 4
        copies.append(
            pltpu.make_async_copy(
                inner.at[:, pl.ds((4 * py + px) * wide, wide)],
                out.at[member, pl.ds(0, rows), pl.ds(0, wide)],
                sem.at[member],
            )
        )
        copies.append(
            pltpu.make_async_copy(
                pairs.at[:, pl.ds((2 * py + px // 2) * narrow, narrow)],
                out.at[member, pl.ds(0, rows), pl.ds(wide, narrow)],
                pairs_sem.at[member],
            )
        )
    for copy in copies:
        copy.start()
    mine = jnp.zeros((1, wide), F32)
    for px in range(4):
        mine = jnp.where(x == px, gain[:, px * wide : (px + 1) * wide], mine)
    top = mine.astype(BF16).astype(F32)
    mid = (mine - top).astype(BF16).astype(F32)
    low = (mine - top - mid).astype(BF16).astype(F32)
    row = iota((EXTRA, wide), 0)
    pieces = jnp.where(row == 0, top, jnp.where(row == 1, mid, jnp.where(row == 2, low, 0.0)))
    pieces = pieces.astype(BF16)
    span = steps.shape[1]
    for member in range(TEAM):
        px = member // 4
        extra[member, :, 0:span] = steps[8 * px : 8 * px + 8]
        extra[member, :, span:] = pieces
    last = pltpu.make_async_copy(extra, out.at[:, pl.ds(rows, EXTRA)], extra_sem)
    last.start()
    for copy in copies:
        copy.wait()
    last.wait()


def pack(place, inner, pairs, steps, gain):
    rows = inner.shape[0]
    width = inner.shape[1] // TEAM + pairs.shape[1] // 8
    return pl.pallas_call(
        pack_kernel,
        out_shape=jax.ShapeDtypeStruct((TEAM, rows + EXTRA, width), BF16),
        in_specs=[SMEM, HBM, ANY, VMEM, VMEM],
        out_specs=ANY,
        scratch_shapes=[
            pltpu.VMEM((TEAM, EXTRA, width), BF16),
            pltpu.SemaphoreType.DMA((TEAM,)),
            pltpu.SemaphoreType.DMA((TEAM,)),
            pltpu.SemaphoreType.DMA,
        ],
        compiler_params=PARAMS,
        cost_estimate=cost(0, 4 * TEAM * rows * width),
        name="pack",
    )(place, inner, pairs, steps, gain)


def taps(ext, row, rows, cols, weight):
    window = ext[pl.ds(row, rows + 8), cols]
    total = weight[4:5] + weight[0:1] * window[4 : 4 + rows]
    for k in range(1, 4):
        total = total + weight[k : k + 1] * window[4 + k : 4 + k + rows]
    return silu(total).astype(BF16)


def conv_kernel(
    place, recv, w_inner, w_pairs, bias, rate, xc, bc, lc_t, dt_t, tail, decay, logs, gains, ext
):
    x, y = place[0], place[1]
    members, tall, width = recv.shape
    rows = tall - EXTRA
    wide = xc.shape[1]
    ext[0:8] = jnp.zeros((8, width), F32)
    for m in range(members):
        ext[8 + m * rows : 8 + (m + 1) * rows] = recv[m, 0:rows].astype(F32)

    def chunk(m, _):
        row = pl.multiple_of(m * rows, rows)
        for start in range(0, wide, LANES):
            cols = slice(start, start + LANES)
            xc[pl.ds(row, rows), cols] = taps(ext, row, rows, cols, w_inner[:, cols])
        for start in range(0, width - wide, LANES):
            bc[pl.ds(row, rows), start : start + LANES] = taps(
                ext,
                row,
                rows,
                slice(wide + start, wide + start + LANES),
                w_pairs[:, start : start + LANES],
            )
        return 0

    lax.fori_loop(0, members, chunk, 0)

    own = bias.shape[1]
    mine = iota((8, own), 1) == 8 * x + iota((8, own), 0)
    shift = jnp.sum(jnp.where(mine, bias[...], 0.0), axis=1, keepdims=True)
    speed = jnp.sum(jnp.where(mine, -jnp.exp(rate[...]), 0.0), axis=1, keepdims=True)
    upper = (iota((BLOCK, BLOCK), 0) <= iota((BLOCK, BLOCK), 1)).astype(F32)
    one_hot = spread(LANES, wide)
    total = jnp.zeros((8, 1), F32)
    for b in range(4):
        v = recv[4 * b + y, rows:tall, 0:BLOCK].astype(F32) + shift
        step = jnp.maximum(v, 0.0) + jnp.log1p(jnp.exp(-jnp.abs(v)))
        cum = widen(step * speed, upper)
        end = cum[:, BLOCK - 1 : BLOCK]
        total = total + end
        lc_t[b] = cum
        dt_t[b] = step
        tail[b] = widen(columns(jnp.exp(end - cum) * step), one_hot)
        ends = columns(jnp.broadcast_to(end, (8, LANES)))
        decay[b] = widen(jnp.exp(ends[0:8]), one_hot)
    logs[...] = columns(jnp.broadcast_to(total, (8, LANES)))[0:8]
    for m in range(members):
        pieces = recv[m, rows:tall, BLOCK:].astype(F32)
        gains[m : m + 1] = pieces[0:1] + pieces[1:2] + pieces[2:3]


def whole(shape):
    return pl.BlockSpec(shape, lambda i, p: (0,) * len(shape))


def weight_specs(wide, narrow):
    return [
        pl.BlockSpec((5, wide), lambda i, p: (0, 4 * p[1] + p[0])),
        pl.BlockSpec((5, narrow), lambda i, p: (0, 2 * p[1] + lax.div(p[0], 2))),
    ]


def conv(place, recv, w_inner, w_pairs, bias, rate):
    members, tall, width = recv.shape
    wide = w_inner.shape[1] // TEAM
    narrow = width - wide
    total = members * (tall - EXTRA)
    shapes = (
        ((total, wide), BF16),
        ((total, narrow), BF16),
        ((4, 8, BLOCK), F32),
        ((4, 8, BLOCK), F32),
        ((4, BLOCK, wide), F32),
        ((4, 8, wide), F32),
        ((8, LANES), F32),
        ((members, wide), F32),
    )
    return pl.pallas_call(
        conv_kernel,
        out_shape=tuple(jax.ShapeDtypeStruct(*s) for s in shapes),
        grid_spec=pltpu.PrefetchScalarGridSpec(
            num_scalar_prefetch=1,
            grid=(1,),
            in_specs=[whole(recv.shape)]
            + weight_specs(wide, narrow)
            + [whole(bias.shape), whole(rate.shape)],
            out_specs=tuple(whole(s[0]) for s in shapes),
            scratch_shapes=[pltpu.VMEM((8 + total, width), F32)],
        ),
        compiler_params=PARAMS,
        cost_estimate=cost(20 * total * width, 4 * total * width, 2 * total * width),
        name="conv",
    )(place, recv, w_inner, w_pairs, bias, rate)


def state_kernel(
    place, first, halo, w_inner, w_pairs, xc0, bc0, tail, decay, logs, xc, bc, states, payload, ext
):
    count = first.shape[0]
    wide = xc.shape[1]
    narrow = bc.shape[1]
    ext[0:8] = halo[count - 8 : count].astype(F32)
    ext[8 : 8 + count] = first[...].astype(F32)
    xc[...] = xc0[...]
    bc[...] = bc0[...]
    for start in range(0, wide, LANES):
        cols = slice(start, start + LANES)
        xc[0:count, cols] = taps(ext, 0, count, cols, w_inner[:, cols])
    for start in range(0, narrow, LANES):
        bc[0:count, start : start + LANES] = taps(
            ext,
            0,
            count,
            slice(wide + start, wide + start + LANES),
            w_pairs[:, start : start + LANES],
        )
    total = jnp.zeros((LANES, wide), F32)
    for b in range(4):
        rows = slice(b * BLOCK, (b + 1) * BLOCK)
        weighted = (xc[rows].astype(F32) * tail[b]).astype(BF16)
        local = lax.dot_general(
            bc[rows, 0:LANES],
            weighted,
            (((0,), (0,)), ((), ())),
            preferred_element_type=F32,
        )
        states[b] = local
        total = decay[b, 0:1] * total + local
    parts, depth, _ = payload.shape
    payload[:, :, 0:wide] = total.reshape(parts, depth, wide)
    for part in range(parts):
        for row in range(0, depth, 8):
            payload[part, row : row + 8, wide : wide + LANES] = logs[...]


def state(place, first, halo, w_inner, w_pairs, xc0, bc0, tail, decay, logs, parts):
    count, width = first.shape
    total, wide = xc0.shape
    narrow = width - wide
    shapes = (
        ((total, wide), BF16),
        ((total, narrow), BF16),
        ((4, LANES, wide), F32),
        ((parts, LANES // parts, wide + LANES), F32),
    )
    return pl.pallas_call(
        state_kernel,
        out_shape=tuple(jax.ShapeDtypeStruct(*s) for s in shapes),
        grid_spec=pltpu.PrefetchScalarGridSpec(
            num_scalar_prefetch=1,
            grid=(1,),
            in_specs=[whole(first.shape), whole(halo.shape)]
            + weight_specs(wide, narrow)
            + [whole(a.shape) for a in (xc0, bc0, tail, decay, logs)],
            out_specs=tuple(whole(s[0]) for s in shapes),
            scratch_shapes=[pltpu.VMEM((8 + count, width), F32)],
        ),
        compiler_params=PARAMS,
        cost_estimate=cost(2 * total * wide * LANES, 8 * total * wide),
        name="state",
    )(place, first, halo, w_inner, w_pairs, xc0, bc0, tail, decay, logs)


def intra_kernel(place, xc, bc, lc_t, dt_t, skip, gate_rows, out, factor):
    wide = out.shape[1]
    heads = lc_t.shape[1]
    scores = lax.dot_general(
        bc[:, LANES:], bc[:, 0:LANES], (((1,), (1,)), ((), ())), preferred_element_type=F32
    )
    lower = iota((BLOCK, BLOCK), 0) >= iota((BLOCK, BLOCK), 1)
    own = skip.shape[1]
    gain = widen(
        jnp.broadcast_to(skip[...], (8, own)),
        (iota((own, wide), 1) // 64 + heads * place[0] == iota((own, wide), 0)).astype(F32),
    )[0:1]
    gate = silu(gate_rows[0].astype(F32))
    cum = columns(lc_t[0])
    factor[...] = gate * widen(jnp.exp(cum), spread(LANES, wide))
    for pair in range(heads // 2):
        outs = []
        for h in (2 * pair, 2 * pair + 1):
            gap = cum[:, h : h + 1] - lc_t[0, h : h + 1]
            decay = jnp.exp(jnp.where(lower, gap, -jnp.inf))
            weights = (scores * (decay * dt_t[0, h : h + 1])).astype(BF16)
            outs.append(
                jnp.dot(weights, xc[:, h * 64 : (h + 1) * 64], preferred_element_type=F32)
            )
        cols = slice(2 * pair * 64, 2 * (pair + 1) * 64)
        mixed = jnp.concatenate(outs, axis=1) + gain[:, cols] * xc[:, cols].astype(F32)
        out[:, cols] = mixed * gate[:, cols]


def intra(place, xc, bc, lc_t, dt_t, skip, gate_rows):
    total, wide = xc.shape
    narrow = bc.shape[1]
    heads = lc_t.shape[1]
    return pl.pallas_call(
        intra_kernel,
        out_shape=(jax.ShapeDtypeStruct((total, wide), F32),) * 2,
        grid_spec=pltpu.PrefetchScalarGridSpec(
            num_scalar_prefetch=1,
            grid=(4,),
            in_specs=[
                pl.BlockSpec((BLOCK, wide), lambda b, p: (b, 0)),
                pl.BlockSpec((BLOCK, narrow), lambda b, p: (b, 0)),
                pl.BlockSpec((1, heads, BLOCK), lambda b, p: (b, 0, 0)),
                pl.BlockSpec((1, heads, BLOCK), lambda b, p: (b, 0, 0)),
                whole(skip.shape),
                pl.BlockSpec((1, BLOCK, wide), lambda b, p: (b, 0, 0)),
            ],
            out_specs=(pl.BlockSpec((BLOCK, wide), lambda b, p: (b, 0)),) * 2,
        ),
        compiler_params=LARGE,
        cost_estimate=cost(2 * total * BLOCK * wide * 4, 12 * total * wide, heads * total * BLOCK),
        name="intra",
    )(place, xc, bc, lc_t, dt_t, skip, gate_rows)


def scan_kernel(recv, out):
    chunks, rows, width = recv.shape
    wide = out.shape[2]
    logs = jnp.concatenate([recv[k, 0:1, wide:width] for k in range(chunks)], axis=0)
    logs = jnp.where(iota(logs.shape, 1) < wide // 64, logs, 0.0)
    decay = widen(jnp.exp(logs), spread(LANES, wide))
    carry = jnp.zeros((rows, wide), F32)
    for k in range(chunks):
        out[k] = carry
        carry = decay[k : k + 1] * carry + recv[k, :, 0:wide]


def scan(recv):
    chunks, rows, width = recv.shape
    return pl.pallas_call(
        scan_kernel,
        out_shape=jax.ShapeDtypeStruct((chunks, rows, width - LANES), F32),
        in_specs=[VMEM],
        out_specs=VMEM,
        compiler_params=PARAMS,
        cost_estimate=cost(4 * chunks * rows * width, 8 * chunks * rows * width),
        name="scan",
    )(recv)


def finish_kernel(carry, states, decay, bc, mixed, factor, out, held):
    b = pl.program_id(0)

    @pl.when(b == 0)
    def _():
        held[...] = carry[...].reshape(held.shape)

    start = held[...]
    carried = jnp.dot(bc[:, LANES:], start.astype(BF16), preferred_element_type=F32)
    out[...] = (mixed[...] + carried * factor[...]).astype(BF16).reshape(out.shape)
    held[...] = decay[0, 0:1] * start + states[0]


def finish(carry, states, decay, bc, mixed, factor, rows):
    total, wide = mixed.shape
    narrow = bc.shape[1]
    return pl.pallas_call(
        finish_kernel,
        out_shape=jax.ShapeDtypeStruct((total // rows, rows, wide), BF16),
        grid=(4,),
        in_specs=[
            pl.BlockSpec(carry.shape, lambda b: (0, 0, 0)),
            pl.BlockSpec((1, LANES, wide), lambda b: (b, 0, 0)),
            pl.BlockSpec((1, 8, wide), lambda b: (b, 0, 0)),
            pl.BlockSpec((BLOCK, narrow), lambda b: (b, 0)),
            pl.BlockSpec((BLOCK, wide), lambda b: (b, 0)),
            pl.BlockSpec((BLOCK, wide), lambda b: (b, 0)),
        ],
        out_specs=pl.BlockSpec((BLOCK // rows, rows, wide), lambda b: (b, 0, 0)),
        scratch_shapes=[pltpu.VMEM((LANES, wide), F32)],
        compiler_params=LARGE,
        cost_estimate=cost(2 * total * wide * 200, 10 * total * wide),
        name="finish",
    )(carry, states, decay, bc, mixed, factor)


def post_kernel(slabs, gains, out):
    wide = slabs.shape[2]
    for y in range(4):
        for half in range(2):
            left, right = 8 * half + y, 8 * half + 4 + y
            a, b = slabs[left].astype(F32), slabs[right].astype(F32)
            mean = (
                jnp.sum(a * a, axis=1, keepdims=True) + jnp.sum(b * b, axis=1, keepdims=True)
            ) / (2 * wide)
            inv = lax.rsqrt(mean + 1e-5)
            at = (4 * y + 2 * half) * wide
            out[:, at : at + wide] = (a * inv * gains[left : left + 1]).astype(BF16)
            out[:, at + wide : at + 2 * wide] = (b * inv * gains[right : right + 1]).astype(BF16)


def post(slabs, gains):
    members, rows, wide = slabs.shape
    return pl.pallas_call(
        post_kernel,
        out_shape=jax.ShapeDtypeStruct((rows, members * wide), BF16),
        in_specs=[VMEM, VMEM],
        out_specs=VMEM,
        compiler_params=PARAMS,
        cost_estimate=cost(6 * members * rows * wide, 4 * members * rows * wide),
        name="post",
    )(slabs, gains)


def on_device(
    inner_raw,
    pairs_raw,
    gate_raw,
    step_raw,
    step_bias,
    rate_log,
    skip_gain,
    conv_inner,
    conv_pairs,
    norm_gain,
):
    places = lax.axis_size("context")
    shards = lax.axis_size("head")
    chunks = places // 4
    x = (lax.axis_index("context") % 4).astype(jnp.int32)
    place = jnp.stack([x, lax.axis_index("head").astype(jnp.int32)])
    rows = inner_raw.shape[0]
    after = [(c, c + 4) for c in range(places - 4)]
    teams = [list(range(TEAM * k, TEAM * (k + 1))) for k in range(places * shards // TEAM)]
    lines = [[4 * k + s for k in range(chunks)] for s in range(4)]
    rings = [[4 * k + s for s in range(4)] for k in range(chunks)]

    packed = pack(
        place, inner_raw, pairs_raw.reshape(rows, -1), step_raw.T, norm_gain.reshape(1, -1)
    )
    recv = lax.all_to_all(
        packed, ("context", "head"), split_axis=0, concat_axis=0, axis_index_groups=teams
    )
    gate_rows = gate_raw.reshape(gate_raw.shape[0], 4, -1).transpose(1, 0, 2)
    gate_rows, recv = lax.optimization_barrier((gate_rows, recv))
    halo = lax.ppermute(recv[TEAM - 1, rows - 16 : rows], "context", after)

    pair_taps = conv_pairs.reshape(conv_pairs.shape[0], -1)
    xc0, bc0, lc_t, dt_t, tail, decay, logs, gains = conv(
        place, recv, conv_inner, pair_taps, step_bias.reshape(1, -1), rate_log.reshape(1, -1)
    )
    xc, bc, states, payload = state(
        place, recv[0, :16], halo, conv_inner, pair_taps, xc0, bc0, tail, decay, logs, chunks
    )
    gate_rows = lax.all_to_all(
        gate_rows, "context", split_axis=0, concat_axis=0, axis_index_groups=rings
    )
    totals = lax.all_to_all(
        payload, "context", split_axis=0, concat_axis=0, axis_index_groups=lines
    )
    carry = lax.all_to_all(
        scan(totals), "context", split_axis=0, concat_axis=0, axis_index_groups=lines
    )
    mixed, factor = intra(place, xc, bc, lc_t, dt_t, skip_gain.reshape(1, -1), gate_rows)
    slabs = finish(carry, states, decay, bc, mixed, factor, rows)
    slabs = lax.all_to_all(
        slabs, ("context", "head"), split_axis=0, concat_axis=0, axis_index_groups=teams
    )
    return post(slabs, gains)


def solution(mesh):
    placed = (
        P(("rollout", "context", "head"), None),
        P(("rollout", "context", "head"), None, None, None),
        P(("rollout", "context"), "head"),
        P(("rollout", "context"), "head"),
        P("head"),
        P("head"),
        P("head"),
        P(),
        P(),
        P("head"),
    )
    return jax.shard_map(
        on_device,
        mesh=mesh,
        in_specs=placed,
        out_specs=P(("rollout", "context", "head"), None),
        check_vma=False,
    )
```

time: 500 us -> 125 us (0.25)
  the two profiles are of different devices: /device:TPU:230 before, /device:TPU:8 now
where the time goes in v3:
time: 125 us
  blocking collectives  35.5 us (28%)
  waiting for transfers between devices  35 us (28%)
  Pallas kernels  25.5 us (20%)
  starting transfers between devices  18.1 us (14%)
  local copies, waits for them, and re-layouts  10.2 us (8%)
    all_to_all x1, waiting for transfers between devices, on_device(): lax.all_to_all(packed, ('context', 'head'), split_axis=0, concat_axis=0,...  21.9 us
    all_to_all x1, blocking collectives, on_device(): lax.all_to_all(payload, 'context', split_axis=0, concat_axis=0, axis_inde...  18.5 us
    all_to_all x1, blocking collectives, on_device(): lax.all_to_all(slabs, ('context', 'head'), split_axis=0, concat_axis=0, a...  17 us
    all_to_all x1, waiting for transfers between devices, on_device(): lax.all_to_all(gate_rows, 'context', split_axis=0, concat_axis=0, axis_in...  9.94 us
    pallas_call x1, Pallas kernels, conv(): pl.pallas_call(conv_kernel, out_shape=tuple((jax.ShapeDtypeStruct(*s) for...  7.92 us
    unnamed x33, local copies, waits for them, and re-layouts  7.69 us
    all_to_all x1, starting transfers between devices, on_device(): lax.all_to_all(packed, ('context', 'head'), split_axis=0, concat_axis=0,...  7.4 us
    pallas_call x1, Pallas kernels, intra(): pl.pallas_call(intra_kernel, out_shape=(jax.ShapeDtypeStruct((total, wide...  7.26 us
  transfers between devices with their start and end apart: 4, of which 3 were waited for; matrix products, arithmetic and copies ran while one was open for 2% of the time, Pallas kernels for 13%

profile of v3, /device:TPU:8, one launch (start us, length us, event | category | flops | bytes accessed | tf_op | source)
XLA Modules:
  0.0 124.6 jit_solution(11728258908538096798)
XLA Ops:
  0.0 1.1 reshape.22.pairs
  1.1 0.1 pad_add_fusion.place
  1.2 0.0 copy-start.7
  1.2 0.0 copy-start
  1.2 1.2 copy-done
  2.5 0.0 copy-start.5
  2.5 0.7 copy-done.5
  3.2 0.0 copy-start.6
  3.2 0.7 copy-done.6
  3.9 2.1 %pack.1 = bf16[16,72,768]{2,1,0:T(8,128)(2,1)} custom-call(s32[2]{0:T(128)S(1)} %pad_add_fusion.place, bf16[64,8192]{1,0:T(8,128)(2,1)S(1)} %copy-done, bf16[64,2048]{1,0:T(8,128)(2,1)S(1)} %reshape.22.pairs, bf16[32,256]{1,0:T(8,128)(2,1)S(1)} %bitcast.13, f32[1,2048]{1,0:T(1,128)S(1)} %bitcast.14), custom_call_target="tpu_custom_call" | custom-call | bytes 3145728 | tf_op jit(solution)/shard_map/pack/pallas_call | solution.py:99
  6.0 7.4 %all-to-all-start = ((bf16[16,72,768]{2,1,0:T(8,128)(2,1)}), bf16[16,72,768]{2,1,0:T(8,128)(2,1)S(1)}, u32[]{:S(2)}, u32[]{:S(2)}) async-start(bf16[16,72,768]{2,1,0:T(8,128)(2,1)} %pack.1), calls=%async_computation | async-start | bytes 3538944 | tf_op jit(solution)/shard_map/all_to_all | solution.py:458
  13.4 0.0 copy-start.15
  13.4 0.0 copy-start.4
  13.4 0.0 copy-start.9
  13.4 0.0 copy-start.10
  13.4 1.5 %copy.11 = bf16[256,2048]{0,1:T(8,128)(2,1)S(1)} copy(bf16[256,2048]{1,0:T(8,128)(2,1)} %param.12) | data formatting | bytes 2097152 | tf_op args[2]
  14.9 1.3 %copy.12 = bf16[256,4,512]{2,0,1:T(8,128)(2,1)} copy(bf16[256,4,512]{0,2,1:T(8,128)(2,1)S(1)} %bitcast.17) | data formatting | bytes 2097152 | tf_op jit(solution)/shard_map/reshape | solution.py:461
  16.3 21.9 %all-to-all-done.recv = bf16[16,72,768]{2,1,0:T(8,128)(2,1)S(1)} async-done(((bf16[16,72,768]{2,1,0:T(8,128)(2,1)}), bf16[16,72,768]{2,1,0:T(8,128)(2,1)S(1)}, u32[]{:S(2)}, u32[]{:S(2)}) %all-to-all-start) | async-done | bytes 1769504 | tf_op jit(solution)/shard_map/all_to_all | solution.py:458
  38.2 3.8 %collective-permute-start = (bf16[16,768]{1,0:T(8,128)(2,1)S(1)}, bf16[16,768]{1,0:T(8,128)(2,1)S(1)}, u32[]{:S(2)}, u32[]{:S(2)}) collective-permute-start(bf16[16,768]{1,0:T(8,128)(2,1)S(1)} %get-tuple-element.37), channel_id=1, source_target_pairs={{0,16},{4,20},{8,24},{12,28},{16,32},{20,36},{24,40},{28,44},{32,4... | collective-permute-start | bytes 73736 | tf_op jit(solution)/shard_map/ppermute | solution.py:463
  42.0 0.0 copy-done.15
  42.1 0.0 copy-done.4
  42.1 0.0 copy-done.9
  42.1 0.0 copy-done.10
  42.1 7.9 %conv.1 = (bf16[1024,512]{1,0:T(8,128)(2,1)S(1)}, bf16[1024,256]{1,0:T(8,128)(2,1)S(1)}, f32[4,8,256]{2,1,0:T(8,128)S(1)}, f32[4,8,256]{2,1,0:T(8,128)S(1)}, f32...) custom-call(s32[2]{0:T(128)S(1)} %pad_add_fusion.place, ...), custom_call_target="tpu_custom_call" | custom-call | flops 15728640 | bytes 3145728 | tf_op jit(solution)/shard_map/conv/pallas_call | solution.py:202
  50.0 0.0 copy-start.11
  50.0 0.0 copy-start.12
  50.0 0.0 copy-start.3
  50.0 0.0 collective-permute-done.halo
  50.1 0.0 copy-done.7
  50.1 1.0 state.1
  51.1 0.0 copy-done.11
  51.1 0.0 copy-start.1
  51.1 1.0 copy-done.1
  52.1 0.0 copy-start.2
  52.1 0.8 copy-done.2
  52.9 0.0 copy-start.8
  52.9 1.0 copy-done.8
  53.9 0.0 copy-done.12
  53.9 18.5 %all_to_all.25.recv = f32[8,16,640]{2,1,0:T(8,128)S(1)} all-to-all(f32[8,16,640]{2,1,0:T(8,128)S(1)} %get-tuple-element.27), channel_id=1, replica_groups={{0,16,32,48,64,80,96,112},{4,20,36,52,68,84,100,116},{8,24,40,56,72,88,..., dimensions={0} | all-to-all | bytes 655360 | tf_op jit(solution)/shard_map/all_to_all | solution.py:475
  72.5 0.0 copy-done.3
  72.5 3.5 %all-to-all-start.3 = ((bf16[4,256,512]{2,1,0:T(8,128)(2,1)}), bf16[4,256,512]{2,1,0:T(8,128)(2,1)S(1)}, u32[]{:S(2)}, u32[]{:S(2)}) async-start(bf16[4,256,512]{2,1,0:T(8,128)(2,1)} %bitcast.3), calls=%async_computation.3 | async-start | bytes 2097152 | tf_op jit(solution)/shard_map/all_to_all | solution.py:472
  76.0 0.9 scan.1
  76.9 9.9 %all-to-all-done.3.gate_rows = bf16[4,256,512]{2,1,0:T(8,128)(2,1)S(1)} async-done(((bf16[4,256,512]{2,1,0:T(8,128)(2,1)}), bf16[4,256,512]{2,1,0:T(8,128)(2,1)S(1)}, u32[]{:S(2)}, u32[]{:S(2)}) %all-to-all-start.3) | async-done | bytes 1048608 | tf_op jit(solution)/shard_map/all_to_all | solution.py:472
  86.8 0.0 copy-start.14
  86.8 3.4 %all-to-all-start.2 = ((f32[8,16,512]{2,1,0:T(8,128)}), f32[8,16,512]{2,1,0:T(8,128)S(1)}, u32[]{:S(2)}, u32[]{:S(2)}) async-start(f32[8,16,512]{2,1,0:T(8,128)} %scan.1), calls=%async_computation.2 | async-start | bytes 524288 | tf_op jit(solution)/shard_map/all_to_all | solution.py:478
  90.3 0.0 copy-done.14
  90.3 7.3 %intra.1 = (f32[1024,512]{1,0:T(8,128)}, f32[1024,512]{1,0:T(8,128)}) custom-call(s32[2]{0:T(128)} %copy-done.7, bf16[1024,512]{1,0:T(8,128)(2,1)} %copy-done.8, bf16[1024,256]{1,0:T(8,128)(2,1)} %copy-done.2, f32[4,8,256]{2,1,0:T(8,128)} %copy-done.11, f32[4,8,256]{2,1,0:T(8,128)} %copy-done.12, f32[1,32]{1,0:T(1,128)} %bitcast.18, ...), custom_call_target="tpu_custom_call" | custom-call | flops 1073741824 | bytes 6291456 | tf_op jit(solution)/shard_map/intra/pallas_call | solution.py:321
  97.5 3.1 %all-to-all-done.2.carry = f32[8,16,512]{2,1,0:T(8,128)S(1)} async-done(((f32[8,16,512]{2,1,0:T(8,128)}), f32[8,16,512]{2,1,0:T(8,128)S(1)}, u32[]{:S(2)}, u32[]{:S(2)}) %all-to-all-start.2) | async-done | bytes 262176 | tf_op jit(solution)/shard_map/all_to_all | solution.py:478
  100.7 0.0 copy-start.13
  100.7 0.7 copy-done.13
  101.4 4.9 %finish.1 = bf16[16,64,512]{2,1,0:T(8,128)(2,1)} custom-call(f32[8,16,512]{2,1,0:T(8,128)} %copy-done.13, f32[4,128,512]{2,1,0:T(8,128)} %copy-done.1, f32[4,8,512]{2,1,0:T(8,128)} %copy-done.3, bf16[1024,256]{1,0:T(8,128)(2,1)} %copy-done.2, f32[1024,512]{1,0:T(8,128)} %get-tuple-element.34.mixed, f32[1024,512]{1,0:T(8,128)} %get-tuple-element.35.factor), custom_call_target="tpu_custom_call" | custom-call | flops 209715200 | bytes 5242880 | tf_op jit(solution)/shard_map/finish/pallas_call | solution.py:384
  106.3 17.0 %all_to_all.26.slabs = bf16[16,64,512]{2,1,0:T(8,128)(2,1)S(1)} all-to-all(bf16[16,64,512]{2,1,0:T(8,128)(2,1)} %finish.1), channel_id=1, replica_groups={{0,1,2,3,4,5,6,7,8,9,10,11,12,13,14,15},{16,17,18,19,20,21,22,23,24,25,..., dimensions={0} | all-to-all | bytes 2097152 | tf_op jit(solution)/shard_map/all_to_all | solution.py:483
  123.2 1.4 %post.1 = bf16[64,8192]{1,0:T(8,128)(2,1)} custom-call(bf16[16,64,512]{2,1,0:T(8,128)(2,1)S(1)} %all_to_all.26.slabs, f32[16,512]{1,0:T(8,128)S(1)} %get-tuple-element.36.gains), custom_call_target="tpu_custom_call" | custom-call | flops 3145728 | bytes 2097152 | tf_op jit(solution)/shard_map/post/pallas_call | solution.py:421
  (2 shorter events, 0.0 us)
Async XLA Ops:
  1.2 48.8 %copy-start.7 = (s32[2]{0:T(128)}, s32[2]{0:T(128)S(1)}, u32[]{:S(2)}) copy-start(s32[2]{0:T(128)S(1)} %pad_add_fusion.place) | copy-start | bytes 28
  1.2 1.2 copy-start
  2.5 0.7 copy-start.5
  3.2 0.7 copy-start.6
  6.0 32.3 %all-to-all-start = ((bf16[16,72,768]{2,1,0:T(8,128)(2,1)}), bf16[16,72,768]{2,1,0:T(8,128)(2,1)S(1)}, u32[]{:S(2)}, u32[]{:S(2)}) async-start(bf16[16,72,768]{2,1,0:T(8,128)(2,1)} %pack.1), calls=%async_computation | async-start | bytes 3538944 | tf_op jit(solution)/shard_map/all_to_all | solution.py:458
  13.4 28.7 %copy-start.15 = (f32[5,8,2,128]{3,2,1,0:T(2,128)S(1)}, f32[5,8,2,128]{3,2,1,0:T(2,128)}, u32[]{:S(2)}) copy-start(f32[5,8,2,128]{3,2,1,0:T(2,128)} %param.18) | copy-start | bytes 122884
  13.4 28.7 %copy-start.4 = (f32[5,8192]{1,0:T(8,128)S(1)}, f32[5,8192]{1,0:T(8,128)}, u32[]{:S(2)}) copy-start(f32[5,8192]{1,0:T(8,128)} %w_inner.3) | copy-start | bytes 491524
  13.4 28.7 %copy-start.9 = (f32[32]{0:T(128)S(1)}, f32[32]{0:T(128)}, u32[]{:S(2)}) copy-start(f32[32]{0:T(128)} %param.14) | copy-start | bytes 388
  13.4 28.7 %copy-start.10 = (f32[32]{0:T(128)S(1)}, f32[32]{0:T(128)}, u32[]{:S(2)}) copy-start(f32[32]{0:T(128)} %param.15) | copy-start | bytes 388
  38.2 11.8 %collective-permute-start = (bf16[16,768]{1,0:T(8,128)(2,1)S(1)}, bf16[16,768]{1,0:T(8,128)(2,1)S(1)}, u32[]{:S(2)}, u32[]{:S(2)}) collective-permute-start(bf16[16,768]{1,0:T(8,128)(2,1)S(1)} %get-tuple-element.37), channel_id=1, source_target_pairs={{0,16},{4,20},{8,24},{12,28},{16,32},{20,36},{24,40},{28,44},{32,4... | collective-permute-start | bytes 73736 | tf_op jit(solution)/shard_map/ppermute | solution.py:463
  50.0 1.1 copy-start.11
  50.0 3.9 %copy-start.12 = (f32[4,8,256]{2,1,0:T(8,128)}, f32[4,8,256]{2,1,0:T(8,128)S(1)}, u32[]{:S(2)}) copy-start(f32[4,8,256]{2,1,0:T(8,128)S(1)} %get-tuple-element.32.dt_t) | copy-start | bytes 98308
  50.0 22.4 %copy-start.3 = (f32[4,8,512]{2,1,0:T(8,128)}, f32[4,8,512]{2,1,0:T(8,128)S(1)}, u32[]{:S(2)}) copy-start(f32[4,8,512]{2,1,0:T(8,128)S(1)} %get-tuple-element.25.decay) | copy-start | bytes 196612
  51.1 1.0 copy-start.1
  52.1 0.8 copy-start.2
  52.9 1.0 copy-start.8
  72.5 14.4 %all-to-all-start.3 = ((bf16[4,256,512]{2,1,0:T(8,128)(2,1)}), bf16[4,256,512]{2,1,0:T(8,128)(2,1)S(1)}, u32[]{:S(2)}, u32[]{:S(2)}) async-start(bf16[4,256,512]{2,1,0:T(8,128)(2,1)} %bitcast.3), calls=%async_computation.3 | async-start | bytes 2097152 | tf_op jit(solution)/shard_map/all_to_all | solution.py:472
  86.8 3.4 %copy-start.14 = (bf16[4,256,512]{2,1,0:T(8,128)(2,1)}, bf16[4,256,512]{2,1,0:T(8,128)(2,1)S(1)}, u32[]{:S(2)}) copy-start(bf16[4,256,512]{2,1,0:T(8,128)(2,1)S(1)} %all-to-all-done.3.gate_rows) | copy-start | bytes 3145732
  86.8 13.8 %all-to-all-start.2 = ((f32[8,16,512]{2,1,0:T(8,128)}), f32[8,16,512]{2,1,0:T(8,128)S(1)}, u32[]{:S(2)}, u32[]{:S(2)}) async-start(f32[8,16,512]{2,1,0:T(8,128)} %scan.1), calls=%async_computation.2 | async-start | bytes 524288 | tf_op jit(solution)/shard_map/all_to_all | solution.py:478
  100.7 0.7 copy-start.13

commit v4 on v3

--- a/solution.py
+++ b/solution.py
@@ -28,6 +28,10 @@
     )
 
 
+def keep(array):
+    return pltpu.with_memory_space_constraint(array, pltpu.HBM)
+
+
 def iota(shape, dim):
     return lax.broadcasted_iota(jnp.int32, shape, dim)
 
@@ -43,6 +47,20 @@
 def columns(value):
     padding = jnp.zeros((LANES - value.shape[0], value.shape[1]), F32)
     return jnp.concatenate([value, padding], axis=0).T
+
+
+def split(value):
+    top = value.astype(BF16).astype(F32)
+    mid = (value - top).astype(BF16).astype(F32)
+    return [top, mid, value - top - mid]
+
+
+def spread_columns(value, channels):
+    padding = jnp.zeros((LANES - 24, value.shape[1]), F32)
+    left = jnp.concatenate(split(value) + [padding], axis=0).T.astype(BF16)
+    row = iota((LANES, channels), 0)
+    one_hot = (row % 8 == iota((LANES, channels), 1) // 64) & (row < 24)
+    return jnp.dot(left, one_hot.astype(BF16), preferred_element_type=F32)
 
 
 def silu(v):
@@ -110,7 +128,7 @@
         compiler_params=PARAMS,
         cost_estimate=cost(0, 4 * TEAM * rows * width),
         name="pack",
-    )(place, inner, pairs, steps, gain)
+    )(place, keep(inner), pairs, keep(steps), keep(gain))
 
 
 def taps(ext, row, rows, cols, weight):
@@ -153,21 +171,27 @@
     mine = iota((8, own), 1) == 8 * x + iota((8, own), 0)
     shift = jnp.sum(jnp.where(mine, bias[...], 0.0), axis=1, keepdims=True)
     speed = jnp.sum(jnp.where(mine, -jnp.exp(rate[...]), 0.0), axis=1, keepdims=True)
-    upper = (iota((BLOCK, BLOCK), 0) <= iota((BLOCK, BLOCK), 1)).astype(F32)
-    one_hot = spread(LANES, wide)
-    total = jnp.zeros((8, 1), F32)
+    upper = (iota((BLOCK, BLOCK), 0) <= iota((BLOCK, BLOCK), 1)).astype(BF16)
+    steps = []
     for b in range(4):
         v = recv[4 * b + y, rows:tall, 0:BLOCK].astype(F32) + shift
-        step = jnp.maximum(v, 0.0) + jnp.log1p(jnp.exp(-jnp.abs(v)))
-        cum = widen(step * speed, upper)
+        steps.append(jnp.maximum(v, 0.0) + jnp.log1p(jnp.exp(-jnp.abs(v))))
+    parts = split(jnp.concatenate([step * speed for step in steps], axis=0))
+    parts = jnp.concatenate(parts, axis=0).astype(BF16)
+    sums = jnp.dot(parts, upper, preferred_element_type=F32)
+    ends = jnp.zeros((8, LANES), F32)
+    for b in range(4):
+        cum = sums[8 * b : 8 * b + 8] + sums[8 * b + 32 : 8 * b + 40] + sums[8 * b + 64 : 8 * b + 72]
         end = cum[:, BLOCK - 1 : BLOCK]
-        total = total + end
+        ends = jnp.where(iota((8, LANES), 1) == b, end, ends)
         lc_t[b] = cum
-        dt_t[b] = step
-        tail[b] = widen(columns(jnp.exp(end - cum) * step), one_hot)
-        ends = columns(jnp.broadcast_to(end, (8, LANES)))
-        decay[b] = widen(jnp.exp(ends[0:8]), one_hot)
-    logs[...] = columns(jnp.broadcast_to(total, (8, LANES)))[0:8]
+        dt_t[b] = steps[b]
+        tail[b] = spread_columns(jnp.exp(end - cum) * steps[b], wide)
+    decay[...] = spread_columns(jnp.exp(ends), wide)[0:8]
+    by_block = columns(ends)
+    logs[...] = jnp.broadcast_to(
+        by_block[0:1] + by_block[1:2] + by_block[2:3] + by_block[3:4], (8, LANES)
+    )
     for m in range(members):
         pieces = recv[m, rows:tall, BLOCK:].astype(F32)
         gains[m : m + 1] = pieces[0:1] + pieces[1:2] + pieces[2:3]
@@ -195,7 +219,7 @@
         ((4, 8, BLOCK), F32),
         ((4, 8, BLOCK), F32),
         ((4, BLOCK, wide), F32),
-        ((4, 8, wide), F32),
+        ((8, wide), F32),
         ((8, LANES), F32),
         ((members, wide), F32),
     )
@@ -249,7 +273,7 @@
             preferred_element_type=F32,
         )
         states[b] = local
-        total = decay[b, 0:1] * total + local
+        total = decay[b : b + 1] * total + local
     parts, depth, _ = payload.shape
     payload[:, :, 0:wide] = total.reshape(parts, depth, wide)
     for part in range(parts):
@@ -269,7 +293,7 @@
     )
     return pl.pallas_call(
         state_kernel,
-        out_shape=tuple(jax.ShapeDtypeStruct(*s) for s in shapes),
+        out_shape=tuple(pltpu.HBM(*s) for s in shapes),
         grid_spec=pltpu.PrefetchScalarGridSpec(
             num_scalar_prefetch=1,
             grid=(1,),
@@ -285,7 +309,7 @@
     )(place, first, halo, w_inner, w_pairs, xc0, bc0, tail, decay, logs)
 
 
-def intra_kernel(place, xc, bc, lc_t, dt_t, skip, gate_rows, out, factor):
+def intra_kernel(place, xc, bc, lc_t, dt_t, skip, own_gate, got_a, got_b, got_c, out, factor):
     wide = out.shape[1]
     heads = lc_t.shape[1]
     scores = lax.dot_general(
@@ -297,9 +321,13 @@
         jnp.broadcast_to(skip[...], (8, own)),
         (iota((own, wide), 1) // 64 + heads * place[0] == iota((own, wide), 0)).astype(F32),
     )[0:1]
-    gate = silu(gate_rows[0].astype(F32))
+    far = lax.rem(place[0] - pl.program_id(0) + 4, 4)
+    gate = own_gate[...].astype(F32)
+    for distance, got in ((1, got_a), (2, got_b), (3, got_c)):
+        gate = jnp.where(far == distance, got[...].astype(F32), gate)
+    gate = silu(gate)
     cum = columns(lc_t[0])
-    factor[...] = gate * widen(jnp.exp(cum), spread(LANES, wide))
+    factor[...] = (gate * spread_columns(jnp.exp(lc_t[0]), wide)).astype(BF16)
     for pair in range(heads // 2):
         outs = []
         for h in (2 * pair, 2 * pair + 1):
@@ -311,16 +339,16 @@
             )
         cols = slice(2 * pair * 64, 2 * (pair + 1) * 64)
         mixed = jnp.concatenate(outs, axis=1) + gain[:, cols] * xc[:, cols].astype(F32)
-        out[:, cols] = mixed * gate[:, cols]
-
-
-def intra(place, xc, bc, lc_t, dt_t, skip, gate_rows):
+        out[:, cols] = (mixed * gate[:, cols]).astype(BF16)
+
+
+def intra(place, xc, bc, lc_t, dt_t, skip, gate_raw, got):
     total, wide = xc.shape
     narrow = bc.shape[1]
     heads = lc_t.shape[1]
     return pl.pallas_call(
         intra_kernel,
-        out_shape=(jax.ShapeDtypeStruct((total, wide), F32),) * 2,
+        out_shape=(pltpu.HBM((total, wide), BF16),) * 2,
         grid_spec=pltpu.PrefetchScalarGridSpec(
             num_scalar_prefetch=1,
             grid=(4,),
@@ -330,14 +358,15 @@
                 pl.BlockSpec((1, heads, BLOCK), lambda b, p: (b, 0, 0)),
                 pl.BlockSpec((1, heads, BLOCK), lambda b, p: (b, 0, 0)),
                 whole(skip.shape),
-                pl.BlockSpec((1, BLOCK, wide), lambda b, p: (b, 0, 0)),
-            ],
+                pl.BlockSpec((BLOCK, wide), lambda b, p: (0, p[0])),
+            ]
+            + [whole(a.shape) for a in got],
             out_specs=(pl.BlockSpec((BLOCK, wide), lambda b, p: (b, 0)),) * 2,
         ),
-        compiler_params=LARGE,
+        compiler_params=PARAMS,
         cost_estimate=cost(2 * total * BLOCK * wide * 4, 12 * total * wide, heads * total * BLOCK),
         name="intra",
-    )(place, xc, bc, lc_t, dt_t, skip, gate_rows)
+    )(place, xc, bc, lc_t, dt_t, skip, keep(gate_raw), *got)
 
 
 def scan_kernel(recv, out):
@@ -365,40 +394,51 @@
     )(recv)
 
 
-def finish_kernel(carry, states, decay, bc, mixed, factor, out, held):
-    b = pl.program_id(0)
-
-    @pl.when(b == 0)
-    def _():
-        held[...] = carry[...].reshape(held.shape)
-
-    start = held[...]
-    carried = jnp.dot(bc[:, LANES:], start.astype(BF16), preferred_element_type=F32)
-    out[...] = (mixed[...] + carried * factor[...]).astype(BF16).reshape(out.shape)
-    held[...] = decay[0, 0:1] * start + states[0]
+def finish_kernel(carry, states, decay, bc, mixed, factor, out, s_in, c_in, m_in, f_in, sem):
+    wide = mixed.shape[1]
+    copies = []
+    for b in range(4):
+        rows = pl.ds(b * BLOCK, BLOCK)
+        copies.append(
+            [
+                pltpu.make_async_copy(bc.at[rows, pl.ds(LANES, LANES)], c_in.at[b], sem.at[b, 0]),
+                pltpu.make_async_copy(mixed.at[rows], m_in.at[b], sem.at[b, 1]),
+                pltpu.make_async_copy(factor.at[rows], f_in.at[b], sem.at[b, 2]),
+                pltpu.make_async_copy(states.at[b], s_in.at[b], sem.at[b, 3]),
+            ]
+        )
+    for group in copies:
+        for copy in group:
+            copy.start()
+    start = carry[...].reshape(LANES, wide)
+    for b in range(4):
+        for copy in copies[b]:
+            copy.wait()
+        carried = jnp.dot(c_in[b], start.astype(BF16), preferred_element_type=F32)
+        gated = m_in[b].astype(F32) + carried * f_in[b].astype(F32)
+        count = BLOCK // out.shape[1]
+        out[b * count : (b + 1) * count] = gated.astype(BF16).reshape(count, -1, wide)
+        start = decay[b : b + 1] * start + s_in[b]
 
 
 def finish(carry, states, decay, bc, mixed, factor, rows):
     total, wide = mixed.shape
-    narrow = bc.shape[1]
     return pl.pallas_call(
         finish_kernel,
         out_shape=jax.ShapeDtypeStruct((total // rows, rows, wide), BF16),
-        grid=(4,),
-        in_specs=[
-            pl.BlockSpec(carry.shape, lambda b: (0, 0, 0)),
-            pl.BlockSpec((1, LANES, wide), lambda b: (b, 0, 0)),
-            pl.BlockSpec((1, 8, wide), lambda b: (b, 0, 0)),
-            pl.BlockSpec((BLOCK, narrow), lambda b: (b, 0)),
-            pl.BlockSpec((BLOCK, wide), lambda b: (b, 0)),
-            pl.BlockSpec((BLOCK, wide), lambda b: (b, 0)),
+        in_specs=[VMEM, ANY, VMEM, ANY, ANY, ANY],
+        out_specs=VMEM,
+        scratch_shapes=[
+            pltpu.VMEM((4, LANES, wide), F32),
+            pltpu.VMEM((4, BLOCK, LANES), BF16),
+            pltpu.VMEM((4, BLOCK, wide), BF16),
+            pltpu.VMEM((4, BLOCK, wide), BF16),
+            pltpu.SemaphoreType.DMA((4, 4)),
         ],
-        out_specs=pl.BlockSpec((BLOCK // rows, rows, wide), lambda b: (b, 0, 0)),
-        scratch_shapes=[pltpu.VMEM((LANES, wide), F32)],
-        compiler_params=LARGE,
-        cost_estimate=cost(2 * total * wide * 200, 10 * total * wide),
+        compiler_params=PARAMS,
+        cost_estimate=cost(2 * total * wide * 200, 6 * total * wide),
         name="finish",
-    )(carry, states, decay, bc, mixed, factor)
+    )(carry, keep(states), decay, keep(bc), keep(mixed), keep(factor))
 
 
 def post_kernel(slabs, gains, out):
@@ -458,8 +498,11 @@
     recv = lax.all_to_all(
         packed, ("context", "head"), split_axis=0, concat_axis=0, axis_index_groups=teams
     )
-    gate_rows = gate_raw.reshape(gate_raw.shape[0], 4, -1).transpose(1, 0, 2)
-    gate_rows, recv = lax.optimization_barrier((gate_rows, recv))
+    width = gate_raw.shape[1] // 4
+    gates = [
+        lax.dynamic_slice_in_dim(gate_raw, (x + far) % 4 * width, width, 1) for far in (1, 2, 3)
+    ]
+    *gates, recv = lax.optimization_barrier((*gates, recv))
     halo = lax.ppermute(recv[TEAM - 1, rows - 16 : rows], "context", after)
 
     pair_taps = conv_pairs.reshape(conv_pairs.shape[0], -1)
@@ -469,16 +512,19 @@
     xc, bc, states, payload = state(
         place, recv[0, :16], halo, conv_inner, pair_taps, xc0, bc0, tail, decay, logs, chunks
     )
-    gate_rows = lax.all_to_all(
-        gate_rows, "context", split_axis=0, concat_axis=0, axis_index_groups=rings
-    )
+    *gates, payload = lax.optimization_barrier((*gates, payload))
+    gates = [
+        lax.ppermute(gate, "context", [(c, c - c % 4 + (c + far) % 4) for c in range(places)])
+        for far, gate in zip((1, 2, 3), gates)
+    ]
     totals = lax.all_to_all(
         payload, "context", split_axis=0, concat_axis=0, axis_index_groups=lines
     )
+    *gates, totals = lax.optimization_barrier((*gates, totals))
     carry = lax.all_to_all(
         scan(totals), "context", split_axis=0, concat_axis=0, axis_index_groups=lines
     )
-    mixed, factor = intra(place, xc, bc, lc_t, dt_t, skip_gain.reshape(1, -1), gate_rows)
+    mixed, factor = intra(place, xc, bc, lc_t, dt_t, skip_gain.reshape(1, -1), gate_raw, gates)
     slabs = finish(carry, states, decay, bc, mixed, factor, rows)
     slabs = lax.all_to_all(
         slabs, ("context", "head"), split_axis=0, concat_axis=0, axis_index_groups=teams

time: 125 us -> 140 us (1.12)
  Pallas kernels: 25.5 us -> 53.1 us
  blocking collectives: 35.5 us -> 19.2 us
  starting transfers between devices: 18.1 us -> 30.1 us
  local copies, waits for them, and re-layouts: 10.2 us -> 2.11 us
    pallas_call x1, Pallas kernels: 2.09 us -> 33.9 us  [pack(): pl.pallas_call(pack_kernel, out_shape=jax.ShapeDtypeStruct((TEAM, rows +...]
    all_to_all x1 -> x0, blocking collectives: 18.5 us -> none  [on_device(): lax.all_to_all(payload, 'context', split_axis=0, concat_axis=0, axis_inde...]
    all_to_all x1, waiting for transfers between devices: 9.94 us -> 0.01 us  [on_device(): lax.all_to_all(payload, 'context', split_axis=0, concat_axis=0, axis_inde...]
    unnamed x33 -> x16, local copies, waits for them, and re-layouts: 7.69 us -> 0.04 us
    ppermute x0 -> x3, waiting for transfers between devices: none -> 7.63 us  [on_device(): lax.ppermute(gate, 'context', [(c, c - c % 4 + (c + far) % 4) for c in ra...]
    all_to_all x1, starting transfers between devices: 3.52 us -> 7.7 us  [on_device(): lax.all_to_all(payload, 'context', split_axis=0, concat_axis=0, axis_inde...]
    ppermute x0 -> x3, starting transfers between devices: none -> 4.07 us  [on_device(): lax.ppermute(gate, 'context', [(c, c - c % 4 + (c + far) % 4) for c in ra...]
    all_to_all x1, starting transfers between devices: 3.41 us -> 7 us  [on_device(): lax.all_to_all(scan(totals), 'context', split_axis=0, concat_axis=0, axis...]
  transfers between devices with their start and end apart: 4 -> 7, of which waited for: 3 -> 4; matrix products, arithmetic and copies ran while one was open for 2% -> 1% of each run, Pallas kernels for 13% -> 9%
where the time goes in v4:
time: 140 us; the launch traced here: 139 us
  Pallas kernels  53.1 us (38%)
  waiting for transfers between devices  34.6 us (25%)
  starting transfers between devices  30.1 us (22%)
  blocking collectives  19.2 us (14%)
  local copies, waits for them, and re-layouts  2.11 us (2%)
    pallas_call x1, Pallas kernels, pack(): pl.pallas_call(pack_kernel, out_shape=jax.ShapeDtypeStruct((TEAM, rows +...  33.9 us
    all_to_all x1, waiting for transfers between devices, on_device(): lax.all_to_all(packed, ('context', 'head'), split_axis=0, concat_axis=0,...  23.8 us
    all_to_all x1, blocking collectives, on_device(): lax.all_to_all(slabs, ('context', 'head'), split_axis=0, concat_axis=0, a...  19.2 us
    all_to_all x1, starting transfers between devices, on_device(): lax.all_to_all(payload, 'context', split_axis=0, concat_axis=0, axis_inde...  7.7 us
    ppermute x3, waiting for transfers between devices, on_device(): lax.ppermute(gate, 'context', [(c, c - c % 4 + (c + far) % 4) for c in ra...  7.63 us
    all_to_all x1, starting transfers between devices, on_device(): lax.all_to_all(packed, ('context', 'head'), split_axis=0, concat_axis=0,...  7.54 us
    pallas_call x1, Pallas kernels, intra(): pl.pallas_call(intra_kernel, out_shape=(pltpu.HBM((total, wide), BF16),)...  7.35 us
    all_to_all x1, starting transfers between devices, on_device(): lax.all_to_all(scan(totals), 'context', split_axis=0, concat_axis=0, axis...  7 us
  transfers between devices with their start and end apart: 7, of which 4 were waited for; matrix products, arithmetic and copies ran while one was open for 1% of the time, Pallas kernels for 9%

profile of v4, /device:TPU:8, one launch (start us, length us, event | category | flops | bytes accessed | tf_op | source)
XLA Modules:
  0.0 139.4 jit_solution(16099633975528348845)
XLA Ops:
  0.0 1.1 reshape.18.pairs
  1.1 0.1 pad_add_fusion.place
  1.2 33.9 %pack.1 = bf16[16,72,768]{2,1,0:T(8,128)(2,1)} custom-call(s32[2]{0:T(128)S(1)} %pad_add_fusion.place, bf16[64,8192]{1,0:T(8,128)(2,1)} %inner.1, bf16[64,2048]{1,0:T(8,128)(2,1)S(1)} %reshape.18.pairs, bf16[32,256]{1,0:T(8,128)(2,1)} %bitcast.14, f32[1,2048]{1,0:T(1,128)} %bitcast.15), custom_call_target="tpu_custom_call" | custom-call | bytes 3145728 | tf_op jit(solution)/shard_map/pack/pallas_call | solution.py:117
  35.1 0.0 copy-start.6
  35.1 7.5 %all-to-all-start = ((bf16[16,72,768]{2,1,0:T(8,128)(2,1)}), bf16[16,72,768]{2,1,0:T(8,128)(2,1)S(1)}, u32[]{:S(2)}, u32[]{:S(2)}) async-start(bf16[16,72,768]{2,1,0:T(8,128)(2,1)} %pack.1), calls=%async_computation | async-start | bytes 3538944 | tf_op jit(solution)/shard_map/all_to_all | solution.py:498
  42.7 0.0 copy-start.7
  42.7 0.0 copy-start.1
  42.7 0.0 copy-start.3
  42.7 0.0 copy-start.4
  42.8 0.0 copy-done.6
  42.8 0.9 constant_dynamic-slice_fusion
  43.7 23.8 %all-to-all-done.recv = bf16[16,72,768]{2,1,0:T(8,128)(2,1)S(1)} async-done(((bf16[16,72,768]{2,1,0:T(8,128)(2,1)}), bf16[16,72,768]{2,1,0:T(8,128)(2,1)S(1)}, u32[]{:S(2)}, u32[]{:S(2)}) %all-to-all-start) | async-done | bytes 1769504 | tf_op jit(solution)/shard_map/all_to_all | solution.py:498
  67.5 3.8 %collective-permute-start = (bf16[16,768]{1,0:T(8,128)(2,1)S(1)}, bf16[16,768]{1,0:T(8,128)(2,1)S(1)}, u32[]{:S(2)}, u32[]{:S(2)}) collective-permute-start(bf16[16,768]{1,0:T(8,128)(2,1)S(1)} %get-tuple-element.57), channel_id=1, source_target_pairs={{0,16},{4,20},{8,24},{12,28},{16,32},{20,36},{24,40},{28,44},{32,4... | collective-permute-start | bytes 73736 | tf_op jit(solution)/shard_map/ppermute | solution.py:506
  71.3 0.0 copy-done.7
  71.4 0.0 copy-done.1
  71.4 0.0 copy-done.3
  71.4 0.0 copy-done.4
  71.4 4.7 %conv.1 = (bf16[1024,512]{1,0:T(8,128)(2,1)S(1)}, bf16[1024,256]{1,0:T(8,128)(2,1)S(1)}, f32[4,8,256]{2,1,0:T(8,128)S(1)}, f32[4,8,256]{2,1,0:T(8,128)S(1)}, f32...) custom-call(s32[2]{0:T(128)S(1)} %pad_add_fusion.place, ...), custom_call_target="tpu_custom_call" | custom-call | flops 15728640 | bytes 3145728 | tf_op jit(solution)/shard_map/conv/pallas_call | solution.py:226
  76.1 0.0 collective-permute-done.halo
  76.1 2.5 %state.1 = (bf16[1024,512]{1,0:T(8,128)(2,1)}, bf16[1024,256]{1,0:T(8,128)(2,1)}, f32[4,128,512]{2,1,0:T(8,128)}, f32[8,16,640]{2,1,0:T(8,128)}) custom-call(s32[2]{0:T(128)S(1)} %pad_add_fusion.place, bf16[16,768]{1,0:T(8,128)(2,1)S(1)} %get-tuple-element.58.first, bf16[16,768]{1,0:T(8,128)(2,1)S(1)} %collective-permute-done.halo, f32[5,8192]{1,0:T(8,128)S(1)} %copy-done.1, ...), custom_call_target="tpu_custom_call" | custom-call | flops 134217728 | bytes 4194304 | tf_op jit(solution)/shard_map/state/pallas_call | solution.py:294
  78.7 0.0 copy-start
  78.7 0.0 copy-start.2
  78.7 0.0 copy-start.5
  78.7 7.7 %all-to-all-start.1 = ((f32[8,16,640]{2,1,0:T(8,128)}), f32[8,16,640]{2,1,0:T(8,128)S(1)}, u32[]{:S(2)}, u32[]{:S(2)}) async-start(f32[8,16,640]{2,1,0:T(8,128)} %get-tuple-element.44), calls=%async_computation.1 | async-start | bytes 655360 | tf_op jit(solution)/shard_map/all_to_all | solution.py:520
  86.4 0.0 collective-permute-start.1
  86.4 2.2 %collective-permute-start.2 = (bf16[256,512]{1,0:T(8,128)(2,1)}, bf16[256,512]{1,0:T(8,128)(2,1)S(1)}, u32[]{:S(2)}, u32[]{:S(2)}) collective-permute-start(bf16[256,512]{1,0:T(8,128)(2,1)} %get-tuple-element.42), channel_id=1, source_target_pairs={{0,8},{4,12},{8,0},{12,4},{16,24},{20,28},{24,16},{28,20},{32,40},... | collective-permute-start | bytes 786440 | tf_op jit(solution)/shard_map/ppermute | solution.py:517
  88.6 1.9 %collective-permute-start.3 = (bf16[256,512]{1,0:T(8,128)(2,1)S(1)}, bf16[256,512]{1,0:T(8,128)(2,1)S(1)}, u32[]{:S(2)}, u32[]{:S(2)}) collective-permute-start(bf16[256,512]{1,0:T(8,128)(2,1)S(1)} %get-tuple-element.43), channel_id=1, source_target_pairs={{0,12},{4,0},{8,4},{12,8},{16,28},{20,16},{24,20},{28,24},{32,44},... | collective-permute-start | bytes 786440 | tf_op jit(solution)/shard_map/ppermute | solution.py:517
  90.5 7.6 %collective-permute-done.1.got_a = bf16[256,512]{1,0:T(8,128)(2,1)S(1)} collective-permute-done((bf16[256,512]{1,0:T(8,128)(2,1)}, bf16[256,512]{1,0:T(8,128)(2,1)S(1)}, u32[]{:S(2)}, u32[]{:S(2)}) %collective-permute-start.1) | collective-permute-done | bytes 262176 | tf_op jit(solution)/shard_map/ppermute | solution.py:517
  98.1 0.0 collective-permute-done.2.got_b
  98.1 0.1 collective-permute-done.3.got_c
  98.1 0.0 all-to-all-done.1.recv
  98.1 0.9 scan.1
  99.0 7.0 %all-to-all-start.2 = ((f32[8,16,512]{2,1,0:T(8,128)}), f32[8,16,512]{2,1,0:T(8,128)S(1)}, u32[]{:S(2)}, u32[]{:S(2)}) async-start(f32[8,16,512]{2,1,0:T(8,128)} %scan.1), calls=%async_computation.2 | async-start | bytes 524288 | tf_op jit(solution)/shard_map/all_to_all | solution.py:524
  106.0 0.0 copy-done
  106.1 0.0 copy-done.2
  106.1 0.0 copy-done.5
  106.1 7.3 %intra.1 = (bf16[1024,512]{1,0:T(8,128)(2,1)}, bf16[1024,512]{1,0:T(8,128)(2,1)}) custom-call(s32[2]{0:T(128)S(1)} %pad_add_fusion.place, bf16[1024,512]{1,0:T(8,128)(2,1)S(1)} %copy-done.2, bf16[1024,256]{1,0:T(8,128)(2,1)S(1)} %copy-done, f32[4,8,256]{2,1,0:T(8,128)S(1)} %get-tuple-element.49.lc_t, f32[4,8,256]{2,1,0:T(8,128)S(1)} %get-tuple-element.50.dt_t, ...), custom_call_target="tpu_custom_call" | custom-call | flops 1073741824 | bytes 6291456 | tf_op jit(solution)/shard_map/intra/pallas_call | solution.py:349
  113.4 3.1 %all-to-all-done.2.carry = f32[8,16,512]{2,1,0:T(8,128)S(1)} async-done(((f32[8,16,512]{2,1,0:T(8,128)}), f32[8,16,512]{2,1,0:T(8,128)S(1)}, u32[]{:S(2)}, u32[]{:S(2)}) %all-to-all-start.2) | async-done | bytes 262176 | tf_op jit(solution)/shard_map/all_to_all | solution.py:524
  116.5 2.3 %finish.1 = bf16[16,64,512]{2,1,0:T(8,128)(2,1)S(1)} custom-call(f32[8,16,512]{2,1,0:T(8,128)S(1)} %all-to-all-done.2.carry, f32[4,128,512]{2,1,0:T(8,128)} %get-tuple-element.46.states, f32[8,512]{1,0:T(8,128)S(1)} %get-tuple-element.38.decay, bf16[1024,256]{1,0:T(8,128)(2,1)} %get-tuple-element.47.bc, bf16[1024,512]{1,0:T(8,128)(2,1)} %get-tuple-element.54.mixed, ...), custom_call_target="tpu_custom_call" | custom-call | flops 209715200 | bytes 3145728 | tf_op jit(solution)/shard_map/finish/pallas_call | solution.py:426
  118.8 19.2 %all_to_all.20.slabs = bf16[16,64,512]{2,1,0:T(8,128)(2,1)S(1)} all-to-all(bf16[16,64,512]{2,1,0:T(8,128)(2,1)S(1)} %finish.1), channel_id=1, replica_groups={{0,1,2,3,4,5,6,7,8,9,10,11,12,13,14,15},{16,17,18,19,20,21,22,23,24,25,..., dimensions={0} | all-to-all | bytes 2097152 | tf_op jit(solution)/shard_map/all_to_all | solution.py:529
  138.0 1.4 post.1
  (2 shorter events, 0.0 us)
Async XLA Ops:
  35.1 7.7 %copy-start.6 = (bf16[256,2048]{1,0:T(8,128)(2,1)S(1)}, bf16[256,2048]{1,0:T(8,128)(2,1)}, u32[]{:S(2)}) copy-start(bf16[256,2048]{1,0:T(8,128)(2,1)} %own_gate.1) | copy-start | bytes 3145732
  35.1 32.4 %all-to-all-start = ((bf16[16,72,768]{2,1,0:T(8,128)(2,1)}), bf16[16,72,768]{2,1,0:T(8,128)(2,1)S(1)}, u32[]{:S(2)}, u32[]{:S(2)}) async-start(bf16[16,72,768]{2,1,0:T(8,128)(2,1)} %pack.1), calls=%async_computation | async-start | bytes 3538944 | tf_op jit(solution)/shard_map/all_to_all | solution.py:498
  42.7 28.7 %copy-start.7 = (f32[5,8,2,128]{3,2,1,0:T(2,128)S(1)}, f32[5,8,2,128]{3,2,1,0:T(2,128)}, u32[]{:S(2)}) copy-start(f32[5,8,2,128]{3,2,1,0:T(2,128)} %param.18) | copy-start | bytes 122884
  42.7 28.7 %copy-start.1 = (f32[5,8192]{1,0:T(8,128)S(1)}, f32[5,8192]{1,0:T(8,128)}, u32[]{:S(2)}) copy-start(f32[5,8192]{1,0:T(8,128)} %w_inner.3) | copy-start | bytes 491524
  42.7 28.7 %copy-start.3 = (f32[32]{0:T(128)S(1)}, f32[32]{0:T(128)}, u32[]{:S(2)}) copy-start(f32[32]{0:T(128)} %param.14) | copy-start | bytes 388
  42.7 28.7 %copy-start.4 = (f32[32]{0:T(128)S(1)}, f32[32]{0:T(128)}, u32[]{:S(2)}) copy-start(f32[32]{0:T(128)} %param.15) | copy-start | bytes 388
  67.5 8.6 %collective-permute-start = (bf16[16,768]{1,0:T(8,128)(2,1)S(1)}, bf16[16,768]{1,0:T(8,128)(2,1)S(1)}, u32[]{:S(2)}, u32[]{:S(2)}) collective-permute-start(bf16[16,768]{1,0:T(8,128)(2,1)S(1)} %get-tuple-element.57), channel_id=1, source_target_pairs={{0,16},{4,20},{8,24},{12,28},{16,32},{20,36},{24,40},{28,44},{32,4... | collective-permute-start | bytes 73736 | tf_op jit(solution)/shard_map/ppermute | solution.py:506
  78.7 27.4 %copy-start = (bf16[1024,256]{1,0:T(8,128)(2,1)S(1)}, bf16[1024,256]{1,0:T(8,128)(2,1)}, u32[]{:S(2)}) copy-start(bf16[1024,256]{1,0:T(8,128)(2,1)} %get-tuple-element.47.bc) | copy-start | bytes 1572868
  78.7 27.4 %copy-start.2 = (bf16[1024,512]{1,0:T(8,128)(2,1)S(1)}, bf16[1024,512]{1,0:T(8,128)(2,1)}, u32[]{:S(2)}) copy-start(bf16[1024,512]{1,0:T(8,128)(2,1)} %get-tuple-element.48.xc) | copy-start | bytes 3145732
  78.7 27.4 %copy-start.5 = (f32[32]{0:T(128)S(1)}, f32[32]{0:T(128)}, u32[]{:S(2)}) copy-start(f32[32]{0:T(128)} %param.16) | copy-start | bytes 388
  78.7 19.4 %all-to-all-start.1 = ((f32[8,16,640]{2,1,0:T(8,128)}), f32[8,16,640]{2,1,0:T(8,128)S(1)}, u32[]{:S(2)}, u32[]{:S(2)}) async-start(f32[8,16,640]{2,1,0:T(8,128)} %get-tuple-element.44), calls=%async_computation.1 | async-start | bytes 655360 | tf_op jit(solution)/shard_map/all_to_all | solution.py:520
  86.4 11.7 %collective-permute-start.1 = (bf16[256,512]{1,0:T(8,128)(2,1)}, bf16[256,512]{1,0:T(8,128)(2,1)S(1)}, u32[]{:S(2)}, u32[]{:S(2)}) collective-permute-start(bf16[256,512]{1,0:T(8,128)(2,1)} %get-tuple-element.41), channel_id=1, source_target_pairs={{0,4},{4,8},{8,12},{12,0},{16,20},{20,24},{24,28},{28,16},{32,36},... | collective-permute-start | bytes 786440 | tf_op jit(solution)/shard_map/ppermute | solution.py:517
  86.4 11.6 %collective-permute-start.2 = (bf16[256,512]{1,0:T(8,128)(2,1)}, bf16[256,512]{1,0:T(8,128)(2,1)S(1)}, u32[]{:S(2)}, u32[]{:S(2)}) collective-permute-start(bf16[256,512]{1,0:T(8,128)(2,1)} %get-tuple-element.42), channel_id=1, source_target_pairs={{0,8},{4,12},{8,0},{12,4},{16,24},{20,28},{24,16},{28,20},{32,40},... | collective-permute-start | bytes 786440 | tf_op jit(solution)/shard_map/ppermute | solution.py:517
  88.6 9.5 %collective-permute-start.3 = (bf16[256,512]{1,0:T(8,128)(2,1)S(1)}, bf16[256,512]{1,0:T(8,128)(2,1)S(1)}, u32[]{:S(2)}, u32[]{:S(2)}) collective-permute-start(bf16[256,512]{1,0:T(8,128)(2,1)S(1)} %get-tuple-element.43), channel_id=1, source_target_pairs={{0,12},{4,0},{8,4},{12,8},{16,28},{20,16},{24,20},{28,24},{32,44},... | collective-permute-start | bytes 786440 | tf_op jit(solution)/shard_map/ppermute | solution.py:517
  99.0 17.5 %all-to-all-start.2 = ((f32[8,16,512]{2,1,0:T(8,128)}), f32[8,16,512]{2,1,0:T(8,128)S(1)}, u32[]{:S(2)}, u32[]{:S(2)}) async-start(f32[8,16,512]{2,1,0:T(8,128)} %scan.1), calls=%async_computation.2 | async-start | bytes 524288 | tf_op jit(solution)/shard_map/all_to_all | solution.py:524

commit v5 on v4

--- a/solution.py
+++ b/solution.py
@@ -67,28 +67,38 @@
     return v / (1.0 + jnp.exp(-v))
 
 
-def pack_kernel(place, inner, pairs, steps, gain, out, extra, sem, pairs_sem, extra_sem):
+def pack_kernel(
+    place, inner, pairs, steps, gain, out, staged, extra, stage_sem, sem, pairs_sem, extra_sem
+):
     x = place[0]
     rows, full = inner.shape
+    stages = [
+        pltpu.make_async_copy(
+            inner.at[pl.ds(8 * k, 8)], staged.at[pl.ds(8 * k, 8)], stage_sem.at[k]
+        )
+        for k in range(rows // 8)
+    ]
+    for copy in stages:
+        copy.start()
     wide, narrow = full // TEAM, pairs.shape[1] // 8
-    copies = []
+    copies, more = [], []
     for member in range(TEAM):
         px, py = member // 4, member % 4
         copies.append(
             pltpu.make_async_copy(
-                inner.at[:, pl.ds((4 * py + px) * wide, wide)],
+                staged.at[:, pl.ds((4 * py + px) * wide, wide)],
                 out.at[member, pl.ds(0, rows), pl.ds(0, wide)],
                 sem.at[member],
             )
         )
-        copies.append(
+        more.append(
             pltpu.make_async_copy(
                 pairs.at[:, pl.ds((2 * py + px // 2) * narrow, narrow)],
                 out.at[member, pl.ds(0, rows), pl.ds(wide, narrow)],
                 pairs_sem.at[member],
             )
         )
-    for copy in copies:
+    for copy in more:
         copy.start()
     mine = jnp.zeros((1, wide), F32)
     for px in range(4):
@@ -106,7 +116,11 @@
         extra[member, :, span:] = pieces
     last = pltpu.make_async_copy(extra, out.at[:, pl.ds(rows, EXTRA)], extra_sem)
     last.start()
+    for copy in stages:
+        copy.wait()
     for copy in copies:
+        copy.start()
+    for copy in copies + more:
         copy.wait()
     last.wait()
 
@@ -120,7 +134,9 @@
         in_specs=[SMEM, HBM, ANY, VMEM, VMEM],
         out_specs=ANY,
         scratch_shapes=[
+            pltpu.VMEM(inner.shape, BF16),
             pltpu.VMEM((TEAM, EXTRA, width), BF16),
+            pltpu.SemaphoreType.DMA((rows // 8,)),
             pltpu.SemaphoreType.DMA((TEAM,)),
             pltpu.SemaphoreType.DMA((TEAM,)),
             pltpu.SemaphoreType.DMA,
@@ -242,66 +258,105 @@
 
 
 def state_kernel(
-    place, first, halo, w_inner, w_pairs, xc0, bc0, tail, decay, logs, xc, bc, states, payload, ext
+    place,
+    first,
+    halo,
+    w_inner,
+    w_pairs,
+    xc0,
+    bc0,
+    tail,
+    decay,
+    logs,
+    xc,
+    bc,
+    states,
+    payload,
+    ext,
+    head_x,
+    head_b,
+    local,
+    sem,
 ):
     count = first.shape[0]
-    wide = xc.shape[1]
-    narrow = bc.shape[1]
+    total, wide = xc0.shape
+    narrow = bc0.shape[1]
+    rest = pl.ds(count, total - count)
+    copies = [
+        pltpu.make_async_copy(xc0.at[rest], xc.at[rest], sem.at[0]),
+        pltpu.make_async_copy(bc0.at[rest], bc.at[rest], sem.at[1]),
+        pltpu.make_async_copy(head_x, xc.at[pl.ds(0, count)], sem.at[2]),
+        pltpu.make_async_copy(head_b, bc.at[pl.ds(0, count)], sem.at[3]),
+    ]
+    copies[0].start()
+    copies[1].start()
     ext[0:8] = halo[count - 8 : count].astype(F32)
     ext[8 : 8 + count] = first[...].astype(F32)
-    xc[...] = xc0[...]
-    bc[...] = bc0[...]
     for start in range(0, wide, LANES):
         cols = slice(start, start + LANES)
-        xc[0:count, cols] = taps(ext, 0, count, cols, w_inner[:, cols])
+        head_x[:, cols] = taps(ext, 0, count, cols, w_inner[:, cols])
     for start in range(0, narrow, LANES):
-        bc[0:count, start : start + LANES] = taps(
+        head_b[:, start : start + LANES] = taps(
             ext,
             0,
             count,
             slice(wide + start, wide + start + LANES),
             w_pairs[:, start : start + LANES],
         )
-    total = jnp.zeros((LANES, wide), F32)
+    copies[2].start()
+    copies[3].start()
+    sum_state = jnp.zeros((LANES, wide), F32)
     for b in range(4):
         rows = slice(b * BLOCK, (b + 1) * BLOCK)
-        weighted = (xc[rows].astype(F32) * tail[b]).astype(BF16)
-        local = lax.dot_general(
-            bc[rows, 0:LANES],
-            weighted,
-            (((0,), (0,)), ((), ())),
-            preferred_element_type=F32,
+        if b == 0:
+            block = jnp.concatenate([head_x[...], xc0[count:BLOCK]], axis=0)
+            keys = jnp.concatenate([head_b[:, 0:LANES], bc0[count:BLOCK, 0:LANES]], axis=0)
+        else:
+            block, keys = xc0[rows], bc0[rows, 0:LANES]
+        weighted = (block.astype(F32) * tail[b]).astype(BF16)
+        one = lax.dot_general(
+            keys, weighted, (((0,), (0,)), ((), ())), preferred_element_type=F32
         )
-        states[b] = local
-        total = decay[b : b + 1] * total + local
+        local[b] = one
+        copies.append(pltpu.make_async_copy(local.at[b], states.at[b], sem.at[4 + b]))
+        copies[-1].start()
+        sum_state = decay[b : b + 1] * sum_state + one
     parts, depth, _ = payload.shape
-    payload[:, :, 0:wide] = total.reshape(parts, depth, wide)
+    payload[:, :, 0:wide] = sum_state.reshape(parts, depth, wide)
     for part in range(parts):
         for row in range(0, depth, 8):
             payload[part, row : row + 8, wide : wide + LANES] = logs[...]
+    for copy in copies:
+        copy.wait()
 
 
 def state(place, first, halo, w_inner, w_pairs, xc0, bc0, tail, decay, logs, parts):
     count, width = first.shape
     total, wide = xc0.shape
     narrow = width - wide
-    shapes = (
-        ((total, wide), BF16),
-        ((total, narrow), BF16),
-        ((4, LANES, wide), F32),
-        ((parts, LANES // parts, wide + LANES), F32),
-    )
+    payload_shape = (parts, LANES // parts, wide + LANES)
     return pl.pallas_call(
         state_kernel,
-        out_shape=tuple(pltpu.HBM(*s) for s in shapes),
+        out_shape=(
+            pltpu.HBM((total, wide), BF16),
+            pltpu.HBM((total, narrow), BF16),
+            pltpu.HBM((4, LANES, wide), F32),
+            jax.ShapeDtypeStruct(payload_shape, F32),
+        ),
         grid_spec=pltpu.PrefetchScalarGridSpec(
             num_scalar_prefetch=1,
             grid=(1,),
             in_specs=[whole(first.shape), whole(halo.shape)]
             + weight_specs(wide, narrow)
             + [whole(a.shape) for a in (xc0, bc0, tail, decay, logs)],
-            out_specs=tuple(whole(s[0]) for s in shapes),
-            scratch_shapes=[pltpu.VMEM((8 + count, width), F32)],
+            out_specs=(ANY, ANY, ANY, whole(payload_shape)),
+            scratch_shapes=[
+                pltpu.VMEM((8 + count, width), F32),
+                pltpu.VMEM((count, wide), BF16),
+                pltpu.VMEM((count, narrow), BF16),
+                pltpu.VMEM((4, LANES, wide), F32),
+                pltpu.SemaphoreType.DMA((8,)),
+            ],
         ),
         compiler_params=PARAMS,
         cost_estimate=cost(2 * total * wide * LANES, 8 * total * wide),
@@ -315,7 +370,8 @@
     scores = lax.dot_general(
         bc[:, LANES:], bc[:, 0:LANES], (((1,), (1,)), ((), ())), preferred_element_type=F32
     )
-    lower = iota((BLOCK, BLOCK), 0) >= iota((BLOCK, BLOCK), 1)
+    half = BLOCK // 2
+    lower = iota((half, half), 0) >= iota((half, half), 1)
     own = skip.shape[1]
     gain = widen(
         jnp.broadcast_to(skip[...], (8, own)),
@@ -326,16 +382,32 @@
     for distance, got in ((1, got_a), (2, got_b), (3, got_c)):
         gate = jnp.where(far == distance, got[...].astype(F32), gate)
     gate = silu(gate)
-    cum = columns(lc_t[0])
-    factor[...] = (gate * spread_columns(jnp.exp(lc_t[0]), wide)).astype(BF16)
+    cum = lc_t[0]
+    factor[...] = (gate * spread_columns(jnp.exp(cum), wide)).astype(BF16)
+    log2e = 1.4426950408889634
+    late = cum * log2e
+    early = late - jnp.log(dt_t[0]) * log2e
+    late = columns(late)
+    top = scores[0:half, 0:half]
+    left, right = scores[half:, 0:half], scores[half:, half:]
     for pair in range(heads // 2):
         outs = []
         for h in (2 * pair, 2 * pair + 1):
-            gap = cum[:, h : h + 1] - lc_t[0, h : h + 1]
-            decay = jnp.exp(jnp.where(lower, gap, -jnp.inf))
-            weights = (scores * (decay * dt_t[0, h : h + 1])).astype(BF16)
+            upper_col, lower_col = late[0:half, h : h + 1], late[half:, h : h + 1]
+            first, second = early[h : h + 1, 0:half], early[h : h + 1, half:]
+            values = xc[:, h * 64 : (h + 1) * 64]
+            w_top = top * jnp.exp2(jnp.where(lower, upper_col - first, -jnp.inf))
+            w_left = left * jnp.exp2(lower_col - first)
+            w_right = right * jnp.exp2(jnp.where(lower, lower_col - second, -jnp.inf))
+            w_low = jnp.concatenate([w_left, w_right], axis=1).astype(BF16)
             outs.append(
-                jnp.dot(weights, xc[:, h * 64 : (h + 1) * 64], preferred_element_type=F32)
+                jnp.concatenate(
+                    [
+                        jnp.dot(w_top.astype(BF16), values[0:half], preferred_element_type=F32),
+                        jnp.dot(w_low, values, preferred_element_type=F32),
+                    ],
+                    axis=0,
+                )
             )
         cols = slice(2 * pair * 64, 2 * (pair + 1) * 64)
         mixed = jnp.concatenate(outs, axis=1) + gain[:, cols] * xc[:, cols].astype(F32)
@@ -495,32 +567,31 @@
     packed = pack(
         place, inner_raw, pairs_raw.reshape(rows, -1), step_raw.T, norm_gain.reshape(1, -1)
     )
+    width = gate_raw.shape[1] // 4
+    gate_later, packed = lax.optimization_barrier((gate_raw, packed))
+    gates = [
+        lax.dynamic_slice_in_dim(gate_later, (x + far) % 4 * width, width, 1) for far in (1, 2, 3)
+    ]
     recv = lax.all_to_all(
         packed, ("context", "head"), split_axis=0, concat_axis=0, axis_index_groups=teams
     )
-    width = gate_raw.shape[1] // 4
-    gates = [
-        lax.dynamic_slice_in_dim(gate_raw, (x + far) % 4 * width, width, 1) for far in (1, 2, 3)
-    ]
-    *gates, recv = lax.optimization_barrier((*gates, recv))
-    halo = lax.ppermute(recv[TEAM - 1, rows - 16 : rows], "context", after)
-
-    pair_taps = conv_pairs.reshape(conv_pairs.shape[0], -1)
-    xc0, bc0, lc_t, dt_t, tail, decay, logs, gains = conv(
-        place, recv, conv_inner, pair_taps, step_bias.reshape(1, -1), rate_log.reshape(1, -1)
-    )
-    xc, bc, states, payload = state(
-        place, recv[0, :16], halo, conv_inner, pair_taps, xc0, bc0, tail, decay, logs, chunks
-    )
-    *gates, payload = lax.optimization_barrier((*gates, payload))
     gates = [
         lax.ppermute(gate, "context", [(c, c - c % 4 + (c + far) % 4) for c in range(places)])
         for far, gate in zip((1, 2, 3), gates)
     ]
+    halo = lax.ppermute(recv[TEAM - 1, rows - 16 : rows], "context", after)
+
+    pair_taps = conv_pairs.reshape(conv_pairs.shape[0], -1)
+    xc0, bc0, lc_t, dt_t, tail, decay, logs, gains = conv(
+        place, recv, conv_inner, pair_taps, step_bias.reshape(1, -1), rate_log.reshape(1, -1)
+    )
+    xc, bc, states, payload = state(
+        place, recv[0, :16], halo, conv_inner, pair_taps, xc0, bc0, tail, decay, logs, chunks
+    )
+    *gates, payload = lax.optimization_barrier((*gates, payload))
     totals = lax.all_to_all(
         payload, "context", split_axis=0, concat_axis=0, axis_index_groups=lines
     )
-    *gates, totals = lax.optimization_barrier((*gates, totals))
     carry = lax.all_to_all(
         scan(totals), "context", split_axis=0, concat_axis=0, axis_index_groups=lines
     )

time: 140 us -> 105 us (0.75)
  Pallas kernels: 53.1 us -> 21.7 us
  blocking collectives: 19.2 us -> 37.7 us
  waiting for transfers between devices: 34.6 us -> 22.1 us
  starting transfers between devices: 30.1 us -> 20.4 us
    pallas_call x1, Pallas kernels: 33.9 us -> 3.67 us  [pack(): pl.pallas_call(pack_kernel, out_shape=jax.ShapeDtypeStruct((TEAM, rows +...]
    all_to_all x0 -> x1, blocking collectives: none -> 18.7 us  [on_device(): lax.all_to_all(payload, 'context', split_axis=0, concat_axis=0, axis_inde...]
    all_to_all x1 -> x0, starting transfers between devices: 7.7 us -> none  [on_device(): lax.all_to_all(payload, 'context', split_axis=0, concat_axis=0, axis_inde...]
    ppermute x3, waiting for transfers between devices: 7.63 us -> 0.01 us  [on_device(): lax.ppermute(gate, 'context', [(c, c - c % 4 + (c + far) % 4) for c in ra...]
    all_to_all x1, waiting for transfers between devices: 23.8 us -> 18.3 us  [on_device(): lax.all_to_all(packed, ('context', 'head'), split_axis=0, concat_axis=0,...]
    all_to_all x1, starting transfers between devices: 7 us -> 3.41 us  [on_device(): lax.all_to_all(scan(totals), 'context', split_axis=0, concat_axis=0, axis...]
    ppermute x3, starting transfers between devices: 4.07 us -> 5.6 us  [on_device(): lax.ppermute(gate, 'context', [(c, c - c % 4 + (c + far) % 4) for c in ra...]
  transfers between devices with their start and end apart: 7 -> 6, of which waited for: 4 -> 2; matrix products, arithmetic and copies ran while one was open for 1% -> 1% of each run, Pallas kernels for 9% -> 13%
where the time goes in v5:
time: 105 us; the launch traced here: 104 us
  blocking collectives  37.7 us (36%)
  waiting for transfers between devices  22.1 us (21%)
  Pallas kernels  21.7 us (21%)
  starting transfers between devices  20.4 us (19%)
  local copies, waits for them, and re-layouts  2.11 us (2%)
    all_to_all x1, blocking collectives, on_device(): lax.all_to_all(slabs, ('context', 'head'), split_axis=0, concat_axis=0, a...  19 us
    all_to_all x1, blocking collectives, on_device(): lax.all_to_all(payload, 'context', split_axis=0, concat_axis=0, axis_inde...  18.7 us
    all_to_all x1, waiting for transfers between devices, on_device(): lax.all_to_all(packed, ('context', 'head'), split_axis=0, concat_axis=0,...  18.3 us
    all_to_all x1, starting transfers between devices, on_device(): lax.all_to_all(packed, ('context', 'head'), split_axis=0, concat_axis=0,...  7.54 us
    pallas_call x1, Pallas kernels, intra(): pl.pallas_call(intra_kernel, out_shape=(pltpu.HBM((total, wide), BF16),)...  6.64 us
    ppermute x3, starting transfers between devices, on_device(): lax.ppermute(gate, 'context', [(c, c - c % 4 + (c + far) % 4) for c in ra...  5.6 us
    pallas_call x1, Pallas kernels, conv(): pl.pallas_call(conv_kernel, out_shape=tuple((jax.ShapeDtypeStruct(*s) for...  4.7 us
    ppermute x1, starting transfers between devices, on_device(): halo = lax.ppermute(recv[TEAM - 1, rows - 16:rows], 'context', after)  3.81 us
  transfers between devices with their start and end apart: 6, of which 2 were waited for; matrix products, arithmetic and copies ran while one was open for 1% of the time, Pallas kernels for 13%

profile of v5, /device:TPU:8, one launch (start us, length us, event | category | flops | bytes accessed | tf_op | source)
XLA Modules:
  0.0 104.2 jit_solution(14005232474763513959)
XLA Ops:
  0.0 1.1 %reshape.18.pairs = bf16[64,2048]{1,0:T(8,128)(2,1)S(1)} reshape(bf16[64,8,2,128]{3,2,1,0:T(2,128)(2,1)} %param.11) | data formatting | bytes 524288 | tf_op jit(solution)/shard_map/reshape | solution.py:568
  1.1 0.1 pad_add_fusion.place
  1.2 3.7 %pack.1 = bf16[16,72,768]{2,1,0:T(8,128)(2,1)} custom-call(s32[2]{0:T(128)S(1)} %pad_add_fusion.place, bf16[64,8192]{1,0:T(8,128)(2,1)} %inner.1, bf16[64,2048]{1,0:T(8,128)(2,1)S(1)} %reshape.18.pairs, bf16[32,256]{1,0:T(8,128)(2,1)} %bitcast.14, f32[1,2048]{1,0:T(1,128)} %bitcast.15), custom_call_target="tpu_custom_call" | custom-call | bytes 3145728 | tf_op jit(solution)/shard_map/pack/pallas_call | solution.py:131
  4.9 0.0 copy-start.6
  4.9 7.5 %all-to-all-start = ((bf16[16,72,768]{2,1,0:T(8,128)(2,1)}), bf16[16,72,768]{2,1,0:T(8,128)(2,1)S(1)}, u32[]{:S(2)}, u32[]{:S(2)}) async-start(bf16[16,72,768]{2,1,0:T(8,128)(2,1)} %pack.1), calls=%async_computation | async-start | bytes 3538944 | tf_op jit(solution)/shard_map/all_to_all | solution.py:575
  12.4 0.0 copy-start.7
  12.5 0.0 copy-start.1
  12.5 0.0 copy-start.3
  12.5 0.0 copy-start.4
  12.5 0.0 copy-done.6
  12.6 0.9 constant_dynamic-slice_fusion
  13.5 1.5 %collective-permute-start = (bf16[256,512]{1,0:T(8,128)(2,1)}, bf16[256,512]{1,0:T(8,128)(2,1)S(1)}, u32[]{:S(2)}, u32[]{:S(2)}) collective-permute-start(bf16[256,512]{1,0:T(8,128)(2,1)} %get-tuple-element.49), channel_id=1, source_target_pairs={{0,4},{4,8},{8,12},{12,0},{16,20},{20,24},{24,28},{28,16},{32,36},... | collective-permute-start | bytes 786440 | tf_op jit(solution)/shard_map/ppermute | solution.py:579
  14.9 2.7 %collective-permute-start.1 = (bf16[256,512]{1,0:T(8,128)(2,1)}, bf16[256,512]{1,0:T(8,128)(2,1)S(1)}, u32[]{:S(2)}, u32[]{:S(2)}) collective-permute-start(bf16[256,512]{1,0:T(8,128)(2,1)} %get-tuple-element.48), channel_id=1, source_target_pairs={{0,8},{4,12},{8,0},{12,4},{16,24},{20,28},{24,16},{28,20},{32,40},... | collective-permute-start | bytes 786440 | tf_op jit(solution)/shard_map/ppermute | solution.py:579
  17.6 1.5 %collective-permute-start.2 = (bf16[256,512]{1,0:T(8,128)(2,1)S(1)}, bf16[256,512]{1,0:T(8,128)(2,1)S(1)}, u32[]{:S(2)}, u32[]{:S(2)}) collective-permute-start(bf16[256,512]{1,0:T(8,128)(2,1)S(1)} %get-tuple-element.47), channel_id=1, source_target_pairs={{0,12},{4,0},{8,4},{12,8},{16,28},{20,16},{24,20},{28,24},{32,44},... | collective-permute-start | bytes 786440 | tf_op jit(solution)/shard_map/ppermute | solution.py:579
  19.1 18.3 %all-to-all-done.recv = bf16[16,72,768]{2,1,0:T(8,128)(2,1)S(1)} async-done(((bf16[16,72,768]{2,1,0:T(8,128)(2,1)}), bf16[16,72,768]{2,1,0:T(8,128)(2,1)S(1)}, u32[]{:S(2)}, u32[]{:S(2)}) %all-to-all-start) | async-done | bytes 1769504 | tf_op jit(solution)/shard_map/all_to_all | solution.py:575
  37.4 3.8 %collective-permute-start.3 = (bf16[16,768]{1,0:T(8,128)(2,1)S(1)}, bf16[16,768]{1,0:T(8,128)(2,1)S(1)}, u32[]{:S(2)}, u32[]{:S(2)}) collective-permute-start(bf16[16,768]{1,0:T(8,128)(2,1)S(1)} %get-tuple-element.45), channel_id=1, source_target_pairs={{0,16},{4,20},{8,24},{12,28},{16,32},{20,36},{24,40},{28,44},{32,4... | collective-permute-start | bytes 73736 | tf_op jit(solution)/shard_map/ppermute | solution.py:582
  41.2 0.0 copy-done.7
  41.3 0.0 copy-done.1
  41.3 0.0 copy-done.3
  41.3 0.0 copy-done.4
  41.3 4.7 %conv.1 = (bf16[1024,512]{1,0:T(8,128)(2,1)S(1)}, bf16[1024,256]{1,0:T(8,128)(2,1)S(1)}, f32[4,8,256]{2,1,0:T(8,128)S(1)}, f32[4,8,256]{2,1,0:T(8,128)S(1)}, f32...) custom-call(s32[2]{0:T(128)S(1)} %pad_add_fusion.place, ...), custom_call_target="tpu_custom_call" | custom-call | flops 15728640 | bytes 3145728 | tf_op jit(solution)/shard_map/conv/pallas_call | solution.py:242
  46.0 0.0 collective-permute-done.3.halo
  46.0 2.1 %state.1 = (bf16[1024,512]{1,0:T(8,128)(2,1)}, bf16[1024,256]{1,0:T(8,128)(2,1)}, f32[4,128,512]{2,1,0:T(8,128)}, f32[8,16,640]{2,1,0:T(8,128)S(1)}) custom-call(s32[2]{0:T(128)S(1)} %pad_add_fusion.place, bf16[16,768]{1,0:T(8,128)(2,1)S(1)} %get-tuple-element.46.first, bf16[16,768]{1,0:T(8,128)(2,1)S(1)} %collective-permute-done.3.halo, ...), custom_call_target="tpu_custom_call" | custom-call | flops 134217728 | bytes 4194304 | tf_op jit(solution)/shard_map/state/pallas_call | solution.py:338
  48.1 0.0 copy-start
  48.1 0.0 copy-start.2
  48.1 0.0 copy-start.5
  48.1 0.0 collective-permute-done.got_a
  48.2 0.0 collective-permute-done.1.got_b
  48.2 0.0 collective-permute-done.2.got_c
  48.2 18.7 %all_to_all.20.recv = f32[8,16,640]{2,1,0:T(8,128)S(1)} all-to-all(f32[8,16,640]{2,1,0:T(8,128)S(1)} %get-tuple-element.33), channel_id=1, replica_groups={{0,16,32,48,64,80,96,112},{4,20,36,52,68,84,100,116},{8,24,40,56,72,88,..., dimensions={0} | all-to-all | bytes 655360 | tf_op jit(solution)/shard_map/all_to_all | solution.py:592
  66.9 0.9 scan.1
  67.8 3.4 %all-to-all-start.2 = ((f32[8,16,512]{2,1,0:T(8,128)}), f32[8,16,512]{2,1,0:T(8,128)S(1)}, u32[]{:S(2)}, u32[]{:S(2)}) async-start(f32[8,16,512]{2,1,0:T(8,128)} %scan.1), calls=%async_computation.2 | async-start | bytes 524288 | tf_op jit(solution)/shard_map/all_to_all | solution.py:595
  71.2 0.0 copy-done
  71.2 0.0 copy-done.2
  71.2 0.0 copy-done.5
  71.2 6.6 %intra.1 = (bf16[1024,512]{1,0:T(8,128)(2,1)}, bf16[1024,512]{1,0:T(8,128)(2,1)}) custom-call(s32[2]{0:T(128)S(1)} %pad_add_fusion.place, bf16[1024,512]{1,0:T(8,128)(2,1)S(1)} %copy-done.2, bf16[1024,256]{1,0:T(8,128)(2,1)S(1)} %copy-done, f32[4,8,256]{2,1,0:T(8,128)S(1)} %get-tuple-element.37.lc_t, f32[4,8,256]{2,1,0:T(8,128)S(1)} %get-tuple-element.38.dt_t, ...), custom_call_target="tpu_custom_call" | custom-call | flops 1073741824 | bytes 6291456 | tf_op jit(solution)/shard_map/intra/pallas_call | solution.py:421
  77.9 3.7 %all-to-all-done.2.carry = f32[8,16,512]{2,1,0:T(8,128)S(1)} async-done(((f32[8,16,512]{2,1,0:T(8,128)}), f32[8,16,512]{2,1,0:T(8,128)S(1)}, u32[]{:S(2)}, u32[]{:S(2)}) %all-to-all-start.2) | async-done | bytes 262176 | tf_op jit(solution)/shard_map/all_to_all | solution.py:595
  81.6 2.3 %finish.1 = bf16[16,64,512]{2,1,0:T(8,128)(2,1)S(1)} custom-call(f32[8,16,512]{2,1,0:T(8,128)S(1)} %all-to-all-done.2.carry, f32[4,128,512]{2,1,0:T(8,128)} %get-tuple-element.34.states, f32[8,512]{1,0:T(8,128)S(1)} %get-tuple-element.30.decay, bf16[1024,256]{1,0:T(8,128)(2,1)} %get-tuple-element.35.bc, bf16[1024,512]{1,0:T(8,128)(2,1)} %get-tuple-element.42.mixed, ...), custom_call_target="tpu_custom_call" | custom-call | flops 209715200 | bytes 3145728 | tf_op jit(solution)/shard_map/finish/pallas_call | solution.py:498
  83.9 19.0 %all_to_all.21.slabs = bf16[16,64,512]{2,1,0:T(8,128)(2,1)S(1)} all-to-all(bf16[16,64,512]{2,1,0:T(8,128)(2,1)S(1)} %finish.1), channel_id=1, replica_groups={{0,1,2,3,4,5,6,7,8,9,10,11,12,13,14,15},{16,17,18,19,20,21,22,23,24,25,..., dimensions={0} | all-to-all | bytes 2097152 | tf_op jit(solution)/shard_map/all_to_all | solution.py:600
  102.9 1.4 %post.1 = bf16[64,8192]{1,0:T(8,128)(2,1)} custom-call(bf16[16,64,512]{2,1,0:T(8,128)(2,1)S(1)} %all_to_all.21.slabs, f32[16,512]{1,0:T(8,128)S(1)} %get-tuple-element.44.gains), custom_call_target="tpu_custom_call" | custom-call | flops 3145728 | bytes 2097152 | tf_op jit(solution)/shard_map/post/pallas_call | solution.py:533
  (2 shorter events, 0.0 us)
Async XLA Ops:
  4.9 7.7 %copy-start.6 = (bf16[256,2048]{1,0:T(8,128)(2,1)S(1)}, bf16[256,2048]{1,0:T(8,128)(2,1)}, u32[]{:S(2)}) copy-start(bf16[256,2048]{1,0:T(8,128)(2,1)} %own_gate.1) | copy-start | bytes 3145732
  4.9 32.5 %all-to-all-start = ((bf16[16,72,768]{2,1,0:T(8,128)(2,1)}), bf16[16,72,768]{2,1,0:T(8,128)(2,1)S(1)}, u32[]{:S(2)}, u32[]{:S(2)}) async-start(bf16[16,72,768]{2,1,0:T(8,128)(2,1)} %pack.1), calls=%async_computation | async-start | bytes 3538944 | tf_op jit(solution)/shard_map/all_to_all | solution.py:575
  12.4 28.8 %copy-start.7 = (f32[5,8,2,128]{3,2,1,0:T(2,128)S(1)}, f32[5,8,2,128]{3,2,1,0:T(2,128)}, u32[]{:S(2)}) copy-start(f32[5,8,2,128]{3,2,1,0:T(2,128)} %param.18) | copy-start | bytes 122884
  12.5 28.8 %copy-start.1 = (f32[5,8192]{1,0:T(8,128)S(1)}, f32[5,8192]{1,0:T(8,128)}, u32[]{:S(2)}) copy-start(f32[5,8192]{1,0:T(8,128)} %w_inner.3) | copy-start | bytes 491524
  12.5 28.8 %copy-start.3 = (f32[32]{0:T(128)S(1)}, f32[32]{0:T(128)}, u32[]{:S(2)}) copy-start(f32[32]{0:T(128)} %param.14) | copy-start | bytes 388
  12.5 28.8 %copy-start.4 = (f32[32]{0:T(128)S(1)}, f32[32]{0:T(128)}, u32[]{:S(2)}) copy-start(f32[32]{0:T(128)} %param.15) | copy-start | bytes 388
  13.5 34.7 %collective-permute-start = (bf16[256,512]{1,0:T(8,128)(2,1)}, bf16[256,512]{1,0:T(8,128)(2,1)S(1)}, u32[]{:S(2)}, u32[]{:S(2)}) collective-permute-start(bf16[256,512]{1,0:T(8,128)(2,1)} %get-tuple-element.49), channel_id=1, source_target_pairs={{0,4},{4,8},{8,12},{12,0},{16,20},{20,24},{24,28},{28,16},{32,36},... | collective-permute-start | bytes 786440 | tf_op jit(solution)/shard_map/ppermute | solution.py:579
  14.9 33.2 %collective-permute-start.1 = (bf16[256,512]{1,0:T(8,128)(2,1)}, bf16[256,512]{1,0:T(8,128)(2,1)S(1)}, u32[]{:S(2)}, u32[]{:S(2)}) collective-permute-start(bf16[256,512]{1,0:T(8,128)(2,1)} %get-tuple-element.48), channel_id=1, source_target_pairs={{0,8},{4,12},{8,0},{12,4},{16,24},{20,28},{24,16},{28,20},{32,40},... | collective-permute-start | bytes 786440 | tf_op jit(solution)/shard_map/ppermute | solution.py:579
  17.6 30.6 %collective-permute-start.2 = (bf16[256,512]{1,0:T(8,128)(2,1)S(1)}, bf16[256,512]{1,0:T(8,128)(2,1)S(1)}, u32[]{:S(2)}, u32[]{:S(2)}) collective-permute-start(bf16[256,512]{1,0:T(8,128)(2,1)S(1)} %get-tuple-element.47), channel_id=1, source_target_pairs={{0,12},{4,0},{8,4},{12,8},{16,28},{20,16},{24,20},{28,24},{32,44},... | collective-permute-start | bytes 786440 | tf_op jit(solution)/shard_map/ppermute | solution.py:579
  37.4 8.6 %collective-permute-start.3 = (bf16[16,768]{1,0:T(8,128)(2,1)S(1)}, bf16[16,768]{1,0:T(8,128)(2,1)S(1)}, u32[]{:S(2)}, u32[]{:S(2)}) collective-permute-start(bf16[16,768]{1,0:T(8,128)(2,1)S(1)} %get-tuple-element.45), channel_id=1, source_target_pairs={{0,16},{4,20},{8,24},{12,28},{16,32},{20,36},{24,40},{28,44},{32,4... | collective-permute-start | bytes 73736 | tf_op jit(solution)/shard_map/ppermute | solution.py:582
  48.1 23.1 %copy-start = (bf16[1024,256]{1,0:T(8,128)(2,1)S(1)}, bf16[1024,256]{1,0:T(8,128)(2,1)}, u32[]{:S(2)}) copy-start(bf16[1024,256]{1,0:T(8,128)(2,1)} %get-tuple-element.35.bc) | copy-start | bytes 1572868
  48.1 23.1 %copy-start.2 = (bf16[1024,512]{1,0:T(8,128)(2,1)S(1)}, bf16[1024,512]{1,0:T(8,128)(2,1)}, u32[]{:S(2)}) copy-start(bf16[1024,512]{1,0:T(8,128)(2,1)} %get-tuple-element.36.xc) | copy-start | bytes 3145732
  48.1 23.1 %copy-start.5 = (f32[32]{0:T(128)S(1)}, f32[32]{0:T(128)}, u32[]{:S(2)}) copy-start(f32[32]{0:T(128)} %param.16) | copy-start | bytes 388
  67.8 13.8 %all-to-all-start.2 = ((f32[8,16,512]{2,1,0:T(8,128)}), f32[8,16,512]{2,1,0:T(8,128)S(1)}, u32[]{:S(2)}, u32[]{:S(2)}) async-start(f32[8,16,512]{2,1,0:T(8,128)} %scan.1), calls=%async_computation.2 | async-start | bytes 524288 | tf_op jit(solution)/shard_map/all_to_all | solution.py:595

commit v6 on v5

--- a/solution.py
+++ b/solution.py
@@ -19,7 +19,6 @@
 PARAMS = pltpu.CompilerParams(vmem_limit_bytes=24 * 1024 * 1024)
 LARGE = pltpu.CompilerParams(vmem_limit_bytes=56 * 1024 * 1024)
 TEAM = 16
-EXTRA = 8
 
 
 def cost(flops, bytes_accessed, transcendentals=0):
@@ -68,27 +67,20 @@
 
 
 def pack_kernel(
-    place, inner, pairs, steps, gain, out, staged, extra, stage_sem, sem, pairs_sem, extra_sem
+    inner, pairs, out, staged, stage_sem, sem, pairs_sem
 ):
-    x = place[0]
     rows, full = inner.shape
-    stages = [
-        pltpu.make_async_copy(
-            inner.at[pl.ds(8 * k, 8)], staged.at[pl.ds(8 * k, 8)], stage_sem.at[k]
-        )
-        for k in range(rows // 8)
-    ]
-    for copy in stages:
-        copy.start()
     wide, narrow = full // TEAM, pairs.shape[1] // 8
-    copies, more = [], []
+    stages, copies, more = [], [], []
     for member in range(TEAM):
         px, py = member // 4, member % 4
+        part = pl.ds((4 * py + px) * wide, wide)
+        stages.append(
+            pltpu.make_async_copy(inner.at[:, part], staged.at[:, part], stage_sem.at[member])
+        )
         copies.append(
             pltpu.make_async_copy(
-                staged.at[:, pl.ds((4 * py + px) * wide, wide)],
-                out.at[member, pl.ds(0, rows), pl.ds(0, wide)],
-                sem.at[member],
+                staged.at[:, part], out.at[member, pl.ds(0, rows), pl.ds(0, wide)], sem.at[member]
             )
         )
         more.append(
@@ -98,53 +90,35 @@
                 pairs_sem.at[member],
             )
         )
+    for copy in stages:
+        copy.start()
     for copy in more:
         copy.start()
-    mine = jnp.zeros((1, wide), F32)
-    for px in range(4):
-        mine = jnp.where(x == px, gain[:, px * wide : (px + 1) * wide], mine)
-    top = mine.astype(BF16).astype(F32)
-    mid = (mine - top).astype(BF16).astype(F32)
-    low = (mine - top - mid).astype(BF16).astype(F32)
-    row = iota((EXTRA, wide), 0)
-    pieces = jnp.where(row == 0, top, jnp.where(row == 1, mid, jnp.where(row == 2, low, 0.0)))
-    pieces = pieces.astype(BF16)
-    span = steps.shape[1]
-    for member in range(TEAM):
-        px = member // 4
-        extra[member, :, 0:span] = steps[8 * px : 8 * px + 8]
-        extra[member, :, span:] = pieces
-    last = pltpu.make_async_copy(extra, out.at[:, pl.ds(rows, EXTRA)], extra_sem)
-    last.start()
-    for copy in stages:
-        copy.wait()
-    for copy in copies:
+    for stage, copy in zip(stages, copies):
+        stage.wait()
         copy.start()
     for copy in copies + more:
         copy.wait()
-    last.wait()
-
-
-def pack(place, inner, pairs, steps, gain):
+
+
+def pack(inner, pairs):
     rows = inner.shape[0]
     width = inner.shape[1] // TEAM + pairs.shape[1] // 8
     return pl.pallas_call(
         pack_kernel,
-        out_shape=jax.ShapeDtypeStruct((TEAM, rows + EXTRA, width), BF16),
-        in_specs=[SMEM, HBM, ANY, VMEM, VMEM],
+        out_shape=jax.ShapeDtypeStruct((TEAM, rows, width), BF16),
+        in_specs=[ANY, ANY],
         out_specs=ANY,
         scratch_shapes=[
             pltpu.VMEM(inner.shape, BF16),
-            pltpu.VMEM((TEAM, EXTRA, width), BF16),
-            pltpu.SemaphoreType.DMA((rows // 8,)),
             pltpu.SemaphoreType.DMA((TEAM,)),
             pltpu.SemaphoreType.DMA((TEAM,)),
-            pltpu.SemaphoreType.DMA,
+            pltpu.SemaphoreType.DMA((TEAM,)),
         ],
         compiler_params=PARAMS,
         cost_estimate=cost(0, 4 * TEAM * rows * width),
         name="pack",
-    )(place, keep(inner), pairs, keep(steps), keep(gain))
+    )(keep(inner), pairs)
 
 
 def taps(ext, row, rows, cols, weight):
@@ -156,15 +130,31 @@
 
 
 def conv_kernel(
-    place, recv, w_inner, w_pairs, bias, rate, xc, bc, lc_t, dt_t, tail, decay, logs, gains, ext
+    place,
+    recv,
+    w_inner,
+    w_pairs,
+    bias,
+    rate,
+    own_steps,
+    got_a,
+    got_b,
+    got_c,
+    xc,
+    bc,
+    lc_t,
+    dt_t,
+    tail,
+    decay,
+    logs,
+    ext,
 ):
-    x, y = place[0], place[1]
-    members, tall, width = recv.shape
-    rows = tall - EXTRA
+    x = place[0]
+    members, rows, width = recv.shape
     wide = xc.shape[1]
     ext[0:8] = jnp.zeros((8, width), F32)
     for m in range(members):
-        ext[8 + m * rows : 8 + (m + 1) * rows] = recv[m, 0:rows].astype(F32)
+        ext[8 + m * rows : 8 + (m + 1) * rows] = recv[m].astype(F32)
 
     def chunk(m, _):
         row = pl.multiple_of(m * rows, rows)
@@ -190,7 +180,11 @@
     upper = (iota((BLOCK, BLOCK), 0) <= iota((BLOCK, BLOCK), 1)).astype(BF16)
     steps = []
     for b in range(4):
-        v = recv[4 * b + y, rows:tall, 0:BLOCK].astype(F32) + shift
+        far = lax.rem(x - b + 4, 4)
+        v = own_steps[...].astype(F32)
+        for distance, got in ((1, got_a), (2, got_b), (3, got_c)):
+            v = jnp.where(far == distance, got[...].astype(F32), v)
+        v = v + shift
         steps.append(jnp.maximum(v, 0.0) + jnp.log1p(jnp.exp(-jnp.abs(v))))
     parts = split(jnp.concatenate([step * speed for step in steps], axis=0))
     parts = jnp.concatenate(parts, axis=0).astype(BF16)
@@ -208,9 +202,6 @@
     logs[...] = jnp.broadcast_to(
         by_block[0:1] + by_block[1:2] + by_block[2:3] + by_block[3:4], (8, LANES)
     )
-    for m in range(members):
-        pieces = recv[m, rows:tall, BLOCK:].astype(F32)
-        gains[m : m + 1] = pieces[0:1] + pieces[1:2] + pieces[2:3]
 
 
 def whole(shape):
@@ -224,11 +215,11 @@
     ]
 
 
-def conv(place, recv, w_inner, w_pairs, bias, rate):
-    members, tall, width = recv.shape
+def conv(place, recv, w_inner, w_pairs, bias, rate, steps):
+    members, rows, width = recv.shape
     wide = w_inner.shape[1] // TEAM
     narrow = width - wide
-    total = members * (tall - EXTRA)
+    total = members * rows
     shapes = (
         ((total, wide), BF16),
         ((total, narrow), BF16),
@@ -237,7 +228,6 @@
         ((4, BLOCK, wide), F32),
         ((8, wide), F32),
         ((8, LANES), F32),
-        ((members, wide), F32),
     )
     return pl.pallas_call(
         conv_kernel,
@@ -247,14 +237,14 @@
             grid=(1,),
             in_specs=[whole(recv.shape)]
             + weight_specs(wide, narrow)
-            + [whole(bias.shape), whole(rate.shape)],
+            + [whole(a.shape) for a in (bias, rate, *steps)],
             out_specs=tuple(whole(s[0]) for s in shapes),
             scratch_shapes=[pltpu.VMEM((8 + total, width), F32)],
         ),
         compiler_params=PARAMS,
         cost_estimate=cost(20 * total * width, 4 * total * width, 2 * total * width),
         name="conv",
-    )(place, recv, w_inner, w_pairs, bias, rate)
+    )(place, recv, w_inner, w_pairs, bias, rate, *steps)
 
 
 def state_kernel(
@@ -513,9 +503,13 @@
     )(carry, keep(states), decay, keep(bc), keep(mixed), keep(factor))
 
 
-def post_kernel(slabs, gains, out):
+def post_kernel(place, slabs, own_gain, got_a, got_b, got_c, out):
     wide = slabs.shape[2]
     for y in range(4):
+        far = lax.rem(place[1] - y + 4, 4)
+        gain = own_gain[...]
+        for distance, got in ((1, got_a), (2, got_b), (3, got_c)):
+            gain = jnp.where(far == distance, got[...], gain)
         for half in range(2):
             left, right = 8 * half + y, 8 * half + 4 + y
             a, b = slabs[left].astype(F32), slabs[right].astype(F32)
@@ -523,22 +517,24 @@
                 jnp.sum(a * a, axis=1, keepdims=True) + jnp.sum(b * b, axis=1, keepdims=True)
             ) / (2 * wide)
             inv = lax.rsqrt(mean + 1e-5)
-            at = (4 * y + 2 * half) * wide
-            out[:, at : at + wide] = (a * inv * gains[left : left + 1]).astype(BF16)
-            out[:, at + wide : at + 2 * wide] = (b * inv * gains[right : right + 1]).astype(BF16)
-
-
-def post(slabs, gains):
+            at = 2 * half * wide
+            low, high = gain[:, at : at + wide], gain[:, at + wide : at + 2 * wide]
+            at = at + 4 * y * wide
+            out[:, at : at + wide] = (a * inv * low).astype(BF16)
+            out[:, at + wide : at + 2 * wide] = (b * inv * high).astype(BF16)
+
+
+def post(place, slabs, gains):
     members, rows, wide = slabs.shape
     return pl.pallas_call(
         post_kernel,
         out_shape=jax.ShapeDtypeStruct((rows, members * wide), BF16),
-        in_specs=[VMEM, VMEM],
+        in_specs=[SMEM] + [VMEM] * 5,
         out_specs=VMEM,
         compiler_params=PARAMS,
         cost_estimate=cost(6 * members * rows * wide, 4 * members * rows * wide),
         name="post",
-    )(slabs, gains)
+    )(place, slabs, *gains)
 
 
 def on_device(
@@ -562,28 +558,44 @@
     after = [(c, c + 4) for c in range(places - 4)]
     teams = [list(range(TEAM * k, TEAM * (k + 1))) for k in range(places * shards // TEAM)]
     lines = [[4 * k + s for k in range(chunks)] for s in range(4)]
-    rings = [[4 * k + s for s in range(4)] for k in range(chunks)]
-
-    packed = pack(
-        place, inner_raw, pairs_raw.reshape(rows, -1), step_raw.T, norm_gain.reshape(1, -1)
-    )
-    width = gate_raw.shape[1] // 4
-    gate_later, packed = lax.optimization_barrier((gate_raw, packed))
-    gates = [
-        lax.dynamic_slice_in_dim(gate_later, (x + far) % 4 * width, width, 1) for far in (1, 2, 3)
-    ]
+
+    def around(axis, position, pick):
+        count = lax.axis_size(axis)
+        routes = [[(c, c - c % 4 + (c + far) % 4) for c in range(count)] for far in (1, 2, 3)]
+        return [
+            lax.ppermute(pick((position + far) % 4), axis, route)
+            for far, route in zip((1, 2, 3), routes)
+        ]
+
+    packed = pack(inner_raw, pairs_raw.reshape(rows, -1))
+    step_rows = step_raw.T
+    gain_row = norm_gain.reshape(1, -1)
+    gate_later, steps_later, gain_later, packed = lax.optimization_barrier(
+        (gate_raw, step_rows, gain_row, packed)
+    )
     recv = lax.all_to_all(
         packed, ("context", "head"), split_axis=0, concat_axis=0, axis_index_groups=teams
     )
-    gates = [
-        lax.ppermute(gate, "context", [(c, c - c % 4 + (c + far) % 4) for c in range(places)])
-        for far, gate in zip((1, 2, 3), gates)
-    ]
+    width = gate_raw.shape[1] // 4
+    y = lax.axis_index("head").astype(jnp.int32)
+    steps = around("context", x, lambda p: lax.dynamic_slice_in_dim(steps_later, 8 * p, 8, 0))
+    gains = around("head", y, lambda p: gain_later)
+    gates = around(
+        "context", x, lambda p: lax.dynamic_slice_in_dim(gate_later, p * width, width, 1)
+    )
+    *steps, recv = lax.optimization_barrier((*steps, recv))
     halo = lax.ppermute(recv[TEAM - 1, rows - 16 : rows], "context", after)
 
     pair_taps = conv_pairs.reshape(conv_pairs.shape[0], -1)
-    xc0, bc0, lc_t, dt_t, tail, decay, logs, gains = conv(
-        place, recv, conv_inner, pair_taps, step_bias.reshape(1, -1), rate_log.reshape(1, -1)
+    own_steps = lax.dynamic_slice_in_dim(step_rows, 8 * x, 8, 0)
+    xc0, bc0, lc_t, dt_t, tail, decay, logs = conv(
+        place,
+        recv,
+        conv_inner,
+        pair_taps,
+        step_bias.reshape(1, -1),
+        rate_log.reshape(1, -1),
+        [own_steps] + steps,
     )
     xc, bc, states, payload = state(
         place, recv[0, :16], halo, conv_inner, pair_taps, xc0, bc0, tail, decay, logs, chunks
@@ -592,6 +604,7 @@
     totals = lax.all_to_all(
         payload, "context", split_axis=0, concat_axis=0, axis_index_groups=lines
     )
+    *gains, totals = lax.optimization_barrier((*gains, totals))
     carry = lax.all_to_all(
         scan(totals), "context", split_axis=0, concat_axis=0, axis_index_groups=lines
     )
@@ -600,7 +613,7 @@
     slabs = lax.all_to_all(
         slabs, ("context", "head"), split_axis=0, concat_axis=0, axis_index_groups=teams
     )
-    return post(slabs, gains)
+    return post(place, slabs, [gain_row] + gains)
 
 
 def solution(mesh):

time: 105 us -> 101 us (0.962)
  blocking collectives: 37.7 us -> 16.5 us
  starting transfers between devices: 20.4 us -> 35 us
  waiting for transfers between devices: 22.1 us -> 24.1 us
    all_to_all x1 -> x0, blocking collectives: 18.7 us -> none  [on_device(): lax.all_to_all(payload, 'context', split_axis=0, concat_axis=0, axis_inde...]
    all_to_all x1, waiting for transfers between devices: 18.3 us -> 0.5 us  [on_device(): lax.all_to_all(packed, ('context', 'head'), split_axis=0, concat_axis=0,...]
    ppermute x3 -> x9, waiting for transfers between devices: 0.01 us -> 16.1 us  [around(): lax.ppermute(pick((position + far) % 4), axis, route)]
    all_to_all x0 -> x1, starting transfers between devices: none -> 7.71 us  [on_device(): lax.all_to_all(payload, 'context', split_axis=0, concat_axis=0, axis_inde...]
    ppermute x3 -> x9, starting transfers between devices: 5.6 us -> 12.6 us  [around(): lax.ppermute(pick((position + far) % 4), axis, route)]
    all_to_all x0 -> x1, waiting for transfers between devices: none -> 3.92 us  [on_device(): lax.all_to_all(payload, 'context', split_axis=0, concat_axis=0, axis_inde...]
    all_to_all x1, blocking collectives: 19 us -> 16.5 us  [on_device(): lax.all_to_all(slabs, ('context', 'head'), split_axis=0, concat_axis=0, a...]
    pallas_call x1, Pallas kernels: 3.67 us -> 2.57 us  [pack(): pl.pallas_call(pack_kernel, out_shape=jax.ShapeDtypeStruct((TEAM, rows, w...]
  transfers between devices with their start and end apart: 6 -> 13, of which waited for: 2 -> 6; matrix products, arithmetic and copies ran while one was open for 1% -> 1% of each run, Pallas kernels for 13% -> 14%
where the time goes in v6:
time: 101 us; the launch traced here: 100 us
  starting transfers between devices  35 us (35%)
  waiting for transfers between devices  24.1 us (24%)
  Pallas kernels  22.2 us (22%)
  blocking collectives  16.5 us (16%)
  local copies, waits for them, and re-layouts  2.05 us (2%)
    all_to_all x1, blocking collectives, on_device(): lax.all_to_all(slabs, ('context', 'head'), split_axis=0, concat_axis=0, a...  16.5 us
    ppermute x9, waiting for transfers between devices, around(): lax.ppermute(pick((position + far) % 4), axis, route)  16.1 us
    ppermute x9, starting transfers between devices, around(): lax.ppermute(pick((position + far) % 4), axis, route)  12.6 us
    all_to_all x1, starting transfers between devices, on_device(): lax.all_to_all(payload, 'context', split_axis=0, concat_axis=0, axis_inde...  7.71 us
    all_to_all x1, starting transfers between devices, on_device(): lax.all_to_all(packed, ('context', 'head'), split_axis=0, concat_axis=0,...  7.54 us
    pallas_call x1, Pallas kernels, intra(): pl.pallas_call(intra_kernel, out_shape=(pltpu.HBM((total, wide), BF16),)...  6.8 us
    pallas_call x1, Pallas kernels, conv(): pl.pallas_call(conv_kernel, out_shape=tuple((jax.ShapeDtypeStruct(*s) for...  4.65 us
    all_to_all x1, waiting for transfers between devices, on_device(): lax.all_to_all(payload, 'context', split_axis=0, concat_axis=0, axis_inde...  3.92 us
  transfers between devices with their start and end apart: 13, of which 6 were waited for; matrix products, arithmetic and copies ran while one was open for 1% of the time, Pallas kernels for 14%

profile of v6, /device:TPU:8, one launch (start us, length us, event | category | flops | bytes accessed | tf_op | source)
XLA Modules:
  0.0 100.2 jit_solution(5677089006908874664)
XLA Ops:
  0.0 1.1 %reshape.19.pairs = bf16[64,2048]{1,0:T(8,128)(2,1)S(1)} reshape(bf16[64,8,2,128]{3,2,1,0:T(2,128)(2,1)} %param.11) | data formatting | bytes 524288 | tf_op jit(solution)/shard_map/reshape | solution.py:570
  1.1 2.6 %pack.1 = bf16[16,64,768]{2,1,0:T(8,128)(2,1)} custom-call(bf16[64,8192]{1,0:T(8,128)(2,1)} %inner.1, bf16[64,2048]{1,0:T(8,128)(2,1)S(1)} %reshape.19.pairs), custom_call_target="tpu_custom_call" | custom-call | bytes 3145728 | tf_op jit(solution)/shard_map/pack/pallas_call | solution.py:107
  3.7 0.0 copy-start.13
  3.7 0.0 copy-start.11
  3.7 7.5 %all-to-all-start = ((bf16[16,64,768]{2,1,0:T(8,128)(2,1)}), bf16[16,64,768]{2,1,0:T(8,128)(2,1)S(1)}, u32[]{:S(2)}, u32[]{:S(2)}) async-start(bf16[16,64,768]{2,1,0:T(8,128)(2,1)} %pack.1), calls=%async_computation | async-start | bytes 3145728 | tf_op jit(solution)/shard_map/all_to_all | solution.py:576
  11.3 0.0 copy-start.1
  11.3 0.0 copy-start.4
  11.3 0.0 copy-start.5
  11.4 0.0 copy-done.13
  11.4 1.5 %collective-permute-start.6 = (bf16[8,256]{1,0:T(8,128)(2,1)S(1)}, bf16[8,256]{1,0:T(8,128)(2,1)S(1)}, u32[]{:S(2)}, u32[]{:S(2)}) collective-permute-start(bf16[8,256]{1,0:T(8,128)(2,1)S(1)} %get-tuple-element.70), channel_id=1, source_target_pairs={{0,4},{4,8},{8,12},{12,0},{16,20},{20,24},{24,28},{28,16},{32,36},... | collective-permute-start | bytes 12296 | tf_op jit(solution)/shard_map/ppermute | solution.py:566
  13.0 2.7 %collective-permute-start.7 = (bf16[8,256]{1,0:T(8,128)(2,1)S(1)}, bf16[8,256]{1,0:T(8,128)(2,1)S(1)}, u32[]{:S(2)}, u32[]{:S(2)}) collective-permute-start(bf16[8,256]{1,0:T(8,128)(2,1)S(1)} %get-tuple-element.69), channel_id=1, source_target_pairs={{0,8},{4,12},{8,0},{12,4},{16,24},{20,28},{24,16},{28,20},{32,40},... | collective-permute-start | bytes 12296 | tf_op jit(solution)/shard_map/ppermute | solution.py:566
  15.6 1.5 %collective-permute-start.8 = (bf16[8,256]{1,0:T(8,128)(2,1)S(1)}, bf16[8,256]{1,0:T(8,128)(2,1)S(1)}, u32[]{:S(2)}, u32[]{:S(2)}) collective-permute-start(bf16[8,256]{1,0:T(8,128)(2,1)S(1)} %get-tuple-element.68), channel_id=1, source_target_pairs={{0,12},{4,0},{8,4},{12,8},{16,28},{20,16},{24,20},{28,24},{32,44},... | collective-permute-start | bytes 12296 | tf_op jit(solution)/shard_map/ppermute | solution.py:566
  17.1 0.0 copy-done.11
  17.1 0.8 constant_dynamic-slice_fusion.3
  17.9 0.6 collective-permute-start.3
  18.5 0.9 collective-permute-start.4
  19.4 13.1 %collective-permute-done.6.got_a = bf16[8,256]{1,0:T(8,128)(2,1)S(1)} collective-permute-done((bf16[8,256]{1,0:T(8,128)(2,1)S(1)}, bf16[8,256]{1,0:T(8,128)(2,1)S(1)}, u32[]{:S(2)}, u32[]{:S(2)}) %collective-permute-start.6) | collective-permute-done | bytes 4128 | tf_op jit(solution)/shard_map/ppermute | solution.py:566
  32.5 1.2 %collective-permute-start.5 = (bf16[256,512]{1,0:T(8,128)(2,1)S(1)}, bf16[256,512]{1,0:T(8,128)(2,1)}, u32[]{:S(2)}, u32[]{:S(2)}) collective-permute-start(bf16[256,512]{1,0:T(8,128)(2,1)S(1)} %get-tuple-element.65), channel_id=1, source_target_pairs={{0,12},{4,0},{8,4},{12,8},{16,28},{20,16},{24,20},{28,24},{32,44},... | collective-permute-start | bytes 786440 | tf_op jit(solution)/shard_map/ppermute | solution.py:566
  33.6 0.0 collective-permute-done.7.got_b
  33.6 0.0 collective-permute-done.8.got_c
  33.6 0.5 all-to-all-done.recv
  34.1 3.8 %collective-permute-start.9 = (bf16[16,768]{1,0:T(8,128)(2,1)S(1)}, bf16[16,768]{1,0:T(8,128)(2,1)S(1)}, u32[]{:S(2)}, u32[]{:S(2)}) collective-permute-start(bf16[16,768]{1,0:T(8,128)(2,1)S(1)} %get-tuple-element.63), channel_id=1, source_target_pairs={{0,16},{4,20},{8,24},{12,28},{16,32},{20,36},{24,40},{28,44},{32,4... | collective-permute-start | bytes 73736 | tf_op jit(solution)/shard_map/ppermute | solution.py:587
  38.0 0.1 pad_add_fusion.place
  38.0 0.0 copy-done.12
  38.1 0.0 copy-done.1
  38.1 0.0 copy-done.4
  38.1 0.0 copy-done.5
  38.1 4.7 %conv.1 = (bf16[1024,512]{1,0:T(8,128)(2,1)S(1)}, bf16[1024,256]{1,0:T(8,128)(2,1)S(1)}, f32[4,8,256]{2,1,0:T(8,128)S(1)}, f32[4,8,256]{2,1,0:T(8,128)S(1)}, f32...) custom-call(s32[2]{0:T(128)S(1)} %pad_add_fusion.place, ...), custom_call_target="tpu_custom_call" | custom-call | flops 15728640 | bytes 3145728 | tf_op jit(solution)/shard_map/conv/pallas_call | solution.py:232
  42.8 0.0 copy-start.7
  42.8 0.0 copy-start.9
  42.8 0.0 collective-permute-done.9.halo
  42.8 0.0 copy-start.2
  42.8 3.0 %state.1 = (bf16[1024,512]{1,0:T(8,128)(2,1)}, bf16[1024,256]{1,0:T(8,128)(2,1)}, f32[4,128,512]{2,1,0:T(8,128)}, f32[8,16,640]{2,1,0:T(8,128)}) custom-call(s32[2]{0:T(128)S(1)} %pad_add_fusion.place, bf16[16,768]{1,0:T(8,128)(2,1)S(1)} %get-tuple-element.64.first, bf16[16,768]{1,0:T(8,128)(2,1)S(1)} %collective-permute-done.9.halo, ...), custom_call_target="tpu_custom_call" | custom-call | flops 134217728 | bytes 4194304 | tf_op jit(solution)/shard_map/state/pallas_call | solution.py:328
  45.9 0.0 copy-done.7
  45.9 0.0 copy-done.9
  45.9 0.0 copy-start
  45.9 0.0 copy-start.3
  45.9 0.0 copy-start.6
  45.9 0.0 collective-permute-done.3.got_a
  45.9 0.0 copy-start.8
  45.9 0.0 copy-start.10
  45.9 0.0 collective-permute-done.4.got_b
  45.9 0.0 collective-permute-done.5.got_c
  46.0 7.7 %all-to-all-start.1 = ((f32[8,16,640]{2,1,0:T(8,128)}), f32[8,16,640]{2,1,0:T(8,128)S(1)}, u32[]{:S(2)}, u32[]{:S(2)}) async-start(f32[8,16,640]{2,1,0:T(8,128)} %get-tuple-element.48), calls=%async_computation.1 | async-start | bytes 655360 | tf_op jit(solution)/shard_map/all_to_all | solution.py:604
  53.7 0.0 copy-done.2
  53.7 1.0 %collective-permute-start = (f32[1,2048]{1,0:T(1,128)S(1)}, f32[1,2048]{1,0:T(1,128)S(1)}, u32[]{:S(2)}, u32[]{:S(2)}) collective-permute-start(f32[1,2048]{1,0:T(1,128)S(1)} %bitcast.13), channel_id=1, source_target_pairs={{0,1},{1,2},{2,3},{3,0},{4,5},{5,6},{6,7},{7,4},{8,9},{9,10},{10,1... | collective-permute-start | bytes 24584 | tf_op jit(solution)/shard_map/ppermute | solution.py:566
  54.7 2.6 %collective-permute-start.1 = (f32[1,2048]{1,0:T(1,128)S(1)}, f32[1,2048]{1,0:T(1,128)S(1)}, u32[]{:S(2)}, u32[]{:S(2)}) collective-permute-start(f32[1,2048]{1,0:T(1,128)S(1)} %bitcast.14), channel_id=1, source_target_pairs={{0,2},{1,3},{2,0},{3,1},{4,6},{5,7},{6,4},{7,5},{8,10},{9,11},{10,... | collective-permute-start | bytes 24584 | tf_op jit(solution)/shard_map/ppermute | solution.py:566
  57.3 0.7 collective-permute-start.2
  57.9 0.0 collective-permute-done.got_a
  57.9 1.9 %collective-permute-done.1.got_b = f32[1,2048]{1,0:T(1,128)S(1)} collective-permute-done((f32[1,2048]{1,0:T(1,128)S(1)}, f32[1,2048]{1,0:T(1,128)S(1)}, u32[]{:S(2)}, u32[]{:S(2)}) %collective-permute-start.1) | collective-permute-done | bytes 8224 | tf_op jit(solution)/shard_map/ppermute | solution.py:566
  59.9 1.1 %collective-permute-done.2.got_c = f32[1,2048]{1,0:T(1,128)S(1)} collective-permute-done((f32[1,2048]{1,0:T(1,128)S(1)}, f32[1,2048]{1,0:T(1,128)S(1)}, u32[]{:S(2)}, u32[]{:S(2)}) %collective-permute-start.2) | collective-permute-done | bytes 8224 | tf_op jit(solution)/shard_map/ppermute | solution.py:566
  60.9 3.9 %all-to-all-done.1.recv = f32[8,16,640]{2,1,0:T(8,128)S(1)} async-done(((f32[8,16,640]{2,1,0:T(8,128)}), f32[8,16,640]{2,1,0:T(8,128)S(1)}, u32[]{:S(2)}, u32[]{:S(2)}) %all-to-all-start.1) | async-done | bytes 327712 | tf_op jit(solution)/shard_map/all_to_all | solution.py:604
  64.9 0.9 scan.1
  65.8 3.4 %all-to-all-start.2 = ((f32[8,16,512]{2,1,0:T(8,128)}), f32[8,16,512]{2,1,0:T(8,128)S(1)}, u32[]{:S(2)}, u32[]{:S(2)}) async-start(f32[8,16,512]{2,1,0:T(8,128)} %scan.1), calls=%async_computation.2 | async-start | bytes 524288 | tf_op jit(solution)/shard_map/all_to_all | solution.py:608
  69.2 0.0 copy-done
  69.2 0.0 copy-done.3
  69.2 0.0 copy-done.6
  69.2 0.0 copy-done.8
  69.2 0.0 copy-done.10
  69.2 6.8 %intra.1 = (bf16[1024,512]{1,0:T(8,128)(2,1)}, bf16[1024,512]{1,0:T(8,128)(2,1)}) custom-call(s32[2]{0:T(128)S(1)} %pad_add_fusion.place, bf16[1024,512]{1,0:T(8,128)(2,1)S(1)} %copy-done.3, bf16[1024,256]{1,0:T(8,128)(2,1)S(1)} %copy-done, f32[4,8,256]{2,1,0:T(8,128)S(1)} %copy-done.8, f32[4,8,256]{2,1,0:T(8,128)S(1)} %copy-done.10, f32[1,32]{1,0:T(1,128)S(1)} %bitcast.19, ...), custom_call_target="tpu_custom_call" | custom-call | flops 1073741824 | bytes 6291456 | tf_op jit(solution)/shard_map/intra/pallas_call | solution.py:411
  76.0 3.5 %all-to-all-done.2.carry = f32[8,16,512]{2,1,0:T(8,128)S(1)} async-done(((f32[8,16,512]{2,1,0:T(8,128)}), f32[8,16,512]{2,1,0:T(8,128)S(1)}, u32[]{:S(2)}, u32[]{:S(2)}) %all-to-all-start.2) | async-done | bytes 262176 | tf_op jit(solution)/shard_map/all_to_all | solution.py:608
  79.6 2.3 %finish.1 = bf16[16,64,512]{2,1,0:T(8,128)(2,1)S(1)} custom-call(f32[8,16,512]{2,1,0:T(8,128)S(1)} %all-to-all-done.2.carry, f32[4,128,512]{2,1,0:T(8,128)} %get-tuple-element.50.states, f32[8,512]{1,0:T(8,128)S(1)} %get-tuple-element.45.decay, bf16[1024,256]{1,0:T(8,128)(2,1)} %get-tuple-element.51.bc, bf16[1024,512]{1,0:T(8,128)(2,1)} %get-tuple-element.58.mixed, ...), custom_call_target="tpu_custom_call" | custom-call | flops 209715200 | bytes 3145728 | tf_op jit(solution)/shard_map/finish/pallas_call | solution.py:488
  81.9 16.5 %all_to_all.20.slabs = bf16[16,64,512]{2,1,0:T(8,128)(2,1)S(1)} all-to-all(bf16[16,64,512]{2,1,0:T(8,128)(2,1)S(1)} %finish.1), channel_id=1, replica_groups={{0,1,2,3,4,5,6,7,8,9,10,11,12,13,14,15},{16,17,18,19,20,21,22,23,24,25,..., dimensions={0} | all-to-all | bytes 2097152 | tf_op jit(solution)/shard_map/all_to_all | solution.py:613
  98.3 1.9 %post.1 = bf16[64,8192]{1,0:T(8,128)(2,1)} custom-call(s32[2]{0:T(128)S(1)} %pad_add_fusion.place, bf16[16,64,512]{2,1,0:T(8,128)(2,1)S(1)} %all_to_all.20.slabs, f32[1,2048]{1,0:T(1,128)S(1)} %bitcast.16, f32[1,2048]{1,0:T(1,128)S(1)} %collective-permute-done.got_a, f32[1,2048]{1,0:T(1,128)S(1)} %collective-permute-done.1.got_b, ...), custom_call_target="tpu_custom_call" | custom-call | flops 3145728 | bytes 2097152 | tf_op jit(solution)/shard_map/post/pallas_call | solution.py:529
  (5 shorter events, 0.1 us)
Async XLA Ops:
  3.7 7.7 %copy-start.13 = (bf16[256,32]{0,1:T(8,128)(2,1)S(1)}, bf16[256,32]{0,1:T(8,128)(2,1)}, u32[]{:S(2)}) copy-start(bf16[256,32]{0,1:T(8,128)(2,1)} %param.13) | copy-start | bytes 49156
  3.7 13.4 %copy-start.11 = (bf16[256,2048]{1,0:T(8,128)(2,1)S(1)}, bf16[256,2048]{1,0:T(8,128)(2,1)}, u32[]{:S(2)}) copy-start(bf16[256,2048]{1,0:T(8,128)(2,1)} %own_gate.1) | copy-start | bytes 3145732
  3.7 30.4 %all-to-all-start = ((bf16[16,64,768]{2,1,0:T(8,128)(2,1)}), bf16[16,64,768]{2,1,0:T(8,128)(2,1)S(1)}, u32[]{:S(2)}, u32[]{:S(2)}) async-start(bf16[16,64,768]{2,1,0:T(8,128)(2,1)} %pack.1), calls=%async_computation | async-start | bytes 3145728 | tf_op jit(solution)/shard_map/all_to_all | solution.py:576
  11.3 26.8 %copy-start.12 = (f32[5,8,2,128]{3,2,1,0:T(2,128)S(1)}, f32[5,8,2,128]{3,2,1,0:T(2,128)}, u32[]{:S(2)}) copy-start(f32[5,8,2,128]{3,2,1,0:T(2,128)} %param.18) | copy-start | bytes 122884
  11.3 26.8 %copy-start.1 = (f32[5,8192]{1,0:T(8,128)S(1)}, f32[5,8192]{1,0:T(8,128)}, u32[]{:S(2)}) copy-start(f32[5,8192]{1,0:T(8,128)} %w_inner.3) | copy-start | bytes 491524
  11.3 26.8 %copy-start.4 = (f32[32]{0:T(128)S(1)}, f32[32]{0:T(128)}, u32[]{:S(2)}) copy-start(f32[32]{0:T(128)} %param.14) | copy-start | bytes 388
  11.3 26.8 %copy-start.5 = (f32[32]{0:T(128)S(1)}, f32[32]{0:T(128)}, u32[]{:S(2)}) copy-start(f32[32]{0:T(128)} %param.15) | copy-start | bytes 388
  11.4 21.1 %collective-permute-start.6 = (bf16[8,256]{1,0:T(8,128)(2,1)S(1)}, bf16[8,256]{1,0:T(8,128)(2,1)S(1)}, u32[]{:S(2)}, u32[]{:S(2)}) collective-permute-start(bf16[8,256]{1,0:T(8,128)(2,1)S(1)} %get-tuple-element.70), channel_id=1, source_target_pairs={{0,4},{4,8},{8,12},{12,0},{16,20},{20,24},{24,28},{28,16},{32,36},... | collective-permute-start | bytes 12296 | tf_op jit(solution)/shard_map/ppermute | solution.py:566
  13.0 20.7 %collective-permute-start.7 = (bf16[8,256]{1,0:T(8,128)(2,1)S(1)}, bf16[8,256]{1,0:T(8,128)(2,1)S(1)}, u32[]{:S(2)}, u32[]{:S(2)}) collective-permute-start(bf16[8,256]{1,0:T(8,128)(2,1)S(1)} %get-tuple-element.69), channel_id=1, source_target_pairs={{0,8},{4,12},{8,0},{12,4},{16,24},{20,28},{24,16},{28,20},{32,40},... | collective-permute-start | bytes 12296 | tf_op jit(solution)/shard_map/ppermute | solution.py:566
  15.6 18.0 %collective-permute-start.8 = (bf16[8,256]{1,0:T(8,128)(2,1)S(1)}, bf16[8,256]{1,0:T(8,128)(2,1)S(1)}, u32[]{:S(2)}, u32[]{:S(2)}) collective-permute-start(bf16[8,256]{1,0:T(8,128)(2,1)S(1)} %get-tuple-element.68), channel_id=1, source_target_pairs={{0,12},{4,0},{8,4},{12,8},{16,28},{20,16},{24,20},{28,24},{32,44},... | collective-permute-start | bytes 12296 | tf_op jit(solution)/shard_map/ppermute | solution.py:566
  17.9 28.0 %collective-permute-start.3 = (bf16[256,512]{1,0:T(8,128)(2,1)}, bf16[256,512]{1,0:T(8,128)(2,1)S(1)}, u32[]{:S(2)}, u32[]{:S(2)}) collective-permute-start(bf16[256,512]{1,0:T(8,128)(2,1)} %get-tuple-element.67), channel_id=1, source_target_pairs={{0,4},{4,8},{8,12},{12,0},{16,20},{20,24},{24,28},{28,16},{32,36},... | collective-permute-start | bytes 786440 | tf_op jit(solution)/shard_map/ppermute | solution.py:566
  18.5 27.5 %collective-permute-start.4 = (bf16[256,512]{1,0:T(8,128)(2,1)S(1)}, bf16[256,512]{1,0:T(8,128)(2,1)S(1)}, u32[]{:S(2)}, u32[]{:S(2)}) collective-permute-start(bf16[256,512]{1,0:T(8,128)(2,1)S(1)} %get-tuple-element.66), channel_id=1, source_target_pairs={{0,8},{4,12},{8,0},{12,4},{16,24},{20,28},{24,16},{28,20},{32,40},... | collective-permute-start | bytes 786440 | tf_op jit(solution)/shard_map/ppermute | solution.py:566
  32.5 13.5 %collective-permute-start.5 = (bf16[256,512]{1,0:T(8,128)(2,1)S(1)}, bf16[256,512]{1,0:T(8,128)(2,1)}, u32[]{:S(2)}, u32[]{:S(2)}) collective-permute-start(bf16[256,512]{1,0:T(8,128)(2,1)S(1)} %get-tuple-element.65), channel_id=1, source_target_pairs={{0,12},{4,0},{8,4},{12,8},{16,28},{20,16},{24,20},{28,24},{32,44},... | collective-permute-start | bytes 786440 | tf_op jit(solution)/shard_map/ppermute | solution.py:566
  34.1 8.6 %collective-permute-start.9 = (bf16[16,768]{1,0:T(8,128)(2,1)S(1)}, bf16[16,768]{1,0:T(8,128)(2,1)S(1)}, u32[]{:S(2)}, u32[]{:S(2)}) collective-permute-start(bf16[16,768]{1,0:T(8,128)(2,1)S(1)} %get-tuple-element.63), channel_id=1, source_target_pairs={{0,16},{4,20},{8,24},{12,28},{16,32},{20,36},{24,40},{28,44},{32,4... | collective-permute-start | bytes 73736 | tf_op jit(solution)/shard_map/ppermute | solution.py:587
  42.8 3.1 %copy-start.7 = (f32[4,8,256]{2,1,0:T(8,128)}, f32[4,8,256]{2,1,0:T(8,128)S(1)}, u32[]{:S(2)}) copy-start(f32[4,8,256]{2,1,0:T(8,128)S(1)} %get-tuple-element.53.lc_t) | copy-start | bytes 98308
  42.8 3.1 %copy-start.9 = (f32[4,8,256]{2,1,0:T(8,128)}, f32[4,8,256]{2,1,0:T(8,128)S(1)}, u32[]{:S(2)}) copy-start(f32[4,8,256]{2,1,0:T(8,128)S(1)} %get-tuple-element.54.dt_t) | copy-start | bytes 98308
  42.8 10.9 %copy-start.2 = (f32[2048]{0:T(1024)S(1)}, f32[2048]{0:T(1024)}, u32[]{:S(2)}) copy-start(f32[2048]{0:T(1024)} %param.19) | copy-start | bytes 24580
  45.9 23.3 %copy-start = (bf16[1024,256]{1,0:T(8,128)(2,1)S(1)}, bf16[1024,256]{1,0:T(8,128)(2,1)}, u32[]{:S(2)}) copy-start(bf16[1024,256]{1,0:T(8,128)(2,1)} %get-tuple-element.51.bc) | copy-start | bytes 1572868
  45.9 23.3 %copy-start.3 = (bf16[1024,512]{1,0:T(8,128)(2,1)S(1)}, bf16[1024,512]{1,0:T(8,128)(2,1)}, u32[]{:S(2)}) copy-start(bf16[1024,512]{1,0:T(8,128)(2,1)} %get-tuple-element.52.xc) | copy-start | bytes 3145732
  45.9 23.3 %copy-start.6 = (f32[32]{0:T(128)S(1)}, f32[32]{0:T(128)}, u32[]{:S(2)}) copy-start(f32[32]{0:T(128)} %param.16) | copy-start | bytes 388
  45.9 23.3 %copy-start.8 = (f32[4,8,256]{2,1,0:T(8,128)S(1)}, f32[4,8,256]{2,1,0:T(8,128)}, u32[]{:S(2)}) copy-start(f32[4,8,256]{2,1,0:T(8,128)} %copy-done.7) | copy-start | bytes 98308
  45.9 23.3 %copy-start.10 = (f32[4,8,256]{2,1,0:T(8,128)S(1)}, f32[4,8,256]{2,1,0:T(8,128)}, u32[]{:S(2)}) copy-start(f32[4,8,256]{2,1,0:T(8,128)} %copy-done.9) | copy-start | bytes 98308
  46.0 18.9 %all-to-all-start.1 = ((f32[8,16,640]{2,1,0:T(8,128)}), f32[8,16,640]{2,1,0:T(8,128)S(1)}, u32[]{:S(2)}, u32[]{:S(2)}) async-start(f32[8,16,640]{2,1,0:T(8,128)} %get-tuple-element.48), calls=%async_computation.1 | async-start | bytes 655360 | tf_op jit(solution)/shard_map/all_to_all | solution.py:604
  53.7 4.3 %collective-permute-start = (f32[1,2048]{1,0:T(1,128)S(1)}, f32[1,2048]{1,0:T(1,128)S(1)}, u32[]{:S(2)}, u32[]{:S(2)}) collective-permute-start(f32[1,2048]{1,0:T(1,128)S(1)} %bitcast.13), channel_id=1, source_target_pairs={{0,1},{1,2},{2,3},{3,0},{4,5},{5,6},{6,7},{7,4},{8,9},{9,10},{10,1... | collective-permute-start | bytes 24584 | tf_op jit(solution)/shard_map/ppermute | solution.py:566
  54.7 5.2 %collective-permute-start.1 = (f32[1,2048]{1,0:T(1,128)S(1)}, f32[1,2048]{1,0:T(1,128)S(1)}, u32[]{:S(2)}, u32[]{:S(2)}) collective-permute-start(f32[1,2048]{1,0:T(1,128)S(1)} %bitcast.14), channel_id=1, source_target_pairs={{0,2},{1,3},{2,0},{3,1},{4,6},{5,7},{6,4},{7,5},{8,10},{9,11},{10,... | collective-permute-start | bytes 24584 | tf_op jit(solution)/shard_map/ppermute | solution.py:566
  57.3 3.7 %collective-permute-start.2 = (f32[1,2048]{1,0:T(1,128)S(1)}, f32[1,2048]{1,0:T(1,128)S(1)}, u32[]{:S(2)}, u32[]{:S(2)}) collective-permute-start(f32[1,2048]{1,0:T(1,128)S(1)} %bitcast.15), channel_id=1, source_target_pairs={{0,3},{1,0},{2,1},{3,2},{4,7},{5,4},{6,5},{7,6},{8,11},{9,8},{10,9... | collective-permute-start | bytes 24584 | tf_op jit(solution)/shard_map/ppermute | solution.py:566
  65.8 13.8 %all-to-all-start.2 = ((f32[8,16,512]{2,1,0:T(8,128)}), f32[8,16,512]{2,1,0:T(8,128)S(1)}, u32[]{:S(2)}, u32[]{:S(2)}) async-start(f32[8,16,512]{2,1,0:T(8,128)} %scan.1), calls=%async_computation.2 | async-start | bytes 524288 | tf_op jit(solution)/shard_map/all_to_all | solution.py:608

commit v7 on v6

--- a/solution.py
+++ b/solution.py
@@ -14,7 +14,6 @@
 LANES = 128
 ANY = pl.BlockSpec(memory_space=pl.ANY)
 VMEM = pl.BlockSpec(memory_space=pltpu.VMEM)
-SMEM = pl.BlockSpec(memory_space=pltpu.SMEM)
 HBM = pl.BlockSpec(memory_space=pltpu.HBM)
 PARAMS = pltpu.CompilerParams(vmem_limit_bytes=24 * 1024 * 1024)
 LARGE = pltpu.CompilerParams(vmem_limit_bytes=56 * 1024 * 1024)
@@ -63,7 +62,8 @@
 
 
 def silu(v):
-    return v / (1.0 + jnp.exp(-v))
+    half = 0.5 * v
+    return half + half * jnp.tanh(half)
 
 
 def pack_kernel(
@@ -130,7 +130,6 @@
 
 
 def conv_kernel(
-    place,
     recv,
     w_inner,
     w_pairs,
@@ -149,7 +148,7 @@
     logs,
     ext,
 ):
-    x = place[0]
+    x = lax.rem(lax.axis_index("context"), 4)
     members, rows, width = recv.shape
     wide = xc.shape[1]
     ext[0:8] = jnp.zeros((8, width), F32)
@@ -204,21 +203,9 @@
     )
 
 
-def whole(shape):
-    return pl.BlockSpec(shape, lambda i, p: (0,) * len(shape))
-
-
-def weight_specs(wide, narrow):
-    return [
-        pl.BlockSpec((5, wide), lambda i, p: (0, 4 * p[1] + p[0])),
-        pl.BlockSpec((5, narrow), lambda i, p: (0, 2 * p[1] + lax.div(p[0], 2))),
-    ]
-
-
-def conv(place, recv, w_inner, w_pairs, bias, rate, steps):
+def conv(recv, w_inner, w_pairs, bias, rate, steps):
     members, rows, width = recv.shape
-    wide = w_inner.shape[1] // TEAM
-    narrow = width - wide
+    wide, narrow = w_inner.shape[1], w_pairs.shape[1]
     total = members * rows
     shapes = (
         ((total, wide), BF16),
@@ -232,23 +219,16 @@
     return pl.pallas_call(
         conv_kernel,
         out_shape=tuple(jax.ShapeDtypeStruct(*s) for s in shapes),
-        grid_spec=pltpu.PrefetchScalarGridSpec(
-            num_scalar_prefetch=1,
-            grid=(1,),
-            in_specs=[whole(recv.shape)]
-            + weight_specs(wide, narrow)
-            + [whole(a.shape) for a in (bias, rate, *steps)],
-            out_specs=tuple(whole(s[0]) for s in shapes),
-            scratch_shapes=[pltpu.VMEM((8 + total, width), F32)],
-        ),
+        in_specs=[VMEM] * 9,
+        out_specs=(VMEM,) * len(shapes),
+        scratch_shapes=[pltpu.VMEM((8 + total, width), F32)],
         compiler_params=PARAMS,
         cost_estimate=cost(20 * total * width, 4 * total * width, 2 * total * width),
         name="conv",
-    )(place, recv, w_inner, w_pairs, bias, rate, *steps)
+    )(recv, w_inner, w_pairs, bias, rate, *steps)
 
 
 def state_kernel(
-    place,
     first,
     halo,
     w_inner,
@@ -320,7 +300,7 @@
         copy.wait()
 
 
-def state(place, first, halo, w_inner, w_pairs, xc0, bc0, tail, decay, logs, parts):
+def state(first, halo, w_inner, w_pairs, xc0, bc0, tail, decay, logs, parts):
     count, width = first.shape
     total, wide = xc0.shape
     narrow = width - wide
@@ -333,28 +313,23 @@
             pltpu.HBM((4, LANES, wide), F32),
             jax.ShapeDtypeStruct(payload_shape, F32),
         ),
-        grid_spec=pltpu.PrefetchScalarGridSpec(
-            num_scalar_prefetch=1,
-            grid=(1,),
-            in_specs=[whole(first.shape), whole(halo.shape)]
-            + weight_specs(wide, narrow)
-            + [whole(a.shape) for a in (xc0, bc0, tail, decay, logs)],
-            out_specs=(ANY, ANY, ANY, whole(payload_shape)),
-            scratch_shapes=[
-                pltpu.VMEM((8 + count, width), F32),
-                pltpu.VMEM((count, wide), BF16),
-                pltpu.VMEM((count, narrow), BF16),
-                pltpu.VMEM((4, LANES, wide), F32),
-                pltpu.SemaphoreType.DMA((8,)),
-            ],
-        ),
+        in_specs=[VMEM] * 9,
+        out_specs=(ANY, ANY, ANY, VMEM),
+        scratch_shapes=[
+            pltpu.VMEM((8 + count, width), F32),
+            pltpu.VMEM((count, wide), BF16),
+            pltpu.VMEM((count, narrow), BF16),
+            pltpu.VMEM((4, LANES, wide), F32),
+            pltpu.SemaphoreType.DMA((8,)),
+        ],
         compiler_params=PARAMS,
         cost_estimate=cost(2 * total * wide * LANES, 8 * total * wide),
         name="state",
-    )(place, first, halo, w_inner, w_pairs, xc0, bc0, tail, decay, logs)
-
-
-def intra_kernel(place, xc, bc, lc_t, dt_t, skip, own_gate, got_a, got_b, got_c, out, factor):
+    )(first, halo, w_inner, w_pairs, xc0, bc0, tail, decay, logs)
+
+
+def intra_kernel(xc, bc, lc_t, dt_t, skip, own_gate, got_a, got_b, got_c, out, factor):
+    x = lax.rem(lax.axis_index("context"), 4)
     wide = out.shape[1]
     heads = lc_t.shape[1]
     scores = lax.dot_general(
@@ -365,9 +340,9 @@
     own = skip.shape[1]
     gain = widen(
         jnp.broadcast_to(skip[...], (8, own)),
-        (iota((own, wide), 1) // 64 + heads * place[0] == iota((own, wide), 0)).astype(F32),
+        (iota((own, wide), 1) // 64 + heads * x == iota((own, wide), 0)).astype(F32),
     )[0:1]
-    far = lax.rem(place[0] - pl.program_id(0) + 4, 4)
+    far = lax.rem(x - pl.program_id(0) + 4, 4)
     gate = own_gate[...].astype(F32)
     for distance, got in ((1, got_a), (2, got_b), (3, got_c)):
         gate = jnp.where(far == distance, got[...].astype(F32), gate)
@@ -404,31 +379,27 @@
         out[:, cols] = (mixed * gate[:, cols]).astype(BF16)
 
 
-def intra(place, xc, bc, lc_t, dt_t, skip, gate_raw, got):
+def intra(xc, bc, lc_t, dt_t, skip, gates):
     total, wide = xc.shape
     narrow = bc.shape[1]
     heads = lc_t.shape[1]
     return pl.pallas_call(
         intra_kernel,
         out_shape=(pltpu.HBM((total, wide), BF16),) * 2,
-        grid_spec=pltpu.PrefetchScalarGridSpec(
-            num_scalar_prefetch=1,
-            grid=(4,),
-            in_specs=[
-                pl.BlockSpec((BLOCK, wide), lambda b, p: (b, 0)),
-                pl.BlockSpec((BLOCK, narrow), lambda b, p: (b, 0)),
-                pl.BlockSpec((1, heads, BLOCK), lambda b, p: (b, 0, 0)),
-                pl.BlockSpec((1, heads, BLOCK), lambda b, p: (b, 0, 0)),
-                whole(skip.shape),
-                pl.BlockSpec((BLOCK, wide), lambda b, p: (0, p[0])),
-            ]
-            + [whole(a.shape) for a in got],
-            out_specs=(pl.BlockSpec((BLOCK, wide), lambda b, p: (b, 0)),) * 2,
-        ),
+        grid=(4,),
+        in_specs=[
+            pl.BlockSpec((BLOCK, wide), lambda b: (b, 0)),
+            pl.BlockSpec((BLOCK, narrow), lambda b: (b, 0)),
+            pl.BlockSpec((1, heads, BLOCK), lambda b: (b, 0, 0)),
+            pl.BlockSpec((1, heads, BLOCK), lambda b: (b, 0, 0)),
+            pl.BlockSpec(skip.shape, lambda b: (0, 0)),
+        ]
+        + [pl.BlockSpec(gate.shape, lambda b: (0, 0)) for gate in gates],
+        out_specs=(pl.BlockSpec((BLOCK, wide), lambda b: (b, 0)),) * 2,
         compiler_params=PARAMS,
         cost_estimate=cost(2 * total * BLOCK * wide * 4, 12 * total * wide, heads * total * BLOCK),
         name="intra",
-    )(place, xc, bc, lc_t, dt_t, skip, keep(gate_raw), *got)
+    )(xc, bc, lc_t, dt_t, skip, *gates)
 
 
 def scan_kernel(recv, out):
@@ -503,10 +474,10 @@
     )(carry, keep(states), decay, keep(bc), keep(mixed), keep(factor))
 
 
-def post_kernel(place, slabs, own_gain, got_a, got_b, got_c, out):
+def post_kernel(slabs, own_gain, got_a, got_b, got_c, out):
     wide = slabs.shape[2]
     for y in range(4):
-        far = lax.rem(place[1] - y + 4, 4)
+        far = lax.rem(lax.axis_index("head") - y + 4, 4)
         gain = own_gain[...]
         for distance, got in ((1, got_a), (2, got_b), (3, got_c)):
             gain = jnp.where(far == distance, got[...], gain)
@@ -524,17 +495,17 @@
             out[:, at + wide : at + 2 * wide] = (b * inv * high).astype(BF16)
 
 
-def post(place, slabs, gains):
+def post(slabs, gains):
     members, rows, wide = slabs.shape
     return pl.pallas_call(
         post_kernel,
         out_shape=jax.ShapeDtypeStruct((rows, members * wide), BF16),
-        in_specs=[SMEM] + [VMEM] * 5,
+        in_specs=[VMEM] * 5,
         out_specs=VMEM,
         compiler_params=PARAMS,
         cost_estimate=cost(6 * members * rows * wide, 4 * members * rows * wide),
         name="post",
-    )(place, slabs, *gains)
+    )(slabs, *gains)
 
 
 def on_device(
@@ -553,7 +524,6 @@
     shards = lax.axis_size("head")
     chunks = places // 4
     x = (lax.axis_index("context") % 4).astype(jnp.int32)
-    place = jnp.stack([x, lax.axis_index("head").astype(jnp.int32)])
     rows = inner_raw.shape[0]
     after = [(c, c + 4) for c in range(places - 4)]
     teams = [list(range(TEAM * k, TEAM * (k + 1))) for k in range(places * shards // TEAM)]
@@ -570,8 +540,8 @@
     packed = pack(inner_raw, pairs_raw.reshape(rows, -1))
     step_rows = step_raw.T
     gain_row = norm_gain.reshape(1, -1)
-    gate_later, steps_later, gain_later, packed = lax.optimization_barrier(
-        (gate_raw, step_rows, gain_row, packed)
+    gate_later, steps_later, gain_later, w_inner, w_pairs, packed = lax.optimization_barrier(
+        (gate_raw, step_rows, gain_row, conv_inner, conv_pairs, packed)
     )
     recv = lax.all_to_all(
         packed, ("context", "head"), split_axis=0, concat_axis=0, axis_index_groups=teams
@@ -586,34 +556,37 @@
     *steps, recv = lax.optimization_barrier((*steps, recv))
     halo = lax.ppermute(recv[TEAM - 1, rows - 16 : rows], "context", after)
 
-    pair_taps = conv_pairs.reshape(conv_pairs.shape[0], -1)
-    own_steps = lax.dynamic_slice_in_dim(step_rows, 8 * x, 8, 0)
+    own_steps = lax.dynamic_slice_in_dim(steps_later, 8 * x, 8, 0)
+    own_gate = lax.dynamic_slice_in_dim(gate_later, x * width, width, 1)
+    w_pairs = w_pairs.reshape(w_pairs.shape[0], -1)
+    wide, narrow = w_inner.shape[1] // TEAM, w_pairs.shape[1] // 8
+    w_inner = lax.dynamic_slice_in_dim(w_inner, (4 * y + x) * wide, wide, 1)
+    w_pairs = lax.dynamic_slice_in_dim(w_pairs, (2 * y + x // 2) * narrow, narrow, 1)
     xc0, bc0, lc_t, dt_t, tail, decay, logs = conv(
-        place,
         recv,
-        conv_inner,
-        pair_taps,
+        w_inner,
+        w_pairs,
         step_bias.reshape(1, -1),
         rate_log.reshape(1, -1),
         [own_steps] + steps,
     )
     xc, bc, states, payload = state(
-        place, recv[0, :16], halo, conv_inner, pair_taps, xc0, bc0, tail, decay, logs, chunks
-    )
-    *gates, payload = lax.optimization_barrier((*gates, payload))
+        recv[0, :16], halo, w_inner, w_pairs, xc0, bc0, tail, decay, logs, chunks
+    )
+    gates[0], gates[1], payload = lax.optimization_barrier((gates[0], gates[1], payload))
     totals = lax.all_to_all(
         payload, "context", split_axis=0, concat_axis=0, axis_index_groups=lines
     )
-    *gains, totals = lax.optimization_barrier((*gains, totals))
+    gates[2], *gains, totals = lax.optimization_barrier((gates[2], *gains, totals))
     carry = lax.all_to_all(
         scan(totals), "context", split_axis=0, concat_axis=0, axis_index_groups=lines
     )
-    mixed, factor = intra(place, xc, bc, lc_t, dt_t, skip_gain.reshape(1, -1), gate_raw, gates)
+    mixed, factor = intra(xc, bc, lc_t, dt_t, skip_gain.reshape(1, -1), [own_gate] + gates)
     slabs = finish(carry, states, decay, bc, mixed, factor, rows)
     slabs = lax.all_to_all(
         slabs, ("context", "head"), split_axis=0, concat_axis=0, axis_index_groups=teams
     )
-    return post(place, slabs, [gain_row] + gains)
+    return post(slabs, [gain_row] + gains)
 
 
 def solution(mesh):

time: 101 us -> 99.7 us (0.987)
  Pallas kernels: 22.2 us -> 19.3 us
  waiting for transfers between devices: 24.1 us -> 25.7 us
  transfers between devices with their start and end apart: 13 -> 13, of which waited for: 6 -> 7; matrix products, arithmetic and copies ran while one was open for 1% -> 1% of each run, Pallas kernels for 14% -> 12%
where the time goes in v7:
time: 99.7 us; the launch traced here: 99.1 us
  starting transfers between devices  34.9 us (35%)
  waiting for transfers between devices  25.7 us (26%)
  Pallas kernels  19.3 us (19%)
  blocking collectives  16.7 us (17%)
  local copies, waits for them, and re-layouts  2.25 us (2%)
    ppermute x9, waiting for transfers between devices, around(): lax.ppermute(pick((position + far) % 4), axis, route)  16.9 us
    all_to_all x1, blocking collectives, on_device(): lax.all_to_all(slabs, ('context', 'head'), split_axis=0, concat_axis=0, a...  16.7 us
    ppermute x9, starting transfers between devices, around(): lax.ppermute(pick((position + far) % 4), axis, route)  12 us
    all_to_all x1, starting transfers between devices, on_device(): lax.all_to_all(payload, 'context', split_axis=0, concat_axis=0, axis_inde...  7.81 us
    all_to_all x1, starting transfers between devices, on_device(): lax.all_to_all(packed, ('context', 'head'), split_axis=0, concat_axis=0,...  7.54 us
    pallas_call x1, Pallas kernels, intra(): pl.pallas_call(intra_kernel, out_shape=(pltpu.HBM((total, wide), BF16),)...  5.97 us
    all_to_all x1, waiting for transfers between devices, on_device(): lax.all_to_all(scan(totals), 'context', split_axis=0, concat_axis=0, axis...  4.49 us
    pallas_call x1, Pallas kernels, conv(): pl.pallas_call(conv_kernel, out_shape=tuple((jax.ShapeDtypeStruct(*s) for...  3.82 us
  transfers between devices with their start and end apart: 13, of which 7 were waited for; matrix products, arithmetic and copies ran while one was open for 1% of the time, Pallas kernels for 12%

profile of v7, /device:TPU:8, one launch (start us, length us, event | category | flops | bytes accessed | tf_op | source)
XLA Modules:
  0.0 99.1 jit_solution(12643244943733116364)
XLA Ops:
  0.0 0.0 copy-start
  0.0 1.2 %reshape.19.pairs = bf16[64,2048]{1,0:T(8,128)(2,1)S(1)} reshape(bf16[64,8,2,128]{3,2,1,0:T(2,128)(2,1)} %param.11) | data formatting | bytes 524288 | tf_op jit(solution)/shard_map/reshape | solution.py:540
  1.2 2.6 %pack.1 = bf16[16,64,768]{2,1,0:T(8,128)(2,1)} custom-call(bf16[64,8192]{1,0:T(8,128)(2,1)} %inner.1, bf16[64,2048]{1,0:T(8,128)(2,1)S(1)} %reshape.19.pairs), custom_call_target="tpu_custom_call" | custom-call | bytes 3145728 | tf_op jit(solution)/shard_map/pack/pallas_call | solution.py:107
  3.8 0.0 copy-start.10
  3.8 0.0 copy-start.7
  3.8 7.5 %all-to-all-start = ((bf16[16,64,768]{2,1,0:T(8,128)(2,1)}), bf16[16,64,768]{2,1,0:T(8,128)(2,1)S(1)}, u32[]{:S(2)}, u32[]{:S(2)}) async-start(bf16[16,64,768]{2,1,0:T(8,128)(2,1)} %pack.1), calls=%async_computation | async-start | bytes 3145728 | tf_op jit(solution)/shard_map/all_to_all | solution.py:546
  11.3 0.0 copy-start.9
  11.3 0.0 copy-start.4
  11.3 0.0 copy-start.5
  11.4 0.0 copy-done.10
  11.5 1.5 %collective-permute-start.6 = (bf16[8,256]{1,0:T(8,128)(2,1)S(1)}, bf16[8,256]{1,0:T(8,128)(2,1)S(1)}, u32[]{:S(2)}, u32[]{:S(2)}) collective-permute-start(bf16[8,256]{1,0:T(8,128)(2,1)S(1)} %get-tuple-element.76), channel_id=1, source_target_pairs={{0,4},{4,8},{8,12},{12,0},{16,20},{20,24},{24,28},{28,16},{32,36},... | collective-permute-start | bytes 12296 | tf_op jit(solution)/shard_map/ppermute | solution.py:536
  13.0 2.7 %collective-permute-start.7 = (bf16[8,256]{1,0:T(8,128)(2,1)S(1)}, bf16[8,256]{1,0:T(8,128)(2,1)S(1)}, u32[]{:S(2)}, u32[]{:S(2)}) collective-permute-start(bf16[8,256]{1,0:T(8,128)(2,1)S(1)} %get-tuple-element.75), channel_id=1, source_target_pairs={{0,8},{4,12},{8,0},{12,4},{16,24},{20,28},{24,16},{28,20},{32,40},... | collective-permute-start | bytes 12296 | tf_op jit(solution)/shard_map/ppermute | solution.py:536
  15.7 1.5 %collective-permute-start.8 = (bf16[8,256]{1,0:T(8,128)(2,1)S(1)}, bf16[8,256]{1,0:T(8,128)(2,1)S(1)}, u32[]{:S(2)}, u32[]{:S(2)}) collective-permute-start(bf16[8,256]{1,0:T(8,128)(2,1)S(1)} %get-tuple-element.74), channel_id=1, source_target_pairs={{0,12},{4,0},{8,4},{12,8},{16,28},{20,16},{24,20},{28,24},{32,44},... | collective-permute-start | bytes 12296 | tf_op jit(solution)/shard_map/ppermute | solution.py:536
  17.1 0.0 copy-done.7
  17.2 0.9 constant_dynamic-slice_fusion
  18.1 0.6 collective-permute-start.4
  18.7 0.9 collective-permute-start.5
  19.6 0.0 copy-done
  19.6 0.0 copy-done.9
  19.6 12.9 %collective-permute-done.6.got_a = bf16[8,256]{1,0:T(8,128)(2,1)S(1)} collective-permute-done((bf16[8,256]{1,0:T(8,128)(2,1)S(1)}, bf16[8,256]{1,0:T(8,128)(2,1)S(1)}, u32[]{:S(2)}, u32[]{:S(2)}) %collective-permute-start.6) | collective-permute-done | bytes 4128 | tf_op jit(solution)/shard_map/ppermute | solution.py:536
  32.5 0.7 collective-permute-done.7.got_b
  33.2 0.0 collective-permute-done.8.got_c
  33.2 1.0 all-to-all-done.recv
  34.2 3.8 %collective-permute-start.9 = (bf16[16,768]{1,0:T(8,128)(2,1)S(1)}, bf16[16,768]{1,0:T(8,128)(2,1)S(1)}, u32[]{:S(2)}, u32[]{:S(2)}) collective-permute-start(bf16[16,768]{1,0:T(8,128)(2,1)S(1)} %get-tuple-element.67), channel_id=1, source_target_pairs={{0,16},{4,20},{8,24},{12,28},{16,32},{20,36},{24,40},{28,44},{32,4... | collective-permute-start | bytes 73736 | tf_op jit(solution)/shard_map/ppermute | solution.py:557
  38.0 0.0 copy-done.4
  38.0 0.0 copy-done.5
  38.1 3.8 %conv.1 = (bf16[1024,512]{1,0:T(8,128)(2,1)S(1)}, bf16[1024,256]{1,0:T(8,128)(2,1)S(1)}, f32[4,8,256]{2,1,0:T(8,128)S(1)}, f32[4,8,256]{2,1,0:T(8,128)S(1)}, f32...) custom-call(bf16[16,64,768]{2,1,0:T(8,128)(2,1)S(1)} %all-to-all-done.recv, ...), custom_call_target="tpu_custom_call" | custom-call | flops 15728640 | bytes 3145728 | tf_op jit(solution)/shard_map/conv/pallas_call | solution.py:219
  41.9 0.0 collective-permute-done.9.halo
  41.9 0.0 copy-start.8
  41.9 0.0 copy-start.2
  41.9 2.3 %state.1 = (bf16[1024,512]{1,0:T(8,128)(2,1)}, bf16[1024,256]{1,0:T(8,128)(2,1)}, f32[4,128,512]{2,1,0:T(8,128)}, f32[8,16,640]{2,1,0:T(8,128)}) custom-call(bf16[16,768]{1,0:T(8,128)(2,1)S(1)} %get-tuple-element.68.first, bf16[16,768]{1,0:T(8,128)(2,1)S(1)} %collective-permute-done.9.halo, f32[5,512]{1,0:T(8,128)S(1)} %constant_dynamic-slice_fusion.3.w_inner, ...), custom_call_target="tpu_custom_call" | custom-call | flops 134217728 | bytes 4194304 | tf_op jit(solution)/shard_map/state/pallas_call | solution.py:308
  44.2 0.0 copy-start.1
  44.3 0.0 copy-start.3
  44.3 0.0 copy-start.6
  44.3 0.0 collective-permute-done.4.got_a
  44.3 0.0 collective-permute-done.5.got_b
  44.3 7.8 %all-to-all-start.1 = ((f32[8,16,640]{2,1,0:T(8,128)}), f32[8,16,640]{2,1,0:T(8,128)S(1)}, u32[]{:S(2)}, u32[]{:S(2)}) async-start(f32[8,16,640]{2,1,0:T(8,128)} %get-tuple-element.52), calls=%async_computation.1 | async-start | bytes 655360 | tf_op jit(solution)/shard_map/all_to_all | solution.py:577
  52.1 0.0 copy-done.8
  52.1 0.9 collective-permute-start
  53.1 0.0 copy-done.2
  53.1 0.7 collective-permute-start.1
  53.7 2.9 %collective-permute-start.2 = (f32[1,2048]{1,0:T(1,128)S(1)}, f32[1,2048]{1,0:T(1,128)S(1)}, u32[]{:S(2)}, u32[]{:S(2)}) collective-permute-start(f32[1,2048]{1,0:T(1,128)S(1)} %bitcast.10), channel_id=1, source_target_pairs={{0,2},{1,3},{2,0},{3,1},{4,6},{5,7},{6,4},{7,5},{8,10},{9,11},{10,... | collective-permute-start | bytes 24584 | tf_op jit(solution)/shard_map/ppermute | solution.py:536
  56.6 0.4 collective-permute-start.3
  57.0 0.0 collective-permute-done.1.got_a
  57.0 1.9 %collective-permute-done.2.got_b = f32[1,2048]{1,0:T(1,128)S(1)} collective-permute-done((f32[1,2048]{1,0:T(1,128)S(1)}, f32[1,2048]{1,0:T(1,128)S(1)}, u32[]{:S(2)}, u32[]{:S(2)}) %collective-permute-start.2) | collective-permute-done | bytes 8224 | tf_op jit(solution)/shard_map/ppermute | solution.py:536
  58.9 1.4 %collective-permute-done.3.got_c = f32[1,2048]{1,0:T(1,128)S(1)} collective-permute-done((f32[1,2048]{1,0:T(1,128)S(1)}, f32[1,2048]{1,0:T(1,128)S(1)}, u32[]{:S(2)}, u32[]{:S(2)}) %collective-permute-start.3) | collective-permute-done | bytes 8224 | tf_op jit(solution)/shard_map/ppermute | solution.py:536
  60.3 0.0 collective-permute-done.got_c
  60.3 3.4 %all-to-all-done.1.recv = f32[8,16,640]{2,1,0:T(8,128)S(1)} async-done(((f32[8,16,640]{2,1,0:T(8,128)}), f32[8,16,640]{2,1,0:T(8,128)S(1)}, u32[]{:S(2)}, u32[]{:S(2)}) %all-to-all-start.1) | async-done | bytes 327712 | tf_op jit(solution)/shard_map/all_to_all | solution.py:577
  63.6 0.9 scan.1
  64.6 3.7 %all-to-all-start.2 = ((f32[8,16,512]{2,1,0:T(8,128)}), f32[8,16,512]{2,1,0:T(8,128)S(1)}, u32[]{:S(2)}, u32[]{:S(2)}) async-start(f32[8,16,512]{2,1,0:T(8,128)} %scan.1), calls=%async_computation.2 | async-start | bytes 524288 | tf_op jit(solution)/shard_map/all_to_all | solution.py:581
  68.3 0.0 copy-done.1
  68.3 0.0 copy-done.3
  68.3 0.0 copy-done.6
  68.3 6.0 %intra.1 = (bf16[1024,512]{1,0:T(8,128)(2,1)}, bf16[1024,512]{1,0:T(8,128)(2,1)}) custom-call(bf16[1024,512]{1,0:T(8,128)(2,1)S(1)} %copy-done.3, bf16[1024,256]{1,0:T(8,128)(2,1)S(1)} %copy-done.1, f32[4,8,256]{2,1,0:T(8,128)S(1)} %get-tuple-element.57.lc_t, f32[4,8,256]{2,1,0:T(8,128)S(1)} %get-tuple-element.58.dt_t, f32[1,32]{1,0:T(1,128)S(1)} %bitcast.15, ...), custom_call_target="tpu_custom_call" | custom-call | flops 1073741824 | bytes 6291456 | tf_op jit(solution)/shard_map/intra/pallas_call | solution.py:386
  74.3 4.5 %all-to-all-done.2.carry = f32[8,16,512]{2,1,0:T(8,128)S(1)} async-done(((f32[8,16,512]{2,1,0:T(8,128)}), f32[8,16,512]{2,1,0:T(8,128)S(1)}, u32[]{:S(2)}, u32[]{:S(2)}) %all-to-all-start.2) | async-done | bytes 262176 | tf_op jit(solution)/shard_map/all_to_all | solution.py:581
  78.8 2.3 %finish.1 = bf16[16,64,512]{2,1,0:T(8,128)(2,1)S(1)} custom-call(f32[8,16,512]{2,1,0:T(8,128)S(1)} %all-to-all-done.2.carry, f32[4,128,512]{2,1,0:T(8,128)} %get-tuple-element.54.states, f32[8,512]{1,0:T(8,128)S(1)} %get-tuple-element.49.decay, bf16[1024,256]{1,0:T(8,128)(2,1)} %get-tuple-element.55.bc, bf16[1024,512]{1,0:T(8,128)(2,1)} %get-tuple-element.62.mixed, ...), custom_call_target="tpu_custom_call" | custom-call | flops 209715200 | bytes 3145728 | tf_op jit(solution)/shard_map/finish/pallas_call | solution.py:459
  81.1 16.7 %all_to_all.20.slabs = bf16[16,64,512]{2,1,0:T(8,128)(2,1)S(1)} all-to-all(bf16[16,64,512]{2,1,0:T(8,128)(2,1)S(1)} %finish.1), channel_id=1, replica_groups={{0,1,2,3,4,5,6,7,8,9,10,11,12,13,14,15},{16,17,18,19,20,21,22,23,24,25,..., dimensions={0} | all-to-all | bytes 2097152 | tf_op jit(solution)/shard_map/all_to_all | solution.py:586
  97.7 1.4 %post.1 = bf16[64,8192]{1,0:T(8,128)(2,1)} custom-call(bf16[16,64,512]{2,1,0:T(8,128)(2,1)S(1)} %all_to_all.20.slabs, f32[1,2048]{1,0:T(1,128)S(1)} %bitcast.12, f32[1,2048]{1,0:T(1,128)S(1)} %collective-permute-done.1.got_a, f32[1,2048]{1,0:T(1,128)S(1)} %collective-permute-done.2.got_b, f32[1,2048]{1,0:T(1,128)S(1)} %collective-permute-done.3.got_c), custom_call_target="tpu_custom_call" | custom-call | flops 3145728 | bytes 2097152 | tf_op jit(solution)/shard_map/post/pallas_call | solution.py:500
  (5 shorter events, 0.1 us)
Async XLA Ops:
  0.0 19.6 %copy-start = (f32[5,8192]{1,0:T(8,128)S(1)}, f32[5,8192]{1,0:T(8,128)}, u32[]{:S(2)}) copy-start(f32[5,8192]{1,0:T(8,128)} %param.17) | copy-start | bytes 491524
  3.8 7.7 %copy-start.10 = (bf16[256,32]{0,1:T(8,128)(2,1)S(1)}, bf16[256,32]{0,1:T(8,128)(2,1)}, u32[]{:S(2)}) copy-start(bf16[256,32]{0,1:T(8,128)(2,1)} %param.13) | copy-start | bytes 49156
  3.8 13.4 %copy-start.7 = (bf16[256,2048]{1,0:T(8,128)(2,1)S(1)}, bf16[256,2048]{1,0:T(8,128)(2,1)}, u32[]{:S(2)}) copy-start(bf16[256,2048]{1,0:T(8,128)(2,1)} %param.12) | copy-start | bytes 3145732
  3.8 30.4 %all-to-all-start = ((bf16[16,64,768]{2,1,0:T(8,128)(2,1)}), bf16[16,64,768]{2,1,0:T(8,128)(2,1)S(1)}, u32[]{:S(2)}, u32[]{:S(2)}) async-start(bf16[16,64,768]{2,1,0:T(8,128)(2,1)} %pack.1), calls=%async_computation | async-start | bytes 3145728 | tf_op jit(solution)/shard_map/all_to_all | solution.py:546
  11.3 8.2 %copy-start.9 = (f32[5,8,2,128]{3,2,1,0:T(2,128)S(1)}, f32[5,8,2,128]{3,2,1,0:T(2,128)}, u32[]{:S(2)}) copy-start(f32[5,8,2,128]{3,2,1,0:T(2,128)} %param.18) | copy-start | bytes 122884
  11.3 26.7 %copy-start.4 = (f32[32]{0:T(128)S(1)}, f32[32]{0:T(128)}, u32[]{:S(2)}) copy-start(f32[32]{0:T(128)} %param.14) | copy-start | bytes 388
  11.3 26.7 %copy-start.5 = (f32[32]{0:T(128)S(1)}, f32[32]{0:T(128)}, u32[]{:S(2)}) copy-start(f32[32]{0:T(128)} %param.15) | copy-start | bytes 388
  11.5 21.1 %collective-permute-start.6 = (bf16[8,256]{1,0:T(8,128)(2,1)S(1)}, bf16[8,256]{1,0:T(8,128)(2,1)S(1)}, u32[]{:S(2)}, u32[]{:S(2)}) collective-permute-start(bf16[8,256]{1,0:T(8,128)(2,1)S(1)} %get-tuple-element.76), channel_id=1, source_target_pairs={{0,4},{4,8},{8,12},{12,0},{16,20},{20,24},{24,28},{28,16},{32,36},... | collective-permute-start | bytes 12296 | tf_op jit(solution)/shard_map/ppermute | solution.py:536
  13.0 20.2 %collective-permute-start.7 = (bf16[8,256]{1,0:T(8,128)(2,1)S(1)}, bf16[8,256]{1,0:T(8,128)(2,1)S(1)}, u32[]{:S(2)}, u32[]{:S(2)}) collective-permute-start(bf16[8,256]{1,0:T(8,128)(2,1)S(1)} %get-tuple-element.75), channel_id=1, source_target_pairs={{0,8},{4,12},{8,0},{12,4},{16,24},{20,28},{24,16},{28,20},{32,40},... | collective-permute-start | bytes 12296 | tf_op jit(solution)/shard_map/ppermute | solution.py:536
  15.7 17.5 %collective-permute-start.8 = (bf16[8,256]{1,0:T(8,128)(2,1)S(1)}, bf16[8,256]{1,0:T(8,128)(2,1)S(1)}, u32[]{:S(2)}, u32[]{:S(2)}) collective-permute-start(bf16[8,256]{1,0:T(8,128)(2,1)S(1)} %get-tuple-element.74), channel_id=1, source_target_pairs={{0,12},{4,0},{8,4},{12,8},{16,28},{20,16},{24,20},{28,24},{32,44},... | collective-permute-start | bytes 12296 | tf_op jit(solution)/shard_map/ppermute | solution.py:536
  18.1 26.2 %collective-permute-start.4 = (bf16[256,512]{1,0:T(8,128)(2,1)}, bf16[256,512]{1,0:T(8,128)(2,1)S(1)}, u32[]{:S(2)}, u32[]{:S(2)}) collective-permute-start(bf16[256,512]{1,0:T(8,128)(2,1)} %get-tuple-element.71), channel_id=1, source_target_pairs={{0,4},{4,8},{8,12},{12,0},{16,20},{20,24},{24,28},{28,16},{32,36},... | collective-permute-start | bytes 786440 | tf_op jit(solution)/shard_map/ppermute | solution.py:536
  18.7 25.6 %collective-permute-start.5 = (bf16[256,512]{1,0:T(8,128)(2,1)}, bf16[256,512]{1,0:T(8,128)(2,1)}, u32[]{:S(2)}, u32[]{:S(2)}) collective-permute-start(bf16[256,512]{1,0:T(8,128)(2,1)} %get-tuple-element.70), channel_id=1, source_target_pairs={{0,8},{4,12},{8,0},{12,4},{16,24},{20,28},{24,16},{28,20},{32,40},... | collective-permute-start | bytes 786440 | tf_op jit(solution)/shard_map/ppermute | solution.py:536
  34.2 7.7 %collective-permute-start.9 = (bf16[16,768]{1,0:T(8,128)(2,1)S(1)}, bf16[16,768]{1,0:T(8,128)(2,1)S(1)}, u32[]{:S(2)}, u32[]{:S(2)}) collective-permute-start(bf16[16,768]{1,0:T(8,128)(2,1)S(1)} %get-tuple-element.67), channel_id=1, source_target_pairs={{0,16},{4,20},{8,24},{12,28},{16,32},{20,36},{24,40},{28,44},{32,4... | collective-permute-start | bytes 73736 | tf_op jit(solution)/shard_map/ppermute | solution.py:557
  41.9 10.2 %copy-start.8 = (bf16[256,512]{1,0:T(8,128)(2,1)S(1)}, bf16[256,512]{1,0:T(8,128)(2,1)}, u32[]{:S(2)}) copy-start(bf16[256,512]{1,0:T(8,128)(2,1)} %get-tuple-element.72) | copy-start | bytes 786436
  41.9 11.2 %copy-start.2 = (f32[2048]{0:T(1024)S(1)}, f32[2048]{0:T(1024)}, u32[]{:S(2)}) copy-start(f32[2048]{0:T(1024)} %param.19) | copy-start | bytes 24580
  44.2 24.1 %copy-start.1 = (bf16[1024,256]{1,0:T(8,128)(2,1)S(1)}, bf16[1024,256]{1,0:T(8,128)(2,1)}, u32[]{:S(2)}) copy-start(bf16[1024,256]{1,0:T(8,128)(2,1)} %get-tuple-element.55.bc) | copy-start | bytes 1572868
  44.3 24.1 %copy-start.3 = (bf16[1024,512]{1,0:T(8,128)(2,1)S(1)}, bf16[1024,512]{1,0:T(8,128)(2,1)}, u32[]{:S(2)}) copy-start(bf16[1024,512]{1,0:T(8,128)(2,1)} %get-tuple-element.56.xc) | copy-start | bytes 3145732
  44.3 24.0 %copy-start.6 = (f32[32]{0:T(128)S(1)}, f32[32]{0:T(128)}, u32[]{:S(2)}) copy-start(f32[32]{0:T(128)} %param.16) | copy-start | bytes 388
  44.3 19.3 %all-to-all-start.1 = ((f32[8,16,640]{2,1,0:T(8,128)}), f32[8,16,640]{2,1,0:T(8,128)S(1)}, u32[]{:S(2)}, u32[]{:S(2)}) async-start(f32[8,16,640]{2,1,0:T(8,128)} %get-tuple-element.52), calls=%async_computation.1 | async-start | bytes 655360 | tf_op jit(solution)/shard_map/all_to_all | solution.py:577
  52.1 8.1 %collective-permute-start = (bf16[256,512]{1,0:T(8,128)(2,1)S(1)}, bf16[256,512]{1,0:T(8,128)(2,1)S(1)}, u32[]{:S(2)}, u32[]{:S(2)}) collective-permute-start(bf16[256,512]{1,0:T(8,128)(2,1)S(1)} %copy-done.8), channel_id=1, source_target_pairs={{0,12},{4,0},{8,4},{12,8},{16,28},{20,16},{24,20},{28,24},{32,44},... | collective-permute-start | bytes 786440 | tf_op jit(solution)/shard_map/ppermute | solution.py:536
  53.1 3.9 %collective-permute-start.1 = (f32[1,2048]{1,0:T(1,128)S(1)}, f32[1,2048]{1,0:T(1,128)S(1)}, u32[]{:S(2)}, u32[]{:S(2)}) collective-permute-start(f32[1,2048]{1,0:T(1,128)S(1)} %bitcast.9), channel_id=1, source_target_pairs={{0,1},{1,2},{2,3},{3,0},{4,5},{5,6},{6,7},{7,4},{8,9},{9,10},{10,1... | collective-permute-start | bytes 24584 | tf_op jit(solution)/shard_map/ppermute | solution.py:536
  53.7 5.2 %collective-permute-start.2 = (f32[1,2048]{1,0:T(1,128)S(1)}, f32[1,2048]{1,0:T(1,128)S(1)}, u32[]{:S(2)}, u32[]{:S(2)}) collective-permute-start(f32[1,2048]{1,0:T(1,128)S(1)} %bitcast.10), channel_id=1, source_target_pairs={{0,2},{1,3},{2,0},{3,1},{4,6},{5,7},{6,4},{7,5},{8,10},{9,11},{10,... | collective-permute-start | bytes 24584 | tf_op jit(solution)/shard_map/ppermute | solution.py:536
  56.6 3.7 %collective-permute-start.3 = (f32[1,2048]{1,0:T(1,128)S(1)}, f32[1,2048]{1,0:T(1,128)S(1)}, u32[]{:S(2)}, u32[]{:S(2)}) collective-permute-start(f32[1,2048]{1,0:T(1,128)S(1)} %bitcast.11), channel_id=1, source_target_pairs={{0,3},{1,0},{2,1},{3,2},{4,7},{5,4},{6,5},{7,6},{8,11},{9,8},{10,9... | collective-permute-start | bytes 24584 | tf_op jit(solution)/shard_map/ppermute | solution.py:536
  64.6 14.2 %all-to-all-start.2 = ((f32[8,16,512]{2,1,0:T(8,128)}), f32[8,16,512]{2,1,0:T(8,128)S(1)}, u32[]{:S(2)}, u32[]{:S(2)}) async-start(f32[8,16,512]{2,1,0:T(8,128)} %scan.1), calls=%async_computation.2 | async-start | bytes 524288 | tf_op jit(solution)/shard_map/all_to_all | solution.py:581

commit v8 on v7

--- a/solution.py
+++ b/solution.py
@@ -67,10 +67,10 @@
 
 
 def pack_kernel(
-    inner, pairs, out, staged, stage_sem, sem, pairs_sem
+    inner, pairs, out, staged, local, flat, stage_sem, sem, pairs_sem, local_sem
 ):
     rows, full = inner.shape
-    wide, narrow = full // TEAM, pairs.shape[1] // 8
+    wide, narrow = full // TEAM, 2 * pairs.shape[3]
     stages, copies, more = [], [], []
     for member in range(TEAM):
         px, py = member // 4, member % 4
@@ -85,13 +85,22 @@
         )
         more.append(
             pltpu.make_async_copy(
-                pairs.at[:, pl.ds((2 * py + px // 2) * narrow, narrow)],
+                flat.at[:, pl.ds((2 * py + px // 2) * narrow, narrow)],
                 out.at[member, pl.ds(0, rows), pl.ds(wide, narrow)],
                 pairs_sem.at[member],
             )
         )
+    fetch = pltpu.make_async_copy(pairs, local, local_sem)
+    fetch.start()
     for copy in stages:
         copy.start()
+    fetch.wait()
+    half = pairs.shape[3]
+    for group in range(pairs.shape[1]):
+        both = local[:, group].astype(F32)
+        for k in range(2):
+            at = group * narrow + k * half
+            flat[:, at : at + half] = both[:, k].astype(BF16)
     for copy in more:
         copy.start()
     for stage, copy in zip(stages, copies):
@@ -103,7 +112,7 @@
 
 def pack(inner, pairs):
     rows = inner.shape[0]
-    width = inner.shape[1] // TEAM + pairs.shape[1] // 8
+    width = inner.shape[1] // TEAM + 2 * pairs.shape[3]
     return pl.pallas_call(
         pack_kernel,
         out_shape=jax.ShapeDtypeStruct((TEAM, rows, width), BF16),
@@ -111,14 +120,17 @@
         out_specs=ANY,
         scratch_shapes=[
             pltpu.VMEM(inner.shape, BF16),
+            pltpu.VMEM(pairs.shape, BF16),
+            pltpu.VMEM((rows, pairs.shape[1] * 2 * pairs.shape[3]), BF16),
             pltpu.SemaphoreType.DMA((TEAM,)),
             pltpu.SemaphoreType.DMA((TEAM,)),
             pltpu.SemaphoreType.DMA((TEAM,)),
+            pltpu.SemaphoreType.DMA,
         ],
         compiler_params=PARAMS,
         cost_estimate=cost(0, 4 * TEAM * rows * width),
         name="pack",
-    )(keep(inner), pairs)
+    )(keep(inner), keep(pairs))
 
 
 def taps(ext, row, rows, cols, weight):
@@ -385,7 +397,7 @@
     heads = lc_t.shape[1]
     return pl.pallas_call(
         intra_kernel,
-        out_shape=(pltpu.HBM((total, wide), BF16),) * 2,
+        out_shape=(jax.ShapeDtypeStruct((total, wide), BF16),) * 2,
         grid=(4,),
         in_specs=[
             pl.BlockSpec((BLOCK, wide), lambda b: (b, 0)),
@@ -399,7 +411,7 @@
         compiler_params=PARAMS,
         cost_estimate=cost(2 * total * BLOCK * wide * 4, 12 * total * wide, heads * total * BLOCK),
         name="intra",
-    )(xc, bc, lc_t, dt_t, skip, *gates)
+    )(keep(xc), keep(bc), lc_t, dt_t, skip, *[keep(gate) for gate in gates])
 
 
 def scan_kernel(recv, out):
@@ -427,7 +439,7 @@
     )(recv)
 
 
-def finish_kernel(carry, states, decay, bc, mixed, factor, out, s_in, c_in, m_in, f_in, sem):
+def finish_kernel(carry, states, decay, bc, mixed, factor, out, s_in, c_in, sem):
     wide = mixed.shape[1]
     copies = []
     for b in range(4):
@@ -435,9 +447,7 @@
         copies.append(
             [
                 pltpu.make_async_copy(bc.at[rows, pl.ds(LANES, LANES)], c_in.at[b], sem.at[b, 0]),
-                pltpu.make_async_copy(mixed.at[rows], m_in.at[b], sem.at[b, 1]),
-                pltpu.make_async_copy(factor.at[rows], f_in.at[b], sem.at[b, 2]),
-                pltpu.make_async_copy(states.at[b], s_in.at[b], sem.at[b, 3]),
+                pltpu.make_async_copy(states.at[b], s_in.at[b], sem.at[b, 1]),
             ]
         )
     for group in copies:
@@ -448,7 +458,8 @@
         for copy in copies[b]:
             copy.wait()
         carried = jnp.dot(c_in[b], start.astype(BF16), preferred_element_type=F32)
-        gated = m_in[b].astype(F32) + carried * f_in[b].astype(F32)
+        rows = slice(b * BLOCK, (b + 1) * BLOCK)
+        gated = mixed[rows].astype(F32) + carried * factor[rows].astype(F32)
         count = BLOCK // out.shape[1]
         out[b * count : (b + 1) * count] = gated.astype(BF16).reshape(count, -1, wide)
         start = decay[b : b + 1] * start + s_in[b]
@@ -459,19 +470,17 @@
     return pl.pallas_call(
         finish_kernel,
         out_shape=jax.ShapeDtypeStruct((total // rows, rows, wide), BF16),
-        in_specs=[VMEM, ANY, VMEM, ANY, ANY, ANY],
+        in_specs=[VMEM, ANY, VMEM, ANY, VMEM, VMEM],
         out_specs=VMEM,
         scratch_shapes=[
             pltpu.VMEM((4, LANES, wide), F32),
             pltpu.VMEM((4, BLOCK, LANES), BF16),
-            pltpu.VMEM((4, BLOCK, wide), BF16),
-            pltpu.VMEM((4, BLOCK, wide), BF16),
-            pltpu.SemaphoreType.DMA((4, 4)),
+            pltpu.SemaphoreType.DMA((4, 2)),
         ],
         compiler_params=PARAMS,
         cost_estimate=cost(2 * total * wide * 200, 6 * total * wide),
         name="finish",
-    )(carry, keep(states), decay, keep(bc), keep(mixed), keep(factor))
+    )(carry, keep(states), decay, keep(bc), mixed, factor)
 
 
 def post_kernel(slabs, own_gain, got_a, got_b, got_c, out):
@@ -537,7 +546,7 @@
             for far, route in zip((1, 2, 3), routes)
         ]
 
-    packed = pack(inner_raw, pairs_raw.reshape(rows, -1))
+    packed = pack(inner_raw, pairs_raw)
     step_rows = step_raw.T
     gain_row = norm_gain.reshape(1, -1)
     gate_later, steps_later, gain_later, w_inner, w_pairs, packed = lax.optimization_barrier(

time: 99.7 us -> 98.9 us (level)
  local copies, waits for them, and re-layouts: 2.25 us -> 1.02 us
    reshape x1 -> x0, local copies, waits for them, and re-layouts: 1.18 us -> none  [on_device(): packed = pack(inner_raw, pairs_raw.reshape(rows, -1))]
where the time goes in v8:
time: 98.9 us; the launch traced here: 98.4 us
  starting transfers between devices  34.7 us (35%)
  waiting for transfers between devices  26.2 us (26%)
  Pallas kernels  19.5 us (20%)
  blocking collectives  16.7 us (17%)
  local copies, waits for them, and re-layouts  1.02 us (1%)
    ppermute x9, waiting for transfers between devices, around(): lax.ppermute(pick((position + far) % 4), axis, route)  16.9 us
    all_to_all x1, blocking collectives, on_device(): lax.all_to_all(slabs, ('context', 'head'), split_axis=0, concat_axis=0, a...  16.7 us
    ppermute x9, starting transfers between devices, around(): lax.ppermute(pick((position + far) % 4), axis, route)  11.9 us
    all_to_all x1, starting transfers between devices, on_device(): lax.all_to_all(payload, 'context', split_axis=0, concat_axis=0, axis_inde...  7.69 us
    all_to_all x1, starting transfers between devices, on_device(): lax.all_to_all(packed, ('context', 'head'), split_axis=0, concat_axis=0,...  7.54 us
    pallas_call x1, Pallas kernels, intra(): pl.pallas_call(intra_kernel, out_shape=(jax.ShapeDtypeStruct((total, wide...  5.66 us
    all_to_all x1, waiting for transfers between devices, on_device(): lax.all_to_all(scan(totals), 'context', split_axis=0, concat_axis=0, axis...  4.79 us
    pallas_call x1, Pallas kernels, conv(): pl.pallas_call(conv_kernel, out_shape=tuple((jax.ShapeDtypeStruct(*s) for...  3.82 us
  transfers between devices with their start and end apart: 13, of which 7 were waited for; matrix products, arithmetic and copies ran while one was open for 1% of the time, Pallas kernels for 12%

profile of v8, /device:TPU:8, one launch (start us, length us, event | category | flops | bytes accessed | tf_op | source)
XLA Modules:
  0.0 98.4 jit_solution(6031503903129084007)
XLA Ops:
  0.0 0.0 copy-start
  0.0 3.4 %pack.1 = bf16[16,64,768]{2,1,0:T(8,128)(2,1)} custom-call(bf16[64,8192]{1,0:T(8,128)(2,1)} %inner.1, bf16[64,8,2,128]{3,2,1,0:T(2,128)(2,1)} %pairs.1), custom_call_target="tpu_custom_call" | custom-call | bytes 3145728 | tf_op jit(solution)/shard_map/pack/pallas_call | solution.py:116
  3.4 0.0 copy-start.7
  3.4 0.0 copy-start.5
  3.4 7.5 %all-to-all-start = ((bf16[16,64,768]{2,1,0:T(8,128)(2,1)}), bf16[16,64,768]{2,1,0:T(8,128)(2,1)S(1)}, u32[]{:S(2)}, u32[]{:S(2)}) async-start(bf16[16,64,768]{2,1,0:T(8,128)(2,1)} %pack.1), calls=%async_computation | async-start | bytes 3145728 | tf_op jit(solution)/shard_map/all_to_all | solution.py:555
  10.9 0.0 copy-start.6
  10.9 0.0 copy-start.2
  10.9 0.0 copy-start.3
  11.0 0.0 copy-done.7
  11.1 1.5 %collective-permute-start.6 = (bf16[8,256]{1,0:T(8,128)(2,1)S(1)}, bf16[8,256]{1,0:T(8,128)(2,1)S(1)}, u32[]{:S(2)}, u32[]{:S(2)}) collective-permute-start(bf16[8,256]{1,0:T(8,128)(2,1)S(1)} %get-tuple-element.76), channel_id=1, source_target_pairs={{0,4},{4,8},{8,12},{12,0},{16,20},{20,24},{24,28},{28,16},{32,36},... | collective-permute-start | bytes 12296 | tf_op jit(solution)/shard_map/ppermute | solution.py:545
  12.6 2.7 %collective-permute-start.7 = (bf16[8,256]{1,0:T(8,128)(2,1)S(1)}, bf16[8,256]{1,0:T(8,128)(2,1)S(1)}, u32[]{:S(2)}, u32[]{:S(2)}) collective-permute-start(bf16[8,256]{1,0:T(8,128)(2,1)S(1)} %get-tuple-element.75), channel_id=1, source_target_pairs={{0,8},{4,12},{8,0},{12,4},{16,24},{20,28},{24,16},{28,20},{32,40},... | collective-permute-start | bytes 12296 | tf_op jit(solution)/shard_map/ppermute | solution.py:545
  15.3 1.5 %collective-permute-start.8 = (bf16[8,256]{1,0:T(8,128)(2,1)S(1)}, bf16[8,256]{1,0:T(8,128)(2,1)S(1)}, u32[]{:S(2)}, u32[]{:S(2)}) collective-permute-start(bf16[8,256]{1,0:T(8,128)(2,1)S(1)} %get-tuple-element.74), channel_id=1, source_target_pairs={{0,12},{4,0},{8,4},{12,8},{16,28},{20,16},{24,20},{28,24},{32,44},... | collective-permute-start | bytes 12296 | tf_op jit(solution)/shard_map/ppermute | solution.py:545
  16.7 0.0 copy-done.5
  16.7 0.9 constant_dynamic-slice_fusion
  17.6 0.6 collective-permute-start.4
  18.2 0.9 collective-permute-start.5
  19.1 0.0 copy-done
  19.1 0.0 copy-done.6
  19.2 13.0 %collective-permute-done.6.got_a = bf16[8,256]{1,0:T(8,128)(2,1)S(1)} collective-permute-done((bf16[8,256]{1,0:T(8,128)(2,1)S(1)}, bf16[8,256]{1,0:T(8,128)(2,1)S(1)}, u32[]{:S(2)}, u32[]{:S(2)}) %collective-permute-start.6) | collective-permute-done | bytes 4128 | tf_op jit(solution)/shard_map/ppermute | solution.py:545
  32.1 0.7 collective-permute-done.7.got_b
  32.8 0.0 collective-permute-done.8.got_c
  32.8 1.0 all-to-all-done.recv
  33.8 3.8 %collective-permute-start.9 = (bf16[16,768]{1,0:T(8,128)(2,1)S(1)}, bf16[16,768]{1,0:T(8,128)(2,1)S(1)}, u32[]{:S(2)}, u32[]{:S(2)}) collective-permute-start(bf16[16,768]{1,0:T(8,128)(2,1)S(1)} %get-tuple-element.67), channel_id=1, source_target_pairs={{0,16},{4,20},{8,24},{12,28},{16,32},{20,36},{24,40},{28,44},{32,4... | collective-permute-start | bytes 73736 | tf_op jit(solution)/shard_map/ppermute | solution.py:566
  37.6 0.0 copy-done.2
  37.6 0.0 copy-done.3
  37.6 3.8 %conv.1 = (bf16[1024,512]{1,0:T(8,128)(2,1)S(1)}, bf16[1024,256]{1,0:T(8,128)(2,1)S(1)}, f32[4,8,256]{2,1,0:T(8,128)S(1)}, f32[4,8,256]{2,1,0:T(8,128)S(1)}, f32...) custom-call(bf16[16,64,768]{2,1,0:T(8,128)(2,1)S(1)} %all-to-all-done.recv, ...), custom_call_target="tpu_custom_call" | custom-call | flops 15728640 | bytes 3145728 | tf_op jit(solution)/shard_map/conv/pallas_call | solution.py:231
  41.5 0.0 collective-permute-done.9.halo
  41.5 0.0 copy-start.1
  41.5 2.4 %state.1 = (bf16[1024,512]{1,0:T(8,128)(2,1)}, bf16[1024,256]{1,0:T(8,128)(2,1)}, f32[4,128,512]{2,1,0:T(8,128)}, f32[8,16,640]{2,1,0:T(8,128)}) custom-call(bf16[16,768]{1,0:T(8,128)(2,1)S(1)} %get-tuple-element.68.first, bf16[16,768]{1,0:T(8,128)(2,1)S(1)} %collective-permute-done.9.halo, f32[5,512]{1,0:T(8,128)S(1)} %constant_dynamic-slice_fusion.3.w_inner, ...), custom_call_target="tpu_custom_call" | custom-call | flops 134217728 | bytes 4194304 | tf_op jit(solution)/shard_map/state/pallas_call | solution.py:320
  43.9 0.0 copy-start.4
  43.9 0.0 collective-permute-done.4.got_a
  43.9 0.0 copy-start.8
  43.9 0.0 collective-permute-done.5.got_b
  43.9 0.0 copy-start.9
  43.9 7.7 %all-to-all-start.1 = ((f32[8,16,640]{2,1,0:T(8,128)}), f32[8,16,640]{2,1,0:T(8,128)S(1)}, u32[]{:S(2)}, u32[]{:S(2)}) async-start(f32[8,16,640]{2,1,0:T(8,128)} %get-tuple-element.52), calls=%async_computation.1 | async-start | bytes 655360 | tf_op jit(solution)/shard_map/all_to_all | solution.py:586
  51.6 0.9 collective-permute-start
  52.5 0.0 copy-done.1
  52.5 0.7 collective-permute-start.1
  53.2 2.9 %collective-permute-start.2 = (f32[1,2048]{1,0:T(1,128)S(1)}, f32[1,2048]{1,0:T(1,128)S(1)}, u32[]{:S(2)}, u32[]{:S(2)}) collective-permute-start(f32[1,2048]{1,0:T(1,128)S(1)} %bitcast.10), channel_id=1, source_target_pairs={{0,2},{1,3},{2,0},{3,1},{4,6},{5,7},{6,4},{7,5},{8,10},{9,11},{10,... | collective-permute-start | bytes 24584 | tf_op jit(solution)/shard_map/ppermute | solution.py:545
  56.0 0.4 collective-permute-start.3
  56.4 0.0 collective-permute-done.1.got_a
  56.4 1.9 %collective-permute-done.2.got_b = f32[1,2048]{1,0:T(1,128)S(1)} collective-permute-done((f32[1,2048]{1,0:T(1,128)S(1)}, f32[1,2048]{1,0:T(1,128)S(1)}, u32[]{:S(2)}, u32[]{:S(2)}) %collective-permute-start.2) | collective-permute-done | bytes 8224 | tf_op jit(solution)/shard_map/ppermute | solution.py:545
  58.3 1.4 %collective-permute-done.3.got_c = f32[1,2048]{1,0:T(1,128)S(1)} collective-permute-done((f32[1,2048]{1,0:T(1,128)S(1)}, f32[1,2048]{1,0:T(1,128)S(1)}, u32[]{:S(2)}, u32[]{:S(2)}) %collective-permute-start.3) | collective-permute-done | bytes 8224 | tf_op jit(solution)/shard_map/ppermute | solution.py:545
  59.7 0.0 collective-permute-done.got_c
  59.7 0.0 copy-start.10
  59.7 3.5 %all-to-all-done.1.recv = f32[8,16,640]{2,1,0:T(8,128)S(1)} async-done(((f32[8,16,640]{2,1,0:T(8,128)}), f32[8,16,640]{2,1,0:T(8,128)S(1)}, u32[]{:S(2)}, u32[]{:S(2)}) %all-to-all-start.1) | async-done | bytes 327712 | tf_op jit(solution)/shard_map/all_to_all | solution.py:586
  63.1 0.9 scan.1
  64.1 0.0 copy-done.9
  64.1 3.7 %all-to-all-start.2 = ((f32[8,16,512]{2,1,0:T(8,128)}), f32[8,16,512]{2,1,0:T(8,128)S(1)}, u32[]{:S(2)}, u32[]{:S(2)}) async-start(f32[8,16,512]{2,1,0:T(8,128)} %scan.1), calls=%async_computation.2 | async-start | bytes 524288 | tf_op jit(solution)/shard_map/all_to_all | solution.py:590
  67.8 0.0 copy-done.8
  67.8 0.0 copy-done.10
  67.9 0.0 copy-done.4
  67.9 5.7 %intra.1 = (bf16[1024,512]{1,0:T(8,128)(2,1)S(1)}, bf16[1024,512]{1,0:T(8,128)(2,1)S(1)}) custom-call(bf16[1024,512]{1,0:T(8,128)(2,1)} %get-tuple-element.56.xc, bf16[1024,256]{1,0:T(8,128)(2,1)} %get-tuple-element.55.bc, f32[4,8,256]{2,1,0:T(8,128)S(1)} %get-tuple-element.57.lc_t, f32[4,8,256]{2,1,0:T(8,128)S(1)} %get-tuple-element.58.dt_t, ...), custom_call_target="tpu_custom_call" | custom-call | flops 1073741824 | bytes 6291456 | tf_op jit(solution)/shard_map/intra/pallas_call | solution.py:398
  73.5 4.8 %all-to-all-done.2.carry = f32[8,16,512]{2,1,0:T(8,128)S(1)} async-done(((f32[8,16,512]{2,1,0:T(8,128)}), f32[8,16,512]{2,1,0:T(8,128)S(1)}, u32[]{:S(2)}, u32[]{:S(2)}) %all-to-all-start.2) | async-done | bytes 262176 | tf_op jit(solution)/shard_map/all_to_all | solution.py:590
  78.3 2.0 %finish.1 = bf16[16,64,512]{2,1,0:T(8,128)(2,1)S(1)} custom-call(f32[8,16,512]{2,1,0:T(8,128)S(1)} %all-to-all-done.2.carry, f32[4,128,512]{2,1,0:T(8,128)} %get-tuple-element.54.states, f32[8,512]{1,0:T(8,128)S(1)} %get-tuple-element.49.decay, bf16[1024,256]{1,0:T(8,128)(2,1)} %get-tuple-element.55.bc, bf16[1024,512]{1,0:T(8,128)(2,1)S(1)} %get-tuple-element.62.mixed, ...), custom_call_target="tpu_custom_call" | custom-call | flops 209715200 | bytes 3145728 | tf_op jit(solution)/shard_map/finish/pallas_call | solution.py:470
  80.3 16.7 %all_to_all.20.slabs = bf16[16,64,512]{2,1,0:T(8,128)(2,1)S(1)} all-to-all(bf16[16,64,512]{2,1,0:T(8,128)(2,1)S(1)} %finish.1), channel_id=1, replica_groups={{0,1,2,3,4,5,6,7,8,9,10,11,12,13,14,15},{16,17,18,19,20,21,22,23,24,25,..., dimensions={0} | all-to-all | bytes 2097152 | tf_op jit(solution)/shard_map/all_to_all | solution.py:595
  97.0 1.4 %post.1 = bf16[64,8192]{1,0:T(8,128)(2,1)} custom-call(bf16[16,64,512]{2,1,0:T(8,128)(2,1)S(1)} %all_to_all.20.slabs, f32[1,2048]{1,0:T(1,128)S(1)} %bitcast.12, f32[1,2048]{1,0:T(1,128)S(1)} %collective-permute-done.1.got_a, f32[1,2048]{1,0:T(1,128)S(1)} %collective-permute-done.2.got_b, f32[1,2048]{1,0:T(1,128)S(1)} %collective-permute-done.3.got_c), custom_call_target="tpu_custom_call" | custom-call | flops 3145728 | bytes 2097152 | tf_op jit(solution)/shard_map/post/pallas_call | solution.py:509
  (5 shorter events, 0.1 us)
Async XLA Ops:
  0.0 19.1 %copy-start = (f32[5,8192]{1,0:T(8,128)S(1)}, f32[5,8192]{1,0:T(8,128)}, u32[]{:S(2)}) copy-start(f32[5,8192]{1,0:T(8,128)} %param.17) | copy-start | bytes 491524
  3.4 7.7 %copy-start.7 = (bf16[256,32]{0,1:T(8,128)(2,1)S(1)}, bf16[256,32]{0,1:T(8,128)(2,1)}, u32[]{:S(2)}) copy-start(bf16[256,32]{0,1:T(8,128)(2,1)} %param.13) | copy-start | bytes 49156
  3.4 13.4 %copy-start.5 = (bf16[256,2048]{1,0:T(8,128)(2,1)S(1)}, bf16[256,2048]{1,0:T(8,128)(2,1)}, u32[]{:S(2)}) copy-start(bf16[256,2048]{1,0:T(8,128)(2,1)} %param.12) | copy-start | bytes 3145732
  3.4 30.4 %all-to-all-start = ((bf16[16,64,768]{2,1,0:T(8,128)(2,1)}), bf16[16,64,768]{2,1,0:T(8,128)(2,1)S(1)}, u32[]{:S(2)}, u32[]{:S(2)}) async-start(bf16[16,64,768]{2,1,0:T(8,128)(2,1)} %pack.1), calls=%async_computation | async-start | bytes 3145728 | tf_op jit(solution)/shard_map/all_to_all | solution.py:555
  10.9 8.2 %copy-start.6 = (f32[5,8,2,128]{3,2,1,0:T(2,128)S(1)}, f32[5,8,2,128]{3,2,1,0:T(2,128)}, u32[]{:S(2)}) copy-start(f32[5,8,2,128]{3,2,1,0:T(2,128)} %param.18) | copy-start | bytes 122884
  10.9 26.7 %copy-start.2 = (f32[32]{0:T(128)S(1)}, f32[32]{0:T(128)}, u32[]{:S(2)}) copy-start(f32[32]{0:T(128)} %param.14) | copy-start | bytes 388
  10.9 26.7 %copy-start.3 = (f32[32]{0:T(128)S(1)}, f32[32]{0:T(128)}, u32[]{:S(2)}) copy-start(f32[32]{0:T(128)} %param.15) | copy-start | bytes 388
  11.1 21.1 %collective-permute-start.6 = (bf16[8,256]{1,0:T(8,128)(2,1)S(1)}, bf16[8,256]{1,0:T(8,128)(2,1)S(1)}, u32[]{:S(2)}, u32[]{:S(2)}) collective-permute-start(bf16[8,256]{1,0:T(8,128)(2,1)S(1)} %get-tuple-element.76), channel_id=1, source_target_pairs={{0,4},{4,8},{8,12},{12,0},{16,20},{20,24},{24,28},{28,16},{32,36},... | collective-permute-start | bytes 12296 | tf_op jit(solution)/shard_map/ppermute | solution.py:545
  12.6 20.2 %collective-permute-start.7 = (bf16[8,256]{1,0:T(8,128)(2,1)S(1)}, bf16[8,256]{1,0:T(8,128)(2,1)S(1)}, u32[]{:S(2)}, u32[]{:S(2)}) collective-permute-start(bf16[8,256]{1,0:T(8,128)(2,1)S(1)} %get-tuple-element.75), channel_id=1, source_target_pairs={{0,8},{4,12},{8,0},{12,4},{16,24},{20,28},{24,16},{28,20},{32,40},... | collective-permute-start | bytes 12296 | tf_op jit(solution)/shard_map/ppermute | solution.py:545
  15.3 17.5 %collective-permute-start.8 = (bf16[8,256]{1,0:T(8,128)(2,1)S(1)}, bf16[8,256]{1,0:T(8,128)(2,1)S(1)}, u32[]{:S(2)}, u32[]{:S(2)}) collective-permute-start(bf16[8,256]{1,0:T(8,128)(2,1)S(1)} %get-tuple-element.74), channel_id=1, source_target_pairs={{0,12},{4,0},{8,4},{12,8},{16,28},{20,16},{24,20},{28,24},{32,44},... | collective-permute-start | bytes 12296 | tf_op jit(solution)/shard_map/ppermute | solution.py:545
  17.6 26.2 %collective-permute-start.4 = (bf16[256,512]{1,0:T(8,128)(2,1)}, bf16[256,512]{1,0:T(8,128)(2,1)S(1)}, u32[]{:S(2)}, u32[]{:S(2)}) collective-permute-start(bf16[256,512]{1,0:T(8,128)(2,1)} %get-tuple-element.71), channel_id=1, source_target_pairs={{0,4},{4,8},{8,12},{12,0},{16,20},{20,24},{24,28},{28,16},{32,36},... | collective-permute-start | bytes 786440 | tf_op jit(solution)/shard_map/ppermute | solution.py:545
  18.2 25.7 %collective-permute-start.5 = (bf16[256,512]{1,0:T(8,128)(2,1)S(1)}, bf16[256,512]{1,0:T(8,128)(2,1)S(1)}, u32[]{:S(2)}, u32[]{:S(2)}) collective-permute-start(bf16[256,512]{1,0:T(8,128)(2,1)S(1)} %get-tuple-element.70), channel_id=1, source_target_pairs={{0,8},{4,12},{8,0},{12,4},{16,24},{20,28},{24,16},{28,20},{32,40},... | collective-permute-start | bytes 786440 | tf_op jit(solution)/shard_map/ppermute | solution.py:545
  33.8 7.7 %collective-permute-start.9 = (bf16[16,768]{1,0:T(8,128)(2,1)S(1)}, bf16[16,768]{1,0:T(8,128)(2,1)S(1)}, u32[]{:S(2)}, u32[]{:S(2)}) collective-permute-start(bf16[16,768]{1,0:T(8,128)(2,1)S(1)} %get-tuple-element.67), channel_id=1, source_target_pairs={{0,16},{4,20},{8,24},{12,28},{16,32},{20,36},{24,40},{28,44},{32,4... | collective-permute-start | bytes 73736 | tf_op jit(solution)/shard_map/ppermute | solution.py:566
  41.5 11.0 %copy-start.1 = (f32[2048]{0:T(1024)S(1)}, f32[2048]{0:T(1024)}, u32[]{:S(2)}) copy-start(f32[2048]{0:T(1024)} %param.19) | copy-start | bytes 24580
  43.9 24.0 %copy-start.4 = (f32[32]{0:T(128)S(1)}, f32[32]{0:T(128)}, u32[]{:S(2)}) copy-start(f32[32]{0:T(128)} %param.16) | copy-start | bytes 388
  43.9 23.9 %copy-start.8 = (bf16[256,512]{1,0:T(8,128)(2,1)}, bf16[256,512]{1,0:T(8,128)(2,1)S(1)}, u32[]{:S(2)}) copy-start(bf16[256,512]{1,0:T(8,128)(2,1)S(1)} %collective-permute-done.4.got_a) | copy-start | bytes 786436
  43.9 20.2 %copy-start.9 = (bf16[256,512]{1,0:T(8,128)(2,1)}, bf16[256,512]{1,0:T(8,128)(2,1)S(1)}, u32[]{:S(2)}) copy-start(bf16[256,512]{1,0:T(8,128)(2,1)S(1)} %collective-permute-done.5.got_b) | copy-start | bytes 786436
  43.9 19.2 %all-to-all-start.1 = ((f32[8,16,640]{2,1,0:T(8,128)}), f32[8,16,640]{2,1,0:T(8,128)S(1)}, u32[]{:S(2)}, u32[]{:S(2)}) async-start(f32[8,16,640]{2,1,0:T(8,128)} %get-tuple-element.52), calls=%async_computation.1 | async-start | bytes 655360 | tf_op jit(solution)/shard_map/all_to_all | solution.py:586
  51.6 8.1 %collective-permute-start = (bf16[256,512]{1,0:T(8,128)(2,1)S(1)}, bf16[256,512]{1,0:T(8,128)(2,1)S(1)}, u32[]{:S(2)}, u32[]{:S(2)}) collective-permute-start(bf16[256,512]{1,0:T(8,128)(2,1)S(1)} %get-tuple-element.72), channel_id=1, source_target_pairs={{0,12},{4,0},{8,4},{12,8},{16,28},{20,16},{24,20},{28,24},{32,44},... | collective-permute-start | bytes 786440 | tf_op jit(solution)/shard_map/ppermute | solution.py:545
  52.5 3.9 %collective-permute-start.1 = (f32[1,2048]{1,0:T(1,128)S(1)}, f32[1,2048]{1,0:T(1,128)S(1)}, u32[]{:S(2)}, u32[]{:S(2)}) collective-permute-start(f32[1,2048]{1,0:T(1,128)S(1)} %bitcast.9), channel_id=1, source_target_pairs={{0,1},{1,2},{2,3},{3,0},{4,5},{5,6},{6,7},{7,4},{8,9},{9,10},{10,1... | collective-permute-start | bytes 24584 | tf_op jit(solution)/shard_map/ppermute | solution.py:545
  53.2 5.2 %collective-permute-start.2 = (f32[1,2048]{1,0:T(1,128)S(1)}, f32[1,2048]{1,0:T(1,128)S(1)}, u32[]{:S(2)}, u32[]{:S(2)}) collective-permute-start(f32[1,2048]{1,0:T(1,128)S(1)} %bitcast.10), channel_id=1, source_target_pairs={{0,2},{1,3},{2,0},{3,1},{4,6},{5,7},{6,4},{7,5},{8,10},{9,11},{10,... | collective-permute-start | bytes 24584 | tf_op jit(solution)/shard_map/ppermute | solution.py:545
  56.0 3.7 %collective-permute-start.3 = (f32[1,2048]{1,0:T(1,128)S(1)}, f32[1,2048]{1,0:T(1,128)S(1)}, u32[]{:S(2)}, u32[]{:S(2)}) collective-permute-start(f32[1,2048]{1,0:T(1,128)S(1)} %bitcast.11), channel_id=1, source_target_pairs={{0,3},{1,0},{2,1},{3,2},{4,7},{5,4},{6,5},{7,6},{8,11},{9,8},{10,9... | collective-permute-start | bytes 24584 | tf_op jit(solution)/shard_map/ppermute | solution.py:545
  59.7 8.2 %copy-start.10 = (bf16[256,512]{1,0:T(8,128)(2,1)}, bf16[256,512]{1,0:T(8,128)(2,1)S(1)}, u32[]{:S(2)}) copy-start(bf16[256,512]{1,0:T(8,128)(2,1)S(1)} %collective-permute-done.got_c) | copy-start | bytes 786436
  64.1 14.2 %all-to-all-start.2 = ((f32[8,16,512]{2,1,0:T(8,128)}), f32[8,16,512]{2,1,0:T(8,128)S(1)}, u32[]{:S(2)}, u32[]{:S(2)}) async-start(f32[8,16,512]{2,1,0:T(8,128)} %scan.1), calls=%async_computation.2 | async-start | bytes 524288 | tf_op jit(solution)/shard_map/all_to_all | solution.py:590

commit v9 on v8

--- a/solution.py
+++ b/solution.py
@@ -418,8 +418,12 @@
     chunks, rows, width = recv.shape
     wide = out.shape[2]
     logs = jnp.concatenate([recv[k, 0:1, wide:width] for k in range(chunks)], axis=0)
-    logs = jnp.where(iota(logs.shape, 1) < wide // 64, logs, 0.0)
-    decay = widen(jnp.exp(logs), spread(LANES, wide))
+    heads = wide // 64
+    top, mid, low = split(jnp.where(iota(logs.shape, 1) < heads, jnp.exp(logs), 0.0))
+    pieces = top + pltpu.roll(mid, heads, 1) + pltpu.roll(low, 2 * heads, 1)
+    row = iota((LANES, wide), 0)
+    one_hot = (row % heads == iota((LANES, wide), 1) // 64) & (row < 3 * heads)
+    decay = jnp.dot(pieces.astype(BF16), one_hot.astype(BF16), preferred_element_type=F32)
     carry = jnp.zeros((rows, wide), F32)
     for k in range(chunks):
         out[k] = carry

time: 98.9 us -> 98.9 us (level)
  no operation moved by 1% of the time
where the time goes in v9:
time: 98.9 us; the launch traced here: 98.4 us
  starting transfers between devices  34.7 us (35%)
  waiting for transfers between devices  26.2 us (26%)
  Pallas kernels  19.6 us (20%)
  blocking collectives  16.7 us (17%)
  local copies, waits for them, and re-layouts  1.02 us (1%)
    ppermute x9, waiting for transfers between devices, around(): lax.ppermute(pick((position + far) % 4), axis, route)  16.9 us
    all_to_all x1, blocking collectives, on_device(): lax.all_to_all(slabs, ('context', 'head'), split_axis=0, concat_axis=0, a...  16.7 us
    ppermute x9, starting transfers between devices, around(): lax.ppermute(pick((position + far) % 4), axis, route)  11.9 us
    all_to_all x1, starting transfers between devices, on_device(): lax.all_to_all(payload, 'context', split_axis=0, concat_axis=0, axis_inde...  7.69 us
    all_to_all x1, starting transfers between devices, on_device(): lax.all_to_all(packed, ('context', 'head'), split_axis=0, concat_axis=0,...  7.54 us
    pallas_call x1, Pallas kernels, intra(): pl.pallas_call(intra_kernel, out_shape=(jax.ShapeDtypeStruct((total, wide...  5.66 us
    all_to_all x1, waiting for transfers between devices, on_device(): lax.all_to_all(scan(totals), 'context', split_axis=0, concat_axis=0, axis...  4.79 us
    pallas_call x1, Pallas kernels, conv(): pl.pallas_call(conv_kernel, out_shape=tuple((jax.ShapeDtypeStruct(*s) for...  3.82 us
  transfers between devices with their start and end apart: 13, of which 7 were waited for; matrix products, arithmetic and copies ran while one was open for 1% of the time, Pallas kernels for 12%

profile of v9, /device:TPU:8, one launch (start us, length us, event | category | flops | bytes accessed | tf_op | source)
XLA Modules:
  0.0 98.4 jit_solution(8178228748243855493)
XLA Ops:
  0.0 0.0 copy-start
  0.0 3.4 %pack.1 = bf16[16,64,768]{2,1,0:T(8,128)(2,1)} custom-call(bf16[64,8192]{1,0:T(8,128)(2,1)} %inner.1, bf16[64,8,2,128]{3,2,1,0:T(2,128)(2,1)} %pairs.1), custom_call_target="tpu_custom_call" | custom-call | bytes 3145728 | tf_op jit(solution)/shard_map/pack/pallas_call | solution.py:116
  3.4 0.0 copy-start.7
  3.4 0.0 copy-start.5
  3.4 7.5 %all-to-all-start = ((bf16[16,64,768]{2,1,0:T(8,128)(2,1)}), bf16[16,64,768]{2,1,0:T(8,128)(2,1)S(1)}, u32[]{:S(2)}, u32[]{:S(2)}) async-start(bf16[16,64,768]{2,1,0:T(8,128)(2,1)} %pack.1), calls=%async_computation | async-start | bytes 3145728 | tf_op jit(solution)/shard_map/all_to_all | solution.py:559
  10.9 0.0 copy-start.6
  10.9 0.0 copy-start.2
  10.9 0.0 copy-start.3
  11.0 0.0 copy-done.7
  11.1 1.5 %collective-permute-start.6 = (bf16[8,256]{1,0:T(8,128)(2,1)S(1)}, bf16[8,256]{1,0:T(8,128)(2,1)S(1)}, u32[]{:S(2)}, u32[]{:S(2)}) collective-permute-start(bf16[8,256]{1,0:T(8,128)(2,1)S(1)} %get-tuple-element.76), channel_id=1, source_target_pairs={{0,4},{4,8},{8,12},{12,0},{16,20},{20,24},{24,28},{28,16},{32,36},... | collective-permute-start | bytes 12296 | tf_op jit(solution)/shard_map/ppermute | solution.py:549
  12.6 2.7 %collective-permute-start.7 = (bf16[8,256]{1,0:T(8,128)(2,1)S(1)}, bf16[8,256]{1,0:T(8,128)(2,1)S(1)}, u32[]{:S(2)}, u32[]{:S(2)}) collective-permute-start(bf16[8,256]{1,0:T(8,128)(2,1)S(1)} %get-tuple-element.75), channel_id=1, source_target_pairs={{0,8},{4,12},{8,0},{12,4},{16,24},{20,28},{24,16},{28,20},{32,40},... | collective-permute-start | bytes 12296 | tf_op jit(solution)/shard_map/ppermute | solution.py:549
  15.3 1.5 %collective-permute-start.8 = (bf16[8,256]{1,0:T(8,128)(2,1)S(1)}, bf16[8,256]{1,0:T(8,128)(2,1)S(1)}, u32[]{:S(2)}, u32[]{:S(2)}) collective-permute-start(bf16[8,256]{1,0:T(8,128)(2,1)S(1)} %get-tuple-element.74), channel_id=1, source_target_pairs={{0,12},{4,0},{8,4},{12,8},{16,28},{20,16},{24,20},{28,24},{32,44},... | collective-permute-start | bytes 12296 | tf_op jit(solution)/shard_map/ppermute | solution.py:549
  16.7 0.0 copy-done.5
  16.7 0.9 constant_dynamic-slice_fusion
  17.6 0.6 collective-permute-start.4
  18.2 0.9 collective-permute-start.5
  19.1 0.0 copy-done
  19.1 0.0 copy-done.6
  19.2 13.0 %collective-permute-done.6.got_a = bf16[8,256]{1,0:T(8,128)(2,1)S(1)} collective-permute-done((bf16[8,256]{1,0:T(8,128)(2,1)S(1)}, bf16[8,256]{1,0:T(8,128)(2,1)S(1)}, u32[]{:S(2)}, u32[]{:S(2)}) %collective-permute-start.6) | collective-permute-done | bytes 4128 | tf_op jit(solution)/shard_map/ppermute | solution.py:549
  32.1 0.7 collective-permute-done.7.got_b
  32.8 0.0 collective-permute-done.8.got_c
  32.8 1.0 all-to-all-done.recv
  33.8 3.8 %collective-permute-start.9 = (bf16[16,768]{1,0:T(8,128)(2,1)S(1)}, bf16[16,768]{1,0:T(8,128)(2,1)S(1)}, u32[]{:S(2)}, u32[]{:S(2)}) collective-permute-start(bf16[16,768]{1,0:T(8,128)(2,1)S(1)} %get-tuple-element.67), channel_id=1, source_target_pairs={{0,16},{4,20},{8,24},{12,28},{16,32},{20,36},{24,40},{28,44},{32,4... | collective-permute-start | bytes 73736 | tf_op jit(solution)/shard_map/ppermute | solution.py:570
  37.6 0.0 copy-done.2
  37.6 0.0 copy-done.3
  37.6 3.8 %conv.1 = (bf16[1024,512]{1,0:T(8,128)(2,1)S(1)}, bf16[1024,256]{1,0:T(8,128)(2,1)S(1)}, f32[4,8,256]{2,1,0:T(8,128)S(1)}, f32[4,8,256]{2,1,0:T(8,128)S(1)}, f32...) custom-call(bf16[16,64,768]{2,1,0:T(8,128)(2,1)S(1)} %all-to-all-done.recv, ...), custom_call_target="tpu_custom_call" | custom-call | flops 15728640 | bytes 3145728 | tf_op jit(solution)/shard_map/conv/pallas_call | solution.py:231
  41.5 0.0 collective-permute-done.9.halo
  41.5 0.0 copy-start.1
  41.5 2.4 %state.1 = (bf16[1024,512]{1,0:T(8,128)(2,1)}, bf16[1024,256]{1,0:T(8,128)(2,1)}, f32[4,128,512]{2,1,0:T(8,128)}, f32[8,16,640]{2,1,0:T(8,128)}) custom-call(bf16[16,768]{1,0:T(8,128)(2,1)S(1)} %get-tuple-element.68.first, bf16[16,768]{1,0:T(8,128)(2,1)S(1)} %collective-permute-done.9.halo, f32[5,512]{1,0:T(8,128)S(1)} %constant_dynamic-slice_fusion.3.w_inner, ...), custom_call_target="tpu_custom_call" | custom-call | flops 134217728 | bytes 4194304 | tf_op jit(solution)/shard_map/state/pallas_call | solution.py:320
  43.9 0.0 copy-start.4
  43.9 0.0 collective-permute-done.4.got_a
  43.9 0.0 copy-start.8
  43.9 0.0 collective-permute-done.5.got_b
  43.9 0.0 copy-start.9
  43.9 7.7 %all-to-all-start.1 = ((f32[8,16,640]{2,1,0:T(8,128)}), f32[8,16,640]{2,1,0:T(8,128)S(1)}, u32[]{:S(2)}, u32[]{:S(2)}) async-start(f32[8,16,640]{2,1,0:T(8,128)} %get-tuple-element.52), calls=%async_computation.1 | async-start | bytes 655360 | tf_op jit(solution)/shard_map/all_to_all | solution.py:590
  51.6 0.9 collective-permute-start
  52.5 0.0 copy-done.1
  52.5 0.7 collective-permute-start.1
  53.2 2.9 %collective-permute-start.2 = (f32[1,2048]{1,0:T(1,128)S(1)}, f32[1,2048]{1,0:T(1,128)S(1)}, u32[]{:S(2)}, u32[]{:S(2)}) collective-permute-start(f32[1,2048]{1,0:T(1,128)S(1)} %bitcast.10), channel_id=1, source_target_pairs={{0,2},{1,3},{2,0},{3,1},{4,6},{5,7},{6,4},{7,5},{8,10},{9,11},{10,... | collective-permute-start | bytes 24584 | tf_op jit(solution)/shard_map/ppermute | solution.py:549
  56.0 0.4 collective-permute-start.3
  56.4 0.0 collective-permute-done.1.got_a
  56.4 1.9 %collective-permute-done.2.got_b = f32[1,2048]{1,0:T(1,128)S(1)} collective-permute-done((f32[1,2048]{1,0:T(1,128)S(1)}, f32[1,2048]{1,0:T(1,128)S(1)}, u32[]{:S(2)}, u32[]{:S(2)}) %collective-permute-start.2) | collective-permute-done | bytes 8224 | tf_op jit(solution)/shard_map/ppermute | solution.py:549
  58.3 1.4 %collective-permute-done.3.got_c = f32[1,2048]{1,0:T(1,128)S(1)} collective-permute-done((f32[1,2048]{1,0:T(1,128)S(1)}, f32[1,2048]{1,0:T(1,128)S(1)}, u32[]{:S(2)}, u32[]{:S(2)}) %collective-permute-start.3) | collective-permute-done | bytes 8224 | tf_op jit(solution)/shard_map/ppermute | solution.py:549
  59.7 0.0 collective-permute-done.got_c
  59.7 0.0 copy-start.10
  59.7 3.5 %all-to-all-done.1.recv = f32[8,16,640]{2,1,0:T(8,128)S(1)} async-done(((f32[8,16,640]{2,1,0:T(8,128)}), f32[8,16,640]{2,1,0:T(8,128)S(1)}, u32[]{:S(2)}, u32[]{:S(2)}) %all-to-all-start.1) | async-done | bytes 327712 | tf_op jit(solution)/shard_map/all_to_all | solution.py:590
  63.1 1.0 scan.1
  64.1 0.0 copy-done.9
  64.1 3.7 %all-to-all-start.2 = ((f32[8,16,512]{2,1,0:T(8,128)}), f32[8,16,512]{2,1,0:T(8,128)S(1)}, u32[]{:S(2)}, u32[]{:S(2)}) async-start(f32[8,16,512]{2,1,0:T(8,128)} %scan.1), calls=%async_computation.2 | async-start | bytes 524288 | tf_op jit(solution)/shard_map/all_to_all | solution.py:594
  67.9 0.0 copy-done.8
  67.9 0.0 copy-done.10
  67.9 0.0 copy-done.4
  67.9 5.7 %intra.1 = (bf16[1024,512]{1,0:T(8,128)(2,1)S(1)}, bf16[1024,512]{1,0:T(8,128)(2,1)S(1)}) custom-call(bf16[1024,512]{1,0:T(8,128)(2,1)} %get-tuple-element.56.xc, bf16[1024,256]{1,0:T(8,128)(2,1)} %get-tuple-element.55.bc, f32[4,8,256]{2,1,0:T(8,128)S(1)} %get-tuple-element.57.lc_t, f32[4,8,256]{2,1,0:T(8,128)S(1)} %get-tuple-element.58.dt_t, ...), custom_call_target="tpu_custom_call" | custom-call | flops 1073741824 | bytes 6291456 | tf_op jit(solution)/shard_map/intra/pallas_call | solution.py:398
  73.5 4.8 %all-to-all-done.2.carry = f32[8,16,512]{2,1,0:T(8,128)S(1)} async-done(((f32[8,16,512]{2,1,0:T(8,128)}), f32[8,16,512]{2,1,0:T(8,128)S(1)}, u32[]{:S(2)}, u32[]{:S(2)}) %all-to-all-start.2) | async-done | bytes 262176 | tf_op jit(solution)/shard_map/all_to_all | solution.py:594
  78.3 2.0 %finish.1 = bf16[16,64,512]{2,1,0:T(8,128)(2,1)S(1)} custom-call(f32[8,16,512]{2,1,0:T(8,128)S(1)} %all-to-all-done.2.carry, f32[4,128,512]{2,1,0:T(8,128)} %get-tuple-element.54.states, f32[8,512]{1,0:T(8,128)S(1)} %get-tuple-element.49.decay, bf16[1024,256]{1,0:T(8,128)(2,1)} %get-tuple-element.55.bc, bf16[1024,512]{1,0:T(8,128)(2,1)S(1)} %get-tuple-element.62.mixed, ...), custom_call_target="tpu_custom_call" | custom-call | flops 209715200 | bytes 3145728 | tf_op jit(solution)/shard_map/finish/pallas_call | solution.py:474
  80.4 16.7 %all_to_all.20.slabs = bf16[16,64,512]{2,1,0:T(8,128)(2,1)S(1)} all-to-all(bf16[16,64,512]{2,1,0:T(8,128)(2,1)S(1)} %finish.1), channel_id=1, replica_groups={{0,1,2,3,4,5,6,7,8,9,10,11,12,13,14,15},{16,17,18,19,20,21,22,23,24,25,..., dimensions={0} | all-to-all | bytes 2097152 | tf_op jit(solution)/shard_map/all_to_all | solution.py:599
  97.0 1.4 %post.1 = bf16[64,8192]{1,0:T(8,128)(2,1)} custom-call(bf16[16,64,512]{2,1,0:T(8,128)(2,1)S(1)} %all_to_all.20.slabs, f32[1,2048]{1,0:T(1,128)S(1)} %bitcast.12, f32[1,2048]{1,0:T(1,128)S(1)} %collective-permute-done.1.got_a, f32[1,2048]{1,0:T(1,128)S(1)} %collective-permute-done.2.got_b, f32[1,2048]{1,0:T(1,128)S(1)} %collective-permute-done.3.got_c), custom_call_target="tpu_custom_call" | custom-call | flops 3145728 | bytes 2097152 | tf_op jit(solution)/shard_map/post/pallas_call | solution.py:513
  (5 shorter events, 0.1 us)
Async XLA Ops:
  0.0 19.1 %copy-start = (f32[5,8192]{1,0:T(8,128)S(1)}, f32[5,8192]{1,0:T(8,128)}, u32[]{:S(2)}) copy-start(f32[5,8192]{1,0:T(8,128)} %param.17) | copy-start | bytes 491524
  3.4 7.7 %copy-start.7 = (bf16[256,32]{0,1:T(8,128)(2,1)S(1)}, bf16[256,32]{0,1:T(8,128)(2,1)}, u32[]{:S(2)}) copy-start(bf16[256,32]{0,1:T(8,128)(2,1)} %param.13) | copy-start | bytes 49156
  3.4 13.4 %copy-start.5 = (bf16[256,2048]{1,0:T(8,128)(2,1)S(1)}, bf16[256,2048]{1,0:T(8,128)(2,1)}, u32[]{:S(2)}) copy-start(bf16[256,2048]{1,0:T(8,128)(2,1)} %param.12) | copy-start | bytes 3145732
  3.4 30.4 %all-to-all-start = ((bf16[16,64,768]{2,1,0:T(8,128)(2,1)}), bf16[16,64,768]{2,1,0:T(8,128)(2,1)S(1)}, u32[]{:S(2)}, u32[]{:S(2)}) async-start(bf16[16,64,768]{2,1,0:T(8,128)(2,1)} %pack.1), calls=%async_computation | async-start | bytes 3145728 | tf_op jit(solution)/shard_map/all_to_all | solution.py:559
  10.9 8.2 %copy-start.6 = (f32[5,8,2,128]{3,2,1,0:T(2,128)S(1)}, f32[5,8,2,128]{3,2,1,0:T(2,128)}, u32[]{:S(2)}) copy-start(f32[5,8,2,128]{3,2,1,0:T(2,128)} %param.18) | copy-start | bytes 122884
  10.9 26.7 %copy-start.2 = (f32[32]{0:T(128)S(1)}, f32[32]{0:T(128)}, u32[]{:S(2)}) copy-start(f32[32]{0:T(128)} %param.14) | copy-start | bytes 388
  10.9 26.7 %copy-start.3 = (f32[32]{0:T(128)S(1)}, f32[32]{0:T(128)}, u32[]{:S(2)}) copy-start(f32[32]{0:T(128)} %param.15) | copy-start | bytes 388
  11.1 21.1 %collective-permute-start.6 = (bf16[8,256]{1,0:T(8,128)(2,1)S(1)}, bf16[8,256]{1,0:T(8,128)(2,1)S(1)}, u32[]{:S(2)}, u32[]{:S(2)}) collective-permute-start(bf16[8,256]{1,0:T(8,128)(2,1)S(1)} %get-tuple-element.76), channel_id=1, source_target_pairs={{0,4},{4,8},{8,12},{12,0},{16,20},{20,24},{24,28},{28,16},{32,36},... | collective-permute-start | bytes 12296 | tf_op jit(solution)/shard_map/ppermute | solution.py:549
  12.6 20.2 %collective-permute-start.7 = (bf16[8,256]{1,0:T(8,128)(2,1)S(1)}, bf16[8,256]{1,0:T(8,128)(2,1)S(1)}, u32[]{:S(2)}, u32[]{:S(2)}) collective-permute-start(bf16[8,256]{1,0:T(8,128)(2,1)S(1)} %get-tuple-element.75), channel_id=1, source_target_pairs={{0,8},{4,12},{8,0},{12,4},{16,24},{20,28},{24,16},{28,20},{32,40},... | collective-permute-start | bytes 12296 | tf_op jit(solution)/shard_map/ppermute | solution.py:549
  15.3 17.5 %collective-permute-start.8 = (bf16[8,256]{1,0:T(8,128)(2,1)S(1)}, bf16[8,256]{1,0:T(8,128)(2,1)S(1)}, u32[]{:S(2)}, u32[]{:S(2)}) collective-permute-start(bf16[8,256]{1,0:T(8,128)(2,1)S(1)} %get-tuple-element.74), channel_id=1, source_target_pairs={{0,12},{4,0},{8,4},{12,8},{16,28},{20,16},{24,20},{28,24},{32,44},... | collective-permute-start | bytes 12296 | tf_op jit(solution)/shard_map/ppermute | solution.py:549
  17.6 26.2 %collective-permute-start.4 = (bf16[256,512]{1,0:T(8,128)(2,1)}, bf16[256,512]{1,0:T(8,128)(2,1)S(1)}, u32[]{:S(2)}, u32[]{:S(2)}) collective-permute-start(bf16[256,512]{1,0:T(8,128)(2,1)} %get-tuple-element.71), channel_id=1, source_target_pairs={{0,4},{4,8},{8,12},{12,0},{16,20},{20,24},{24,28},{28,16},{32,36},... | collective-permute-start | bytes 786440 | tf_op jit(solution)/shard_map/ppermute | solution.py:549
  18.2 25.7 %collective-permute-start.5 = (bf16[256,512]{1,0:T(8,128)(2,1)S(1)}, bf16[256,512]{1,0:T(8,128)(2,1)S(1)}, u32[]{:S(2)}, u32[]{:S(2)}) collective-permute-start(bf16[256,512]{1,0:T(8,128)(2,1)S(1)} %get-tuple-element.70), channel_id=1, source_target_pairs={{0,8},{4,12},{8,0},{12,4},{16,24},{20,28},{24,16},{28,20},{32,40},... | collective-permute-start | bytes 786440 | tf_op jit(solution)/shard_map/ppermute | solution.py:549
  33.8 7.7 %collective-permute-start.9 = (bf16[16,768]{1,0:T(8,128)(2,1)S(1)}, bf16[16,768]{1,0:T(8,128)(2,1)S(1)}, u32[]{:S(2)}, u32[]{:S(2)}) collective-permute-start(bf16[16,768]{1,0:T(8,128)(2,1)S(1)} %get-tuple-element.67), channel_id=1, source_target_pairs={{0,16},{4,20},{8,24},{12,28},{16,32},{20,36},{24,40},{28,44},{32,4... | collective-permute-start | bytes 73736 | tf_op jit(solution)/shard_map/ppermute | solution.py:570
  41.5 11.0 %copy-start.1 = (f32[2048]{0:T(1024)S(1)}, f32[2048]{0:T(1024)}, u32[]{:S(2)}) copy-start(f32[2048]{0:T(1024)} %param.19) | copy-start | bytes 24580
  43.9 24.0 %copy-start.4 = (f32[32]{0:T(128)S(1)}, f32[32]{0:T(128)}, u32[]{:S(2)}) copy-start(f32[32]{0:T(128)} %param.16) | copy-start | bytes 388
  43.9 24.0 %copy-start.8 = (bf16[256,512]{1,0:T(8,128)(2,1)}, bf16[256,512]{1,0:T(8,128)(2,1)S(1)}, u32[]{:S(2)}) copy-start(bf16[256,512]{1,0:T(8,128)(2,1)S(1)} %collective-permute-done.4.got_a) | copy-start | bytes 786436
  43.9 20.2 %copy-start.9 = (bf16[256,512]{1,0:T(8,128)(2,1)}, bf16[256,512]{1,0:T(8,128)(2,1)S(1)}, u32[]{:S(2)}) copy-start(bf16[256,512]{1,0:T(8,128)(2,1)S(1)} %collective-permute-done.5.got_b) | copy-start | bytes 786436
  43.9 19.2 %all-to-all-start.1 = ((f32[8,16,640]{2,1,0:T(8,128)}), f32[8,16,640]{2,1,0:T(8,128)S(1)}, u32[]{:S(2)}, u32[]{:S(2)}) async-start(f32[8,16,640]{2,1,0:T(8,128)} %get-tuple-element.52), calls=%async_computation.1 | async-start | bytes 655360 | tf_op jit(solution)/shard_map/all_to_all | solution.py:590
  51.6 8.1 %collective-permute-start = (bf16[256,512]{1,0:T(8,128)(2,1)S(1)}, bf16[256,512]{1,0:T(8,128)(2,1)S(1)}, u32[]{:S(2)}, u32[]{:S(2)}) collective-permute-start(bf16[256,512]{1,0:T(8,128)(2,1)S(1)} %get-tuple-element.72), channel_id=1, source_target_pairs={{0,12},{4,0},{8,4},{12,8},{16,28},{20,16},{24,20},{28,24},{32,44},... | collective-permute-start | bytes 786440 | tf_op jit(solution)/shard_map/ppermute | solution.py:549
  52.5 3.9 %collective-permute-start.1 = (f32[1,2048]{1,0:T(1,128)S(1)}, f32[1,2048]{1,0:T(1,128)S(1)}, u32[]{:S(2)}, u32[]{:S(2)}) collective-permute-start(f32[1,2048]{1,0:T(1,128)S(1)} %bitcast.9), channel_id=1, source_target_pairs={{0,1},{1,2},{2,3},{3,0},{4,5},{5,6},{6,7},{7,4},{8,9},{9,10},{10,1... | collective-permute-start | bytes 24584 | tf_op jit(solution)/shard_map/ppermute | solution.py:549
  53.2 5.2 %collective-permute-start.2 = (f32[1,2048]{1,0:T(1,128)S(1)}, f32[1,2048]{1,0:T(1,128)S(1)}, u32[]{:S(2)}, u32[]{:S(2)}) collective-permute-start(f32[1,2048]{1,0:T(1,128)S(1)} %bitcast.10), channel_id=1, source_target_pairs={{0,2},{1,3},{2,0},{3,1},{4,6},{5,7},{6,4},{7,5},{8,10},{9,11},{10,... | collective-permute-start | bytes 24584 | tf_op jit(solution)/shard_map/ppermute | solution.py:549
  56.0 3.7 %collective-permute-start.3 = (f32[1,2048]{1,0:T(1,128)S(1)}, f32[1,2048]{1,0:T(1,128)S(1)}, u32[]{:S(2)}, u32[]{:S(2)}) collective-permute-start(f32[1,2048]{1,0:T(1,128)S(1)} %bitcast.11), channel_id=1, source_target_pairs={{0,3},{1,0},{2,1},{3,2},{4,7},{5,4},{6,5},{7,6},{8,11},{9,8},{10,9... | collective-permute-start | bytes 24584 | tf_op jit(solution)/shard_map/ppermute | solution.py:549
  59.7 8.2 %copy-start.10 = (bf16[256,512]{1,0:T(8,128)(2,1)}, bf16[256,512]{1,0:T(8,128)(2,1)S(1)}, u32[]{:S(2)}) copy-start(bf16[256,512]{1,0:T(8,128)(2,1)S(1)} %collective-permute-done.got_c) | copy-start | bytes 786436
  64.1 14.2 %all-to-all-start.2 = ((f32[8,16,512]{2,1,0:T(8,128)}), f32[8,16,512]{2,1,0:T(8,128)S(1)}, u32[]{:S(2)}, u32[]{:S(2)}) async-start(f32[8,16,512]{2,1,0:T(8,128)} %scan.1), calls=%async_computation.2 | async-start | bytes 524288 | tf_op jit(solution)/shard_map/all_to_all | solution.py:594
